TPU v7x, 256 devices: a whole 4x4x8 slice. The times are simulated.
256 devices in a mesh: feat: 64 (over z_lo, y, x), tgt: 4 (over z_hi, core).
Axes of the slice: x: 4, y: 4, z: 8 (z_hi: 2, z_lo: 4; z = z_hi * 4 + z_lo), core: 2. Of those that a mesh axis runs over, the one named last changes fastest.
Arguments:
- tokens: bfloat16 [192, 4096], P('feat'), may hold values from -6 to 6
- encoder_weight: bfloat16 [4096, 16384], P(None, 'feat'), may hold values from -0.09375 to 0.09375
- encoder_bias: float32 [16384], P('feat'), may hold values from -1 to 0.25
- decoder_weight: bfloat16 [4, 16384, 4096], P('tgt', 'feat'), may hold values from -0.046875 to 0.046875
- decoder_bias: float32 [4, 4096], P('tgt'), may hold values from -3 to 3
- targets: bfloat16 [4, 192, 4096], P('tgt', 'feat'), may hold values from -6 to 6
Outputs:
- encoder_grad: float32 [4096, 16384], P(None, ('feat', 'tgt'))
- encoder_bias_grad: float32 [16384], P(('feat', 'tgt'))
- decoder_grad: float32 [4, 16384, 4096], P('tgt', 'feat')
- decoder_bias_grad: float32 [4, 4096], P('tgt')
All inputs are finite; a program needn't handle non-finite values.
Results may differ from a plain program's by a relative error of at most 0.005.
Values may be sent and summed in bfloat16 or wider, within the bound.
No kernel may reach another device: no remote copies, remote signals or barrier semaphores. Data moves between devices by JAX's collectives and lax.ppermute only.
A program may use at most 64 MiB of HBM per device.

v0:
```python
import jax
import jax.numpy as jnp
from jax import lax
from jax.sharding import PartitionSpec as P


def body(tokens, encoder_weight, encoder_bias, decoder_weight, decoder_bias, targets):
    all_rows = lax.all_gather(tokens, "feat", axis=0, tiled=True)
    pre_act = jnp.dot(all_rows, encoder_weight, preferred_element_type=jnp.float32) + encoder_bias
    positive = jnp.maximum(pre_act, 0.0)
    feats = (positive**2).astype(jnp.bfloat16)
    weight = decoder_weight[0]
    bias = decoder_bias[0]
    target = targets[0]
    summed = lax.psum_scatter(
        jnp.dot(feats, weight, preferred_element_type=jnp.float32),
        "feat",
        scatter_dimension=0,
        tiled=True,
    )
    error_part = (summed + bias - target.astype(jnp.float32)).astype(jnp.bfloat16)
    recon_error = lax.all_gather(error_part, "feat", axis=0, tiled=True)
    decoder_grads = [
        lax.dot_general(
            feats, recon_error, (((0,), (0,)), ((), ())), preferred_element_type=jnp.float32
        )
    ]
    bias_grads = [jnp.sum(recon_error.astype(jnp.float32), axis=0)]
    back_grad = lax.dot_general(
        recon_error, weight, (((1,), (1,)), ((), ())), preferred_element_type=jnp.float32
    )
    quarter = pre_act.shape[1] // lax.axis_size("tgt")
    offset = lax.axis_index("tgt") * quarter
    share = lax.psum_scatter(back_grad, "tgt", scatter_dimension=1, tiled=True)
    slope_share = 2.0 * lax.dynamic_slice_in_dim(positive, offset, quarter, 1)
    act_grad = share * slope_share
    encoder_bias_grad = jnp.sum(act_grad, axis=0)
    pre_grad = act_grad.astype(jnp.bfloat16)
    encoder_grad = lax.dot_general(
        all_rows, pre_grad, (((0,), (0,)), ((), ())), preferred_element_type=jnp.float32
    )
    return (encoder_grad, encoder_bias_grad, jnp.stack(decoder_grads), jnp.stack(bias_grads))


def solution(mesh):
    return jax.shard_map(
        body,
        mesh=mesh,
        in_specs=(
            P("feat", None),
            P(None, "feat"),
            P("feat"),
            P("tgt", "feat", None),
            P("tgt", None),
            P("tgt", "feat", None),
        ),
        out_specs=(
            P(None, ("feat", "tgt")),
            P(("feat", "tgt")),
            P("tgt", "feat", None),
            P("tgt", None),
        ),
        check_vma=False,
    )
```

profile of v0, /device:TPU:1, one launch (start us, length us, event | category | flops | bytes accessed | tf_op | source)
XLA Modules:
  0.0 1493.3 jit_solution(6703649330818770816)
XLA Ops:
  7.2 0.0 all-gather.5.cloned.1.call-start
  7.2 0.7 all-gather.5.cloned.1.call-update
  7.9 0.0 all-reduce.3.cloned.1.call-start
  8.0 310.1 %all-gather.5.cloned.1.call-done = bf16[64,3,4096]{2,1,0:T(4,128)(2,1)} async-done(((bf16[1,3,4096]{2,1,0:T(4,128)(2,1)}), bf16[64,3,4096]{2,1,0:T(4,128)(2,1)}) %all-gather.5.cloned.1.call-update) | async-done | bytes 1572880 | tf_op jit(solution)/shard_map/all_gather | solution.py:8
  318.0 4.3 reshape.13
  322.3 2.6 fusion.7
  325.0 2.2 fusion.2
  327.2 0.0 all-reduce.3.cloned.1.call-update
  327.3 0.0 all-gather.7.cloned.1.call-start
  327.3 0.6 copy-done.5
  327.9 0.6 dynamic-slice
  329.1 716.0 %all-reduce.3.cloned.1.call-done = f32[192,4096]{1,0:T(8,128)} async-done(((f32[192,4096]{1,0:T(8,128)}), f32[192,4096]{1,0:T(8,128)}) %all-reduce.3.cloned.1.call-update) | async-done | bytes 3145744
  1045.2 1.6 fusion.10
  1046.8 0.0 all-gather.7.cloned.1.call-update
  1046.8 0.0 reduce-scatter.4.cloned.1.call-start
  1046.9 348.8 %all-gather.7.cloned.1.call-done = bf16[64,3,4096]{2,1,0:T(4,128)(2,1)} async-done(((bf16[1,3,4096]{2,1,0:T(4,128)(2,1)}), bf16[64,3,4096]{2,1,0:T(4,128)(2,1)}) %all-gather.7.cloned.1.call-update) | async-done | bytes 1572880 | tf_op jit(solution)/shard_map/all_gather | solution.py:22
  1395.7 4.3 reshape.15
  1399.9 2.8 fusion.4
  1402.8 2.4 convert_reduce_fusion
  1405.2 2.8 convolution_bitcast_fusion
  1407.9 74.3 %reduce-scatter.4.cloned.1.call-done = f32[64,192]{1,0:T(8,128)} async-done(((f32[256,192]{1,0:T(8,128)}), f32[64,192]{1,0:T(8,128)}) %reduce-scatter.4.cloned.1.call-update) | async-done | bytes 49168
  1482.3 0.9 copy.15
  1483.2 2.9 convolution_bitcast_fusion.1
  1486.1 0.6 fusion.11
  (12 shorter events, 0.0 us)
Async XLA Ops:
  7.2 317.8 %copy-start = (bf16[1,256,4096]{2,1,0:T(8,128)(2,1)S(1)}, bf16[1,256,4096]{2,1,0:T(8,128)(2,1)}, u32[]{:S(2)}) copy-start(bf16[1,256,4096]{2,1,0:T(8,128)(2,1)} %param.9) | copy-start | bytes 6291460
  7.2 315.1 %copy-start.4 = (f32[256]{0:T(256)S(1)}, f32[256]{0:T(256)}, u32[]{:S(2)}) copy-start(f32[256]{0:T(256)} %param.8) | copy-start | bytes 3076
  7.2 310.8 %all-gather.5.cloned.1.call-start = ((), (), s32[]{:S(2)}) async-start(), calls=%async_computation.1 | async-start | bytes 2129920 | tf_op jit(solution)/shard_map/all_gather | solution.py:8
  7.9 1037.2 %all-reduce.3.cloned.1.call-start = ((), (), s32[]{:S(2)}) async-start(), calls=%async_computation.4 | async-start | bytes 6291456
  327.2 0.7 copy-start.5
  327.2 717.9 %copy-start.2 = (bf16[1,3,4096]{2,1,0:T(4,128)(2,1)S(1)}, bf16[1,3,4096]{2,1,0:T(4,128)(2,1)}, u32[]{:S(2)}) copy-start(bf16[1,3,4096]{2,1,0:T(4,128)(2,1)} %param.11) | copy-start | bytes 73732
  327.2 717.9 %copy-start.3 = (f32[1,4096]{1,0:T(1,128)S(1)}, f32[1,4096]{1,0:T(1,128)}, u32[]{:S(2)}) copy-start(f32[1,4096]{1,0:T(1,128)} %param.10) | copy-start | bytes 49156
  327.3 1068.4 %all-gather.7.cloned.1.call-start = ((), (), s32[]{:S(2)}) async-start(), calls=%async_computation.2 | async-start | bytes 2129920 | tf_op jit(solution)/shard_map/all_gather | solution.py:22
  1046.8 435.5 %reduce-scatter.4.cloned.1.call-start = ((), (), s32[]{:S(2)}) async-start(), calls=%async_computation.3 | async-start | bytes 327680
  1402.8 2.4 copy-start.1
Sparse Core Ops, SparseCore 0:
  9.8 308.1 all-gather.4
  327.4 717.7 all-reduce.2
  1047.7 347.9 all-gather.6
  1402.9 79.3 reduce-scatter.3
where the time goes:
time: 1490 us
  waiting for transfers between devices  1450 us (97%)
    unnamed x6, waiting for transfers between devices  791 us
    all_gather x1, waiting for transfers between devices, body(): recon_error = lax.all_gather(error_part, 'feat', axis=0, tiled=True)  349 us
    all_gather x1, waiting for transfers between devices, body(): all_rows = lax.all_gather(tokens, 'feat', axis=0, tiled=True)  310 us
  transfers between devices with their start and end apart: 4, of which 4 were waited for; matrix products, arithmetic and copies ran while one was open for 0% of the time, Pallas kernels for 0%

commit v1 on v0

v1 whole, which is shorter than its diff:
```python
import jax
import jax.numpy as jnp
from jax import lax
from jax.sharding import Mesh, PartitionSpec as P

BF16 = jnp.bfloat16
F32 = jnp.float32
FEAT = ("zl", "y", "x")
TGT = ("zh", "core")
SWAP = [(0, 1), (1, 0)]


def spread(block, axes, count):
    copies = jnp.broadcast_to(block[None], (count,) + block.shape)
    return lax.all_to_all(copies, axes, 0, 0, tiled=True)


def gather_tokens(tokens):
    members = lax.axis_size(FEAT)
    mine, width = tokens.shape
    half = width // 2
    core = lax.axis_index("core")
    part = lax.dynamic_slice_in_dim(tokens, core * half, half, 1)
    flat = part.reshape(mine * half // 128, 128)
    own = spread(flat, FEAT, members)
    other = lax.ppermute(own, "core", SWAP)
    low = jnp.where(core == 0, own, other).reshape(members * mine, half)
    high = jnp.where(core == 0, other, own).reshape(members * mine, half)
    return jnp.concatenate([low, high], axis=1)


def body(tokens, encoder_weight, encoder_bias, decoder_weight, decoder_bias, targets):
    plane = lax.axis_size(("y", "x"))
    depth = lax.axis_size("zl")
    all_rows = gather_tokens(tokens)
    count, width = all_rows.shape
    chunk = width // plane
    pre_act = jnp.dot(all_rows, encoder_weight, preferred_element_type=F32) + encoder_bias
    positive = jnp.maximum(pre_act, 0.0)
    feats = (positive**2).astype(BF16)
    weight = decoder_weight[0]
    target = targets[0].astype(F32)

    partial = jnp.dot(feats, weight, preferred_element_type=F32)
    rows = lax.broadcasted_iota(jnp.int32, (count, 1), 0)
    first = lax.axis_index(FEAT) * target.shape[0]
    for i in range(target.shape[0]):
        partial = partial - jnp.where(rows == first + i, target[i : i + 1], 0.0)
    pieces = partial.astype(BF16).reshape(count, plane, chunk).transpose(1, 0, 2)
    pieces = lax.all_to_all(pieces, ("y", "x"), 0, 0, tiled=True)
    mine = jnp.sum(pieces.astype(F32), axis=0).astype(BF16)
    peers = [
        lax.ppermute(mine, "zl", [(i, i ^ k) for i in range(depth)]) for k in range(1, depth)
    ]
    a, b, c, d = [v.astype(F32) for v in [mine] + peers]
    offset = lax.axis_index(("y", "x")) * chunk
    bias = lax.dynamic_slice_in_dim(decoder_bias[0], offset, chunk, 0)
    error_part = (((a + b) + (c + d)) + bias).astype(BF16)
    recon_error = spread(error_part, ("y", "x"), plane).transpose(1, 0, 2).reshape(count, width)

    back_grad = lax.dot_general(
        weight, recon_error, (((1,), (1,)), ((), ())), preferred_element_type=F32
    )
    quarter = back_grad.shape[0] // 4
    quarters = back_grad.reshape(2, 2, quarter, count)
    zh, core = lax.axis_index("zh"), lax.axis_index("core")
    keep = lax.dynamic_index_in_dim(quarters, zh, 0, False)
    send = lax.dynamic_index_in_dim(quarters, 1 - zh, 0, False)
    pair = keep + lax.ppermute(send, "zh", SWAP)
    keep = lax.dynamic_index_in_dim(pair, core, 0, False)
    send = lax.dynamic_index_in_dim(pair, 1 - core, 0, False)
    share = (keep + lax.ppermute(send, "core", SWAP)).T

    decoder_grad = lax.dot_general(
        feats, recon_error, (((0,), (0,)), ((), ())), preferred_element_type=F32
    )
    bias_grad = jnp.sum(recon_error.astype(F32), axis=0)
    offset = lax.axis_index(TGT) * quarter
    act_grad = share * (2.0 * lax.dynamic_slice_in_dim(positive, offset, quarter, 1))
    encoder_bias_grad = jnp.sum(act_grad, axis=0)
    pre_grad = act_grad.astype(BF16)
    encoder_grad = lax.dot_general(
        all_rows, pre_grad, (((0,), (0,)), ((), ())), preferred_element_type=F32
    )
    return encoder_grad, encoder_bias_grad, decoder_grad[None], bias_grad[None]


def solution(mesh):
    split = Mesh(mesh.devices.reshape(4, 4, 4, 2, 2), FEAT + TGT)
    return jax.shard_map(
        body,
        mesh=split,
        in_specs=(
            P(FEAT, None),
            P(None, FEAT),
            P(FEAT),
            P(TGT, FEAT, None),
            P(TGT, None),
            P(TGT, FEAT, None),
        ),
        out_specs=(
            P(None, FEAT + TGT),
            P(FEAT + TGT),
            P(TGT, FEAT, None),
            P(TGT, None),
        ),
        check_vma=False,
    )
```

time: 1490 us -> 146 us (0.10)
  waiting for transfers between devices: 1450 us -> 80 us
  starting transfers between devices: 0.16 us -> 35 us
    unnamed x6 -> x0, waiting for transfers between devices: 791 us -> none
    all_gather x2 -> x0, waiting for transfers between devices: 659 us -> none  [the longest x1 349 us: body(): recon_error = lax.all_gather(error_part, 'feat', axis=0, tiled=True)]
    all_to_all x0 -> x3, waiting for transfers between devices: none -> 71.7 us  [the longest x2 46.5 us: spread(): return lax.all_to_all(copies, axes, 0, 0, tiled=True)]
    all_to_all x0 -> x3, starting transfers between devices: none -> 21.4 us  [the longest x2 17 us: spread(): return lax.all_to_all(copies, axes, 0, 0, tiled=True)]
  transfers between devices with their start and end apart: 4 -> 9, of which waited for: 4 -> 6; matrix products, arithmetic and copies ran while one was open for 0% -> 5% of each run, Pallas kernels for 0% -> 0%
where the time goes in v1:
time: 146 us
  waiting for transfers between devices  80 us (55%)
  starting transfers between devices  35 us (24%)
  local copies, waits for them, and re-layouts  14.9 us (10%)
  matrix products  9.58 us (7%)
  other arithmetic  5.34 us (4%)
    all_to_all x2, waiting for transfers between devices, spread(): return lax.all_to_all(copies, axes, 0, 0, tiled=True)  46.5 us
    all_to_all x1, waiting for transfers between devices, body(): pieces = lax.all_to_all(pieces, ('y', 'x'), 0, 0, tiled=True)  25.1 us
    all_to_all x2, starting transfers between devices, spread(): return lax.all_to_all(copies, axes, 0, 0, tiled=True)  17 us
    ppermute x3, waiting for transfers between devices, body(): lax.ppermute(mine, 'zl', [(i, i ^ k) for i in range(depth)])  6.44 us
    all_to_all x1, starting transfers between devices, body(): pieces = lax.all_to_all(pieces, ('y', 'x'), 0, 0, tiled=True)  4.4 us
    ppermute x1, starting transfers between devices, body(): pair = keep + lax.ppermute(send, 'zh', SWAP)  4.31 us
    dot_general x1, matrix products, body(): lax.dot_general(feats, recon_error, (((0,), (0,)), ((), ())), preferred_e...  4.15 us
    unnamed x14, local copies, waits for them, and re-layouts  4.12 us
  transfers between devices with their start and end apart: 9, of which 6 were waited for; matrix products, arithmetic and copies ran while one was open for 5% of the time, Pallas kernels for 0%

profile of v1, /device:TPU:1, one launch (start us, length us, event | category | flops | bytes accessed | tf_op | source)
XLA Modules:
  0.0 145.7 jit_solution(10147424198661394591)
XLA Ops:
  2.5 12.6 %all-to-all-start = ((bf16[64,48,128]{2,1,0:T(8,128)(2,1)}), bf16[64,48,128]{2,1,0:T(8,128)(2,1)S(1)}, u32[]{:S(2)}, u32[]{:S(2)}) async-start(bf16[64,48,128]{2,1,0:T(8,128)(2,1)} %broadcast_in_dim.70), calls=%async_computation | async-start | bytes 1572864 | tf_op jit(solution)/shard_map/all_to_all | solution.py:15
  15.2 22.0 %all-to-all-done = bf16[64,48,128]{2,1,0:T(8,128)(2,1)S(1)} async-done(((bf16[64,48,128]{2,1,0:T(8,128)(2,1)}), bf16[64,48,128]{2,1,0:T(8,128)(2,1)S(1)}, u32[]{:S(2)}, u32[]{:S(2)}) %all-to-all-start) | async-done | bytes 786464 | tf_op jit(solution)/shard_map/all_to_all | solution.py:15
  37.1 2.4 %collective-permute-start = (bf16[64,48,128]{2,1,0:T(8,128)(2,1)S(1)}, bf16[64,48,128]{2,1,0:T(8,128)(2,1)S(1)}, u32[]{:S(2)}, u32[]{:S(2)}) collective-permute-start(bf16[64,48,128]{2,1,0:T(8,128)(2,1)S(1)} %all-to-all-done), channel_id=1, source_target_pairs={{0,1},{1,0},{2,3},{3,2},{4,5},{5,4},{6,7},{7,6},{8,9},{9,8},{10,11... | collective-permute-start | bytes 2359304 | tf_op jit(solution)/shard_map/ppermute | solution.py:26
  39.6 1.9 %collective-permute-done = bf16[64,48,128]{2,1,0:T(8,128)(2,1)S(1)} collective-permute-done((bf16[64,48,128]{2,1,0:T(8,128)(2,1)S(1)}, bf16[64,48,128]{2,1,0:T(8,128)(2,1)S(1)}, u32[]{:S(2)}, u32[]{:S(2)}) %collective-permute-start) | collective-permute-done | bytes 786464 | tf_op jit(solution)/shard_map/ppermute | solution.py:26
  41.4 1.3 broadcast_select_fusion
  42.8 1.4 reshape.53
  44.2 2.2 %reshape.52 = bf16[192,2048]{1,0:T(8,128)(2,1)} reshape(bf16[64,48,128]{2,1,0:T(8,128)(2,1)} %get-tuple-element.7) | data formatting | bytes 1572864 | tf_op jit(solution)/shard_map/reshape | solution.py:27
  46.4 1.3 constant_dynamic-update-slice_fusion.1
  50.6 1.3 copy.25
  51.9 4.4 %all-to-all-start.1 = ((bf16[16,192,256]{2,1,0:T(8,128)(2,1)}), bf16[16,192,256]{2,1,0:T(8,128)(2,1)}, u32[]{:S(2)}, u32[]{:S(2)}) async-start(bf16[16,192,256]{2,1,0:T(8,128)(2,1)} %bitcast.51), calls=%async_computation.1 | async-start | bytes 3145728 | tf_op jit(solution)/shard_map/all_to_all | solution.py:50
  56.3 25.1 %all-to-all-done.1 = bf16[16,192,256]{2,1,0:T(8,128)(2,1)} async-done(((bf16[16,192,256]{2,1,0:T(8,128)(2,1)}), bf16[16,192,256]{2,1,0:T(8,128)(2,1)}, u32[]{:S(2)}, u32[]{:S(2)}) %all-to-all-start.1) | async-done | bytes 1572896 | tf_op jit(solution)/shard_map/all_to_all | solution.py:50
  81.4 1.6 %reduce_sum.30 = bf16[192,256]{1,0:T(8,128)(2,1)S(1)} reduce(bf16[16,192,256]{2,1,0:T(8,128)(2,1)} %all-to-all-done.1, bf16[]{:T(256)} %constant.57.clone.1), dimensions={0}, to_apply=%region_0.1 | reduce | flops 737280 | bytes 1671170 | tf_op jit(solution)/shard_map/reduce_sum | solution.py:51
  84.0 2.7 %collective-permute-start.1 = (bf16[192,256]{1,0:T(8,128)(2,1)S(1)}, bf16[192,256]{1,0:T(8,128)(2,1)S(1)}, u32[]{:S(2)}, u32[]{:S(2)}) collective-permute-start(bf16[192,256]{1,0:T(8,128)(2,1)S(1)} %reduce_sum.30), channel_id=1, source_target_pairs={{0,64},{64,0},{128,192},{192,128},{1,65},{65,1},{129,193},{193,129... | collective-permute-start | bytes 294920 | tf_op jit(solution)/shard_map/ppermute | solution.py:53
  87.4 1.2 collective-permute-done.3
  88.6 5.2 %collective-permute-done.2 = bf16[192,256]{1,0:T(8,128)(2,1)S(1)} collective-permute-done((bf16[192,256]{1,0:T(8,128)(2,1)S(1)}, bf16[192,256]{1,0:T(8,128)(2,1)S(1)}, u32[]{:S(2)}, u32[]{:S(2)}) %collective-permute-start.2) | collective-permute-done | bytes 98336 | tf_op jit(solution)/shard_map/ppermute | solution.py:53
  93.9 1.3 broadcast_in_dim.81
  95.2 4.4 %all-to-all-start.2 = ((bf16[16,192,256]{2,1,0:T(8,128)(2,1)}), bf16[16,192,256]{2,1,0:T(8,128)(2,1)}, u32[]{:S(2)}, u32[]{:S(2)}) async-start(bf16[16,192,256]{2,1,0:T(8,128)(2,1)} %broadcast_in_dim.81), calls=%async_computation.2 | async-start | bytes 3145728 | tf_op jit(solution)/shard_map/all_to_all | solution.py:15
  99.6 24.6 %all-to-all-done.2 = bf16[16,192,256]{2,1,0:T(8,128)(2,1)} async-done(((bf16[16,192,256]{2,1,0:T(8,128)(2,1)}), bf16[16,192,256]{2,1,0:T(8,128)(2,1)}, u32[]{:S(2)}, u32[]{:S(2)}) %all-to-all-start.2) | async-done | bytes 1572896 | tf_op jit(solution)/shard_map/all_to_all | solution.py:15
  124.2 1.6 %copy.22 = bf16[16,24,8,256]{3,2,0,1:T(8,128)(2,1)S(1)} copy(bf16[16,24,8,256]{3,2,1,0:T(8,128)(2,1)} %bitcast.17) | data formatting | bytes 3145728 | tf_op jit(solution)/shard_map/reshape | solution.py:59
  127.9 4.3 %collective-permute-start.4 = (f32[2,64,192]{2,1,0:T(8,128)S(1)}, f32[2,64,192]{2,1,0:T(8,128)S(1)}, u32[]{:S(2)}, u32[]{:S(2)}) collective-permute-start(f32[2,64,192]{2,1,0:T(8,128)S(1)} %dynamic-slice_bitcast_fusion), channel_id=1, source_target_pairs={{0,2},{2,0},{1,3},{3,1},{4,6},{6,4},{5,7},{7,5},{8,10},{10,8},{9,1... | collective-permute-start | bytes 294920 | tf_op jit(solution)/shard_map/ppermute | solution.py:69
  132.2 4.2 %convolution_bitcast_fusion = f32[1,256,4096]{2,1,0:T(8,128)} fusion(bf16[192,4096]{1,0:T(8,128)(2,1)} %bitcast.50, f32[192,256]{1,0:T(8,128)S(1)} %fusion.6), kind=kOutput, calls=%fused_computation | convolution fusion | flops 402751488 | bytes 5963776 | tf_op jit(solution)/shard_map/dot_general | solution.py:74
  136.5 3.3 %collective-permute-start.5 = (f32[64,192]{0,1:T(8,128)S(1)}, f32[64,192]{0,1:T(8,128)S(1)}, u32[]{:S(2)}, u32[]{:S(2)}) collective-permute-start(f32[64,192]{0,1:T(8,128)S(1)} %bitcast.55), channel_id=1, source_target_pairs={{0,1},{1,0},{2,3},{3,2},{4,5},{5,4},{6,7},{7,6},{8,9},{9,8},{10,11... | collective-permute-start | bytes 147464 | tf_op jit(solution)/shard_map/ppermute | solution.py:72
  139.8 1.6 %convert_reduce_fusion = f32[16,256]{1,0:T(8,128)S(1)} fusion(bf16[16,192,256]{2,1,0:T(8,128)(2,1)} %all-to-all-done.2), kind=kLoop, calls=%fused_computation.5 | loop fusion | flops 1568768 | bytes 1589248 | tf_op jit(solution)/shard_map/reduce_sum | solution.py:77
  142.8 2.8 %fusion.10 = f32[4096,64]{0,1:T(8,128)} fusion(bf16[192,4096]{1,0:T(8,128)(2,1)} %copy-done.2, bf16[192,64]{1,0:T(8,128)(2,1)S(1)} %get-tuple-element.5), kind=kOutput, calls=%fused_computation.21 | convolution fusion | flops 100663296 | bytes 2646016 | tf_op jit(solution)/shard_map/dot_general | solution.py:82
  (37 shorter events, 10.1 us)
Async XLA Ops:
  0.6 48.7 %copy-start = (bf16[1,256,4096]{2,1,0:T(8,128)(2,1)S(1)}, bf16[1,256,4096]{2,1,0:T(8,128)(2,1)}, u32[]{:S(2)}) copy-start(bf16[1,256,4096]{2,1,0:T(8,128)(2,1)} %param.9) | copy-start | bytes 6291460
  0.6 38.9 %copy-start.3 = (bf16[1,3,4096]{2,1,0:T(4,128)(2,1)S(1)}, bf16[1,3,4096]{2,1,0:T(4,128)(2,1)}, u32[]{:S(2)}) copy-start(bf16[1,3,4096]{2,1,0:T(4,128)(2,1)} %param.11) | copy-start | bytes 73732
  2.5 34.6 %all-to-all-start = ((bf16[64,48,128]{2,1,0:T(8,128)(2,1)}), bf16[64,48,128]{2,1,0:T(8,128)(2,1)S(1)}, u32[]{:S(2)}, u32[]{:S(2)}) async-start(bf16[64,48,128]{2,1,0:T(8,128)(2,1)} %broadcast_in_dim.70), calls=%async_computation | async-start | bytes 1572864 | tf_op jit(solution)/shard_map/all_to_all | solution.py:15
  37.1 4.3 %collective-permute-start = (bf16[64,48,128]{2,1,0:T(8,128)(2,1)S(1)}, bf16[64,48,128]{2,1,0:T(8,128)(2,1)S(1)}, u32[]{:S(2)}, u32[]{:S(2)}) collective-permute-start(bf16[64,48,128]{2,1,0:T(8,128)(2,1)S(1)} %all-to-all-done), channel_id=1, source_target_pairs={{0,1},{1,0},{2,3},{3,2},{4,5},{5,4},{6,7},{7,6},{8,9},{9,8},{10,11... | collective-permute-start | bytes 2359304 | tf_op jit(solution)/shard_map/ppermute | solution.py:26
  46.4 1.8 %copy-start.4 = (bf16[4096,256]{1,0:T(8,128)(2,1)S(1)}, bf16[4096,256]{1,0:T(8,128)(2,1)}, u32[]{:S(2)}) copy-start(bf16[4096,256]{1,0:T(8,128)(2,1)} %param.7) | copy-start | bytes 6291460
  46.4 1.8 %copy-start.5 = (f32[256]{0:T(256)S(1)}, f32[256]{0:T(256)}, u32[]{:S(2)}) copy-start(f32[256]{0:T(256)} %param.8) | copy-start | bytes 3076
  48.2 1.2 copy-start.2
  51.9 29.5 %all-to-all-start.1 = ((bf16[16,192,256]{2,1,0:T(8,128)(2,1)}), bf16[16,192,256]{2,1,0:T(8,128)(2,1)}, u32[]{:S(2)}, u32[]{:S(2)}) async-start(bf16[16,192,256]{2,1,0:T(8,128)(2,1)} %bitcast.51), calls=%async_computation.1 | async-start | bytes 3145728 | tf_op jit(solution)/shard_map/all_to_all | solution.py:50
  83.0 5.5 %collective-permute-start.3 = (bf16[192,256]{1,0:T(8,128)(2,1)S(1)}, bf16[192,256]{1,0:T(8,128)(2,1)S(1)}, u32[]{:S(2)}, u32[]{:S(2)}) collective-permute-start(bf16[192,256]{1,0:T(8,128)(2,1)S(1)} %reduce_sum.30), channel_id=1, source_target_pairs={{0,192},{64,128},{128,64},{192,0},{1,193},{65,129},{129,65},{193,1... | collective-permute-start | bytes 294920 | tf_op jit(solution)/shard_map/ppermute | solution.py:53
  84.0 9.8 %collective-permute-start.2 = (bf16[192,256]{1,0:T(8,128)(2,1)S(1)}, bf16[192,256]{1,0:T(8,128)(2,1)S(1)}, u32[]{:S(2)}, u32[]{:S(2)}) collective-permute-start(bf16[192,256]{1,0:T(8,128)(2,1)S(1)} %reduce_sum.30), channel_id=1, source_target_pairs={{0,128},{64,192},{128,0},{192,64},{1,129},{65,193},{129,1},{193,65... | collective-permute-start | bytes 294920 | tf_op jit(solution)/shard_map/ppermute | solution.py:53
  84.0 9.8 %collective-permute-start.1 = (bf16[192,256]{1,0:T(8,128)(2,1)S(1)}, bf16[192,256]{1,0:T(8,128)(2,1)S(1)}, u32[]{:S(2)}, u32[]{:S(2)}) collective-permute-start(bf16[192,256]{1,0:T(8,128)(2,1)S(1)} %reduce_sum.30), channel_id=1, source_target_pairs={{0,64},{64,0},{128,192},{192,128},{1,65},{65,1},{129,193},{193,129... | collective-permute-start | bytes 294920 | tf_op jit(solution)/shard_map/ppermute | solution.py:53
  95.2 29.0 %all-to-all-start.2 = ((bf16[16,192,256]{2,1,0:T(8,128)(2,1)}), bf16[16,192,256]{2,1,0:T(8,128)(2,1)}, u32[]{:S(2)}, u32[]{:S(2)}) async-start(bf16[16,192,256]{2,1,0:T(8,128)(2,1)} %broadcast_in_dim.81), calls=%async_computation.2 | async-start | bytes 3145728 | tf_op jit(solution)/shard_map/all_to_all | solution.py:15
  125.7 1.2 copy-start.1
  127.9 8.5 %collective-permute-start.4 = (f32[2,64,192]{2,1,0:T(8,128)S(1)}, f32[2,64,192]{2,1,0:T(8,128)S(1)}, u32[]{:S(2)}, u32[]{:S(2)}) collective-permute-start(f32[2,64,192]{2,1,0:T(8,128)S(1)} %dynamic-slice_bitcast_fusion), channel_id=1, source_target_pairs={{0,2},{2,0},{1,3},{3,1},{4,6},{6,4},{5,7},{7,5},{8,10},{10,8},{9,1... | collective-permute-start | bytes 294920 | tf_op jit(solution)/shard_map/ppermute | solution.py:69
  136.5 5.7 %collective-permute-start.5 = (f32[64,192]{0,1:T(8,128)S(1)}, f32[64,192]{0,1:T(8,128)S(1)}, u32[]{:S(2)}, u32[]{:S(2)}) collective-permute-start(f32[64,192]{0,1:T(8,128)S(1)} %bitcast.55), channel_id=1, source_target_pairs={{0,1},{1,0},{2,3},{3,2},{4,5},{5,4},{6,7},{7,6},{8,9},{9,8},{10,11... | collective-permute-start | bytes 147464 | tf_op jit(solution)/shard_map/ppermute | solution.py:72

commit v2 on v0

v2 whole, which is shorter than its diff:
```python
import functools

import jax
import jax.numpy as jnp
from jax import lax
from jax.experimental import pallas as pl
from jax.experimental.pallas import tpu as pltpu
from jax.sharding import Mesh, PartitionSpec as P

BF16 = jnp.bfloat16
F32 = jnp.float32
FEAT = ("zl", "y", "x")
TGT = ("zh", "core")
PLANE = ("y", "x")
TN = (((0,), (0,)), ((), ()))
NT = (((1,), (1,)), ((), ()))

J, ROWS, DEPTH, D, FEATS = 16, 3, 4, 4096, 256
COUNT = J * ROWS * DEPTH
CHUNK = D // J
WIDE = D // 4


def in_vmem(x):
    return pltpu.with_memory_space_constraint(x, pltpu.VMEM)


def call(kernel, outs, *args, vmem=(), **kwargs):
    args = [in_vmem(a) if i in vmem else a for i, a in enumerate(args)]
    return pl.pallas_call(
        kernel,
        out_shape=outs,
        compiler_params=pltpu.CompilerParams(vmem_limit_bytes=40 * 1024 * 1024),
        **kwargs,
    )(*args)


def pack_kernel(own_ref, below_ref, above_ref, far_ref, out_ref):
    core, zl = lax.axis_index("core"), lax.axis_index("zl")
    sub = lax.broadcasted_iota(jnp.int32, (8, WIDE), 0)
    start = pl.multiple_of(core * (D // 2), D // 2)
    sources = [(own_ref, 0), (below_ref, 3), (above_ref, 1), (far_ref, 2)]
    blocks = [(ref[:, pl.ds(start, D // 2)].astype(F32), (zl + step) % 4) for ref, step in sources]
    for i in range(ROWS):
        tile = jnp.zeros((8, WIDE), F32)
        for block, depth in blocks:
            for h in range(2):
                row = block[i : i + 1, h * WIDE : (h + 1) * WIDE]
                tile = jnp.where(sub == depth + 4 * h, row, tile)
        tile = tile.astype(BF16)
        for j in range(J):
            out_ref[j, i] = tile


def forward_kernel(own_ref, other_ref, enc_ref, enc_bias_ref, dec_ref, target_ref, out_ref, pos_ref, feats_ref, acc_ref):
    core, zl = lax.axis_index("core"), lax.axis_index("zl")
    member = lax.axis_index(PLANE)
    sums = []
    for h in range(2):
        mine = pl.multiple_of(core * (D // 2) + h * WIDE, WIDE)
        theirs = pl.multiple_of((1 - core) * (D // 2) + h * WIDE, WIDE)
        sums.append(
            jnp.dot(own_ref[...], enc_ref[pl.ds(mine, WIDE), :], preferred_element_type=F32)
            + jnp.dot(other_ref[...], enc_ref[pl.ds(theirs, WIDE), :], preferred_element_type=F32)
        )
    low, high = [s.reshape(COUNT // 8, 2, 8, FEATS) for s in sums]
    sub = lax.broadcasted_iota(jnp.int32, (COUNT // 8, 8, FEATS), 1)
    both = []
    for g in range(2):
        part = jnp.where(sub < 4, low[:, g], high[:, g])
        both.append(part + pltpu.roll(part, 4, 1))
    pre = jnp.where(sub < 4, both[0], both[1]).reshape(COUNT, FEATS) + enc_bias_ref[...]
    positive = jnp.maximum(pre, 0.0)
    pos_ref[...] = positive
    feats = (positive * positive).astype(BF16)
    feats_ref[...] = feats
    lane_sub = lax.broadcasted_iota(jnp.int32, (8, CHUNK), 0)
    for j in range(J):
        acc_ref[j % 2] = jnp.dot(feats, dec_ref[:, j * CHUNK : (j + 1) * CHUNK], preferred_element_type=F32)
        for i in range(ROWS):
            group = ROWS * member + i
            tile = pl.ds(pl.multiple_of(8 * (group // 2), 8), 8)
            row = 4 * (group % 2) + zl
            value = target_ref[i : i + 1, j * CHUNK : (j + 1) * CHUNK].astype(F32)
            acc_ref[j % 2, tile, :] = acc_ref[j % 2, tile, :] - jnp.where(lane_sub == row, value, 0.0)
        out_ref[j] = acc_ref[j % 2].astype(BF16)


def sum_kernel(pieces_ref, out_ref):
    total = pieces_ref[0].astype(F32)
    for j in range(1, J):
        total = total + pieces_ref[j].astype(F32)
    out_ref[...] = total.astype(BF16)


def error_kernel(a_ref, b_ref, c_ref, d_ref, bias_ref, out_ref):
    member = lax.axis_index(PLANE)
    a, b, c, d = [ref[...].astype(F32) for ref in (a_ref, b_ref, c_ref, d_ref)]
    bias = bias_ref[:, pl.ds(pl.multiple_of(member * CHUNK, CHUNK), CHUNK)]
    error = (((a + b) + (c + d)) + bias).astype(BF16)
    for j in range(J):
        out_ref[j] = error


def back_kernel(error_ref, dec_ref, keep_ref, send_ref):
    zh = lax.axis_index("zh")
    total = jnp.zeros((COUNT, FEATS), F32)
    for j in range(J):
        total = total + lax.dot_general(
            error_ref[j], dec_ref[:, j * CHUNK : (j + 1) * CHUNK], NT, preferred_element_type=F32
        )
    half = FEATS // 2
    keep_ref[...] = jnp.where(zh == 0, total[:, :half], total[:, half:])
    send_ref[...] = jnp.where(zh == 0, total[:, half:], total[:, :half]).astype(BF16)


def decoder_kernel(error_ref, feats_ref, grad_ref, bias_ref):
    grad_ref[...] = lax.dot_general(feats_ref[...], error_ref[0], TN, preferred_element_type=F32)
    bias_ref[...] = jnp.sum(error_ref[0].astype(F32), axis=0, keepdims=True)


def encoder_kernel(own_ref, other_ref, keep_ref, near_ref, far_ref, cross_ref, pos_ref, grad_ref, bias_ref):
    core, zh = lax.axis_index("core"), lax.axis_index("zh")
    quarter = FEATS // 4
    half = pl.multiple_of(zh * (FEATS // 2), FEATS // 2)
    share = (keep_ref[...] + near_ref[...]) + (far_ref[...].astype(F32) + cross_ref[...].astype(F32))
    act = share * (2.0 * pos_ref[:, pl.ds(half, FEATS // 2)])
    act = jnp.where(core == 0, act[:, :quarter], act[:, quarter:])
    bias_ref[...] = jnp.sum(act, axis=0, keepdims=True)
    tiles = act.astype(BF16).astype(F32).reshape(COUNT // 8, 8, quarter)
    turned = pltpu.roll(tiles, 4, 1)
    sub = lax.broadcasted_iota(jnp.int32, tiles.shape, 1)
    zero = jnp.zeros_like(tiles)
    low = jnp.stack([jnp.where(sub < 4, tiles, zero), jnp.where(sub < 4, turned, zero)], axis=1)
    high = jnp.stack([jnp.where(sub < 4, zero, turned), jnp.where(sub < 4, zero, tiles)], axis=1)
    for h, side in enumerate((low, high)):
        side = side.reshape(2 * COUNT, quarter).astype(BF16)
        for ref, owner in ((own_ref, core), (other_ref, 1 - core)):
            start = pl.multiple_of(owner * (D // 2) + h * WIDE, WIDE)
            grad_ref[:, pl.ds(start, WIDE)] = lax.dot_general(side, ref[...], TN, preferred_element_type=F32)


def ring(step):
    index = lambda z: (z % 4) * 2 + z // 4
    return [(index(z), index((z + step) % 8)) for z in range(8)]


def mirror(axes, size, key):
    return lambda x: lax.ppermute(x, axes, [(i, i ^ key) for i in range(size)])


def body(tokens, encoder_weight, encoder_bias, decoder_weight, decoder_bias, targets):
    sds = jax.ShapeDtypeStruct
    below, above, far = [lax.ppermute(tokens, ("zl", "zh"), ring(step)) for step in (1, 7, 2)]
    packed = call(pack_kernel, pltpu.VMEM((J, ROWS, 8, WIDE), BF16), tokens, below, above, far)
    own = lax.all_to_all(packed, PLANE, 0, 0, tiled=True).reshape(2 * COUNT, WIDE)
    other = mirror("core", 2, 1)(own)
    dec = decoder_weight[0]
    pieces, positive, feats = call(
        forward_kernel,
        (pltpu.VMEM((J, COUNT, CHUNK), BF16), pltpu.VMEM((COUNT, FEATS), F32), pltpu.VMEM((COUNT, FEATS), BF16)),
        own, other, encoder_weight, encoder_bias[None], dec, targets[0],
        vmem=(0, 1, 2, 4),
        scratch_shapes=[pltpu.VMEM((2, COUNT, CHUNK), F32)],
    )
    pieces = lax.all_to_all(pieces, PLANE, 0, 0, tiled=True)
    part = call(sum_kernel, pltpu.VMEM((COUNT, CHUNK), BF16), pieces, vmem=(0,))
    peers = [mirror("zl", DEPTH, key)(part) for key in (1, 2, 3)]
    copies = call(error_kernel, pltpu.VMEM((J, COUNT, CHUNK), BF16), part, *peers, decoder_bias, vmem=(0, 1, 2, 3))
    errors = lax.all_to_all(copies, PLANE, 0, 0, tiled=True)
    keep, send = call(
        back_kernel,
        (pltpu.VMEM((COUNT, FEATS // 2), F32), pltpu.VMEM((COUNT, FEATS // 2), BF16)),
        errors, dec,
        vmem=(0, 1),
    )
    near = mirror(TGT, 4, 1)(keep)
    back = [mirror(TGT, 4, key)(send) for key in (2, 3)]
    decoder_grad, bias_grad = call(
        decoder_kernel,
        (sds((FEATS, D), F32), sds((1, D), F32)),
        errors, feats,
        vmem=(0, 1),
        grid=(J,),
        in_specs=[
            pl.BlockSpec((1, COUNT, CHUNK), lambda j: (j, 0, 0)),
            pl.BlockSpec((COUNT, FEATS), lambda j: (0, 0)),
        ],
        out_specs=(pl.BlockSpec((FEATS, CHUNK), lambda j: (0, j)), pl.BlockSpec((1, CHUNK), lambda j: (0, j))),
    )
    encoder_grad, encoder_bias_grad = call(
        encoder_kernel,
        (sds((FEATS // 4, D), F32), sds((1, FEATS // 4), F32)),
        own, other, keep, near, *back, positive,
        vmem=(0, 1, 2, 3, 4, 5, 6),
    )
    return encoder_grad.T, encoder_bias_grad[0], decoder_grad[None], bias_grad


def solution(mesh):
    split = Mesh(mesh.devices.reshape(4, 4, 4, 2, 2), FEAT + TGT)
    return jax.shard_map(
        body,
        mesh=split,
        in_specs=(
            P(FEAT, None),
            P(None, FEAT),
            P(FEAT),
            P(TGT, FEAT, None),
            P(TGT, None),
            P(TGT, FEAT, None),
        ),
        out_specs=(
            P(None, FEAT + TGT),
            P(FEAT + TGT),
            P(TGT, FEAT, None),
            P(TGT, None),
        ),
        check_vma=False,
    )
```

time: 1490 us -> 118 us (0.08)
  waiting for transfers between devices: 1450 us -> 12.1 us
  blocking collectives: 0 us -> 68 us
  starting transfers between devices: 0.16 us -> 22.1 us
    unnamed x6 -> x0, waiting for transfers between devices: 791 us -> none
    all_gather x2 -> x0, waiting for transfers between devices: 659 us -> none  [the longest x1 349 us: body(): recon_error = lax.all_gather(error_part, 'feat', axis=0, tiled=True)]
    all_to_all x0 -> x3, blocking collectives: none -> 68 us  [the longest x1 24.8 us: body(): errors = lax.all_to_all(copies, PLANE, 0, 0, tiled=True)]
    ppermute x0 -> x10, starting transfers between devices: none -> 22.1 us  [the longest x7 15.7 us: mirror(): return lambda x: lax.ppermute(x, axes, [(i, i ^ key) for i in range(size)])]
  transfers between devices with their start and end apart: 4 -> 10, of which waited for: 4 -> 6; matrix products, arithmetic and copies ran while one was open for 0% -> 0% of each run, Pallas kernels for 0% -> 7%
where the time goes in v2:
time: 118 us
  blocking collectives  68 us (58%)
  starting transfers between devices  22.1 us (19%)
  Pallas kernels  12.5 us (11%)
  waiting for transfers between devices  12.1 us (10%)
  local copies, waits for them, and re-layouts  2.36 us (2%)
    all_to_all x1, blocking collectives, body(): errors = lax.all_to_all(copies, PLANE, 0, 0, tiled=True)  24.8 us
    all_to_all x1, blocking collectives, body(): pieces = lax.all_to_all(pieces, PLANE, 0, 0, tiled=True)  24.6 us
    all_to_all x1, blocking collectives, body(): lax.all_to_all(packed, PLANE, 0, 0, tiled=True).reshape(2 * COUNT, WIDE)  18.6 us
    ppermute x7, starting transfers between devices, mirror(): return lambda x: lax.ppermute(x, axes, [(i, i ^ key) for i in range(size)])  15.7 us
    pallas_call x7, Pallas kernels, call(): pl.pallas_call(kernel, out_shape=outs, compiler_params=pltpu.CompilerPara...  12.5 us
    ppermute x7, waiting for transfers between devices, mirror(): return lambda x: lax.ppermute(x, axes, [(i, i ^ key) for i in range(size)])  6.94 us
    ppermute x3, starting transfers between devices, body(): lax.ppermute(tokens, ('zl', 'zh'), ring(step))  6.49 us
    ppermute x3, waiting for transfers between devices, body(): lax.ppermute(tokens, ('zl', 'zh'), ring(step))  5.18 us
  transfers between devices with their start and end apart: 10, of which 6 were waited for; matrix products, arithmetic and copies ran while one was open for 0% of the time, Pallas kernels for 7%

profile of v2, /device:TPU:1, one launch (start us, length us, event | category | flops | bytes accessed | tf_op | source)
XLA Modules:
  0.0 117.9 jit_solution(5760428439480185989)
XLA Ops:
  0.7 6.5 %collective-permute-start.1 = (bf16[3,4096]{1,0:T(4,128)(2,1)}, bf16[3,4096]{1,0:T(4,128)(2,1)S(1)}, u32[]{:S(2)}, u32[]{:S(2)}) collective-permute-start(bf16[3,4096]{1,0:T(4,128)(2,1)} %own_ref.1), channel_id=1, source_target_pairs={{0,194},{64,0},{128,64},{192,128},{2,192},{66,2},{130,66},{194,130... | collective-permute-start | bytes 73736 | tf_op jit(solution)/shard_map/ppermute | solution.py:154
  7.1 1.3 %collective-permute-done.1.above_ref = bf16[3,4096]{1,0:T(4,128)(2,1)S(1)} collective-permute-done((bf16[3,4096]{1,0:T(4,128)(2,1)}, bf16[3,4096]{1,0:T(4,128)(2,1)S(1)}, u32[]{:S(2)}, u32[]{:S(2)}) %collective-permute-start.1) | collective-permute-done | bytes 24608 | tf_op jit(solution)/shard_map/ppermute | solution.py:154
  8.5 2.8 %collective-permute-done.below_ref = bf16[3,4096]{1,0:T(4,128)(2,1)S(1)} collective-permute-done((bf16[3,4096]{1,0:T(4,128)(2,1)}, bf16[3,4096]{1,0:T(4,128)(2,1)S(1)}, u32[]{:S(2)}, u32[]{:S(2)}) %collective-permute-start) | collective-permute-done | bytes 24608 | tf_op jit(solution)/shard_map/ppermute | solution.py:154
  11.3 1.0 collective-permute-done.2.far_ref
  12.3 0.8 copy-done.3
  13.2 18.6 %all_to_all.15 = bf16[16,3,8,1024]{3,2,1,0:T(8,128)(2,1)S(1)} all-to-all(bf16[16,3,8,1024]{3,2,1,0:T(8,128)(2,1)S(1)} %shard_map.93), channel_id=1, replica_groups=mesh['zl'=4,'y'=4,'x'=4,'zh'=2,'core'=2] {'y','x'}, dimensions={0} | all-to-all | bytes 1572864 | tf_op jit(solution)/shard_map/all_to_all | solution.py:156
  31.8 3.3 %collective-permute-start.3 = (bf16[384,1024]{1,0:T(8,128)(2,1)S(1)}, bf16[384,1024]{1,0:T(8,128)(2,1)S(1)}, u32[]{:S(2)}, u32[]{:S(2)}) collective-permute-start(bf16[384,1024]{1,0:T(8,128)(2,1)S(1)} %bitcast.9), channel_id=1, source_target_pairs={{0,1},{1,0},{2,3},{3,2},{4,5},{5,4},{6,7},{7,6},{8,9},{9,8},{10,11... | collective-permute-start | bytes 2359304 | tf_op jit(solution)/shard_map/ppermute | solution.py:149
  35.1 1.9 %collective-permute-done.3.other_ref = bf16[384,1024]{1,0:T(8,128)(2,1)S(1)} collective-permute-done((bf16[384,1024]{1,0:T(8,128)(2,1)S(1)}, bf16[384,1024]{1,0:T(8,128)(2,1)S(1)}, u32[]{:S(2)}, u32[]{:S(2)}) %collective-permute-start.3) | collective-permute-done | bytes 786464 | tf_op jit(solution)/shard_map/ppermute | solution.py:149
  37.0 1.6 %copy-done.1 = bf16[4096,256]{1,0:T(8,128)(2,1)S(1)} copy-done((bf16[4096,256]{1,0:T(8,128)(2,1)S(1)}, bf16[4096,256]{1,0:T(8,128)(2,1)}, u32[]{:S(2)}) %copy-start.1) | copy-done | bytes 2097176
  38.6 1.8 %shard_map.94 = (bf16[16,192,256]{2,1,0:T(8,128)(2,1)S(1)}, f32[192,256]{1,0:T(8,128)S(1)}, bf16[192,256]{1,0:T(8,128)(2,1)S(1)}) custom-call(bf16[384,1024]{1,0:T(8,128)(2,1)S(1)} %bitcast.10, bf16[384,1024]{1,0:T(8,128)(2,1)S(1)} %collective-permute-done.3.other_ref, bf16[4096,256]{1,0:T(8,128)(2,1)S(1)} %copy-done.1, f32[1,256]{1,0:T(1,128)S(1)} %bitcast.13, ...), custom_call_target="tpu_custom_call" | custom-call | tf_op jit(solution)/shard_map/pallas_call | solution.py:30
  40.4 24.6 %all_to_all.16.pieces_ref = bf16[16,192,256]{2,1,0:T(8,128)(2,1)S(1)} all-to-all(bf16[16,192,256]{2,1,0:T(8,128)(2,1)S(1)} %get-tuple-element.13), channel_id=1, replica_groups=mesh['zl'=4,'y'=4,'x'=4,'zh'=2,'core'=2] {'y','x'}, dimensions={0} | all-to-all | bytes 3145728 | tf_op jit(solution)/shard_map/all_to_all | solution.py:166
  65.0 0.2 shard_map.95.a_ref
  65.2 0.5 collective-permute-start.6
  65.7 1.3 %collective-permute-start.5 = (bf16[192,256]{1,0:T(8,128)(2,1)S(1)}, bf16[192,256]{1,0:T(8,128)(2,1)S(1)}, u32[]{:S(2)}, u32[]{:S(2)}) collective-permute-start(bf16[192,256]{1,0:T(8,128)(2,1)S(1)} %shard_map.95.a_ref), channel_id=1, source_target_pairs={{0,128},{64,192},{128,0},{192,64},{1,129},{65,193},{129,1},{193,65... | collective-permute-start | bytes 294920 | tf_op jit(solution)/shard_map/ppermute | solution.py:149
  67.0 1.8 %collective-permute-start.4 = (bf16[192,256]{1,0:T(8,128)(2,1)S(1)}, bf16[192,256]{1,0:T(8,128)(2,1)S(1)}, u32[]{:S(2)}, u32[]{:S(2)}) collective-permute-start(bf16[192,256]{1,0:T(8,128)(2,1)S(1)} %shard_map.95.a_ref), channel_id=1, source_target_pairs={{0,64},{64,0},{128,192},{192,128},{1,65},{65,1},{129,193},{193,129... | collective-permute-start | bytes 294920 | tf_op jit(solution)/shard_map/ppermute | solution.py:149
  68.8 1.9 %collective-permute-done.6.d_ref = bf16[192,256]{1,0:T(8,128)(2,1)S(1)} collective-permute-done((bf16[192,256]{1,0:T(8,128)(2,1)S(1)}, bf16[192,256]{1,0:T(8,128)(2,1)S(1)}, u32[]{:S(2)}, u32[]{:S(2)}) %collective-permute-start.6) | collective-permute-done | bytes 98336 | tf_op jit(solution)/shard_map/ppermute | solution.py:149
  70.7 3.1 %collective-permute-done.5.c_ref = bf16[192,256]{1,0:T(8,128)(2,1)S(1)} collective-permute-done((bf16[192,256]{1,0:T(8,128)(2,1)S(1)}, bf16[192,256]{1,0:T(8,128)(2,1)S(1)}, u32[]{:S(2)}, u32[]{:S(2)}) %collective-permute-start.5) | collective-permute-done | bytes 98336 | tf_op jit(solution)/shard_map/ppermute | solution.py:149
  74.0 24.8 %all_to_all.17.error_ref = bf16[16,192,256]{2,1,0:T(8,128)(2,1)S(1)} all-to-all(bf16[16,192,256]{2,1,0:T(8,128)(2,1)S(1)} %shard_map.96), channel_id=1, replica_groups=mesh['zl'=4,'y'=4,'x'=4,'zh'=2,'core'=2] {'y','x'}, dimensions={0} | all-to-all | bytes 3145728 | tf_op jit(solution)/shard_map/all_to_all | solution.py:170
  98.8 0.9 shard_map.97
  99.7 3.4 %collective-permute-start.7 = (f32[192,128]{1,0:T(8,128)S(1)}, f32[192,128]{1,0:T(8,128)S(1)}, u32[]{:S(2)}, u32[]{:S(2)}) collective-permute-start(f32[192,128]{1,0:T(8,128)S(1)} %get-tuple-element.14.keep_ref), channel_id=1, source_target_pairs={{0,1},{1,0},{2,3},{3,2},{4,5},{5,4},{6,7},{7,6},{8,9},{9,8},{10,11... | collective-permute-start | bytes 294920 | tf_op jit(solution)/shard_map/ppermute | solution.py:149
  103.1 4.1 %collective-permute-start.9 = (bf16[192,128]{1,0:T(8,128)(2,1)S(1)}, bf16[192,128]{1,0:T(8,128)(2,1)S(1)}, u32[]{:S(2)}, u32[]{:S(2)}) collective-permute-start(bf16[192,128]{1,0:T(8,128)(2,1)S(1)} %get-tuple-element.15), channel_id=1, source_target_pairs={{0,3},{1,2},{2,1},{3,0},{4,7},{5,6},{6,5},{7,4},{8,11},{9,10},{10,... | collective-permute-start | bytes 147464 | tf_op jit(solution)/shard_map/ppermute | solution.py:149
  107.2 1.2 %collective-permute-start.8 = (bf16[192,128]{1,0:T(8,128)(2,1)S(1)}, bf16[192,128]{1,0:T(8,128)(2,1)S(1)}, u32[]{:S(2)}, u32[]{:S(2)}) collective-permute-start(bf16[192,128]{1,0:T(8,128)(2,1)S(1)} %get-tuple-element.15), channel_id=1, source_target_pairs={{0,2},{1,3},{2,0},{3,1},{4,6},{5,7},{6,4},{7,5},{8,10},{9,11},{10,... | collective-permute-start | bytes 147464 | tf_op jit(solution)/shard_map/ppermute | solution.py:149
  108.4 7.7 %shard_map.99 = (f32[256,4096]{1,0:T(8,128)}, f32[1,4096]{1,0:T(1,128)}) custom-call(bf16[16,192,256]{2,1,0:T(8,128)(2,1)S(1)} %all_to_all.17.error_ref, bf16[192,256]{1,0:T(8,128)(2,1)S(1)} %get-tuple-element.19.feats_ref), custom_call_target="tpu_custom_call" | custom-call | tf_op jit(solution)/shard_map/pallas_call | solution.py:30
  116.1 1.8 %shard_map.98 = (f32[64,4096]{1,0:T(8,128)}, f32[1,64]{1,0:T(1,128)}) custom-call(bf16[384,1024]{1,0:T(8,128)(2,1)S(1)} %bitcast.11, bf16[384,1024]{1,0:T(8,128)(2,1)S(1)} %collective-permute-done.3.other_ref, f32[192,128]{1,0:T(8,128)S(1)} %get-tuple-element.14.keep_ref, f32[192,128]{1,0:T(8,128)S(1)} %collective-permute-done.7.near_ref, ...), custom_call_target="tpu_custom_call" | custom-call | tf_op jit(solution)/shard_map/pallas_call | solution.py:30
  (18 shorter events, 0.3 us)
Async XLA Ops:
  0.6 36.4 %copy-start.2 = (bf16[1,3,4096]{2,1,0:T(4,128)(2,1)S(1)}, bf16[1,3,4096]{2,1,0:T(4,128)(2,1)}, u32[]{:S(2)}) copy-start(bf16[1,3,4096]{2,1,0:T(4,128)(2,1)} %param.11) | copy-start | bytes 73732
  0.6 36.4 %copy-start = (bf16[1,256,4096]{2,1,0:T(8,128)(2,1)S(1)}, bf16[1,256,4096]{2,1,0:T(8,128)(2,1)}, u32[]{:S(2)}) copy-start(bf16[1,256,4096]{2,1,0:T(8,128)(2,1)} %param.9) | copy-start | bytes 6291460
  0.7 7.8 %collective-permute-start.1 = (bf16[3,4096]{1,0:T(4,128)(2,1)}, bf16[3,4096]{1,0:T(4,128)(2,1)S(1)}, u32[]{:S(2)}, u32[]{:S(2)}) collective-permute-start(bf16[3,4096]{1,0:T(4,128)(2,1)} %own_ref.1), channel_id=1, source_target_pairs={{0,194},{64,0},{128,64},{192,128},{2,192},{66,2},{130,66},{194,130... | collective-permute-start | bytes 73736 | tf_op jit(solution)/shard_map/ppermute | solution.py:154
  7.1 4.2 %collective-permute-start = (bf16[3,4096]{1,0:T(4,128)(2,1)}, bf16[3,4096]{1,0:T(4,128)(2,1)S(1)}, u32[]{:S(2)}, u32[]{:S(2)}) collective-permute-start(bf16[3,4096]{1,0:T(4,128)(2,1)} %own_ref.1), channel_id=1, source_target_pairs={{0,64},{64,128},{128,192},{192,2},{2,66},{66,130},{130,194},{194,0... | collective-permute-start | bytes 73736 | tf_op jit(solution)/shard_map/ppermute | solution.py:154
  7.1 5.2 %collective-permute-start.2 = (bf16[3,4096]{1,0:T(4,128)(2,1)}, bf16[3,4096]{1,0:T(4,128)(2,1)S(1)}, u32[]{:S(2)}, u32[]{:S(2)}) collective-permute-start(bf16[3,4096]{1,0:T(4,128)(2,1)} %own_ref.1), channel_id=1, source_target_pairs={{0,128},{64,192},{128,2},{192,66},{2,130},{66,194},{130,0},{194,64... | collective-permute-start | bytes 73736 | tf_op jit(solution)/shard_map/ppermute | solution.py:154
  12.3 0.8 copy-start.3
  13.1 24.0 %copy-start.5 = (f32[256]{0:T(256)S(1)}, f32[256]{0:T(256)}, u32[]{:S(2)}) copy-start(f32[256]{0:T(256)} %param.8) | copy-start | bytes 3076
  31.8 5.2 %collective-permute-start.3 = (bf16[384,1024]{1,0:T(8,128)(2,1)S(1)}, bf16[384,1024]{1,0:T(8,128)(2,1)S(1)}, u32[]{:S(2)}, u32[]{:S(2)}) collective-permute-start(bf16[384,1024]{1,0:T(8,128)(2,1)S(1)} %bitcast.9), channel_id=1, source_target_pairs={{0,1},{1,0},{2,3},{3,2},{4,5},{5,4},{6,7},{7,6},{8,9},{9,8},{10,11... | collective-permute-start | bytes 2359304 | tf_op jit(solution)/shard_map/ppermute | solution.py:149
  37.0 1.6 %copy-start.1 = (bf16[4096,256]{1,0:T(8,128)(2,1)S(1)}, bf16[4096,256]{1,0:T(8,128)(2,1)}, u32[]{:S(2)}) copy-start(bf16[4096,256]{1,0:T(8,128)(2,1)} %enc_ref.1) | copy-start | bytes 6291460
  65.0 8.9 %copy-start.4 = (f32[1,4096]{1,0:T(1,128)S(1)}, f32[1,4096]{1,0:T(1,128)}, u32[]{:S(2)}) copy-start(f32[1,4096]{1,0:T(1,128)} %bias_ref.1) | copy-start | bytes 49156
  65.2 5.5 %collective-permute-start.6 = (bf16[192,256]{1,0:T(8,128)(2,1)S(1)}, bf16[192,256]{1,0:T(8,128)(2,1)S(1)}, u32[]{:S(2)}, u32[]{:S(2)}) collective-permute-start(bf16[192,256]{1,0:T(8,128)(2,1)S(1)} %shard_map.95.a_ref), channel_id=1, source_target_pairs={{0,192},{64,128},{128,64},{192,0},{1,193},{65,129},{129,65},{193,1... | collective-permute-start | bytes 294920 | tf_op jit(solution)/shard_map/ppermute | solution.py:149
  65.7 8.1 %collective-permute-start.5 = (bf16[192,256]{1,0:T(8,128)(2,1)S(1)}, bf16[192,256]{1,0:T(8,128)(2,1)S(1)}, u32[]{:S(2)}, u32[]{:S(2)}) collective-permute-start(bf16[192,256]{1,0:T(8,128)(2,1)S(1)} %shard_map.95.a_ref), channel_id=1, source_target_pairs={{0,128},{64,192},{128,0},{192,64},{1,129},{65,193},{129,1},{193,65... | collective-permute-start | bytes 294920 | tf_op jit(solution)/shard_map/ppermute | solution.py:149
  67.0 6.8 %collective-permute-start.4 = (bf16[192,256]{1,0:T(8,128)(2,1)S(1)}, bf16[192,256]{1,0:T(8,128)(2,1)S(1)}, u32[]{:S(2)}, u32[]{:S(2)}) collective-permute-start(bf16[192,256]{1,0:T(8,128)(2,1)S(1)} %shard_map.95.a_ref), channel_id=1, source_target_pairs={{0,64},{64,0},{128,192},{192,128},{1,65},{65,1},{129,193},{193,129... | collective-permute-start | bytes 294920 | tf_op jit(solution)/shard_map/ppermute | solution.py:149
  99.7 16.4 %collective-permute-start.7 = (f32[192,128]{1,0:T(8,128)S(1)}, f32[192,128]{1,0:T(8,128)S(1)}, u32[]{:S(2)}, u32[]{:S(2)}) collective-permute-start(f32[192,128]{1,0:T(8,128)S(1)} %get-tuple-element.14.keep_ref), channel_id=1, source_target_pairs={{0,1},{1,0},{2,3},{3,2},{4,5},{5,4},{6,7},{7,6},{8,9},{9,8},{10,11... | collective-permute-start | bytes 294920 | tf_op jit(solution)/shard_map/ppermute | solution.py:149
  103.1 13.0 %collective-permute-start.9 = (bf16[192,128]{1,0:T(8,128)(2,1)S(1)}, bf16[192,128]{1,0:T(8,128)(2,1)S(1)}, u32[]{:S(2)}, u32[]{:S(2)}) collective-permute-start(bf16[192,128]{1,0:T(8,128)(2,1)S(1)} %get-tuple-element.15), channel_id=1, source_target_pairs={{0,3},{1,2},{2,1},{3,0},{4,7},{5,6},{6,5},{7,4},{8,11},{9,10},{10,... | collective-permute-start | bytes 147464 | tf_op jit(solution)/shard_map/ppermute | solution.py:149
  107.2 8.9 %collective-permute-start.8 = (bf16[192,128]{1,0:T(8,128)(2,1)S(1)}, bf16[192,128]{1,0:T(8,128)(2,1)S(1)}, u32[]{:S(2)}, u32[]{:S(2)}) collective-permute-start(bf16[192,128]{1,0:T(8,128)(2,1)S(1)} %get-tuple-element.15), channel_id=1, source_target_pairs={{0,2},{1,3},{2,0},{3,1},{4,6},{5,7},{6,4},{7,5},{8,10},{9,11},{10,... | collective-permute-start | bytes 147464 | tf_op jit(solution)/shard_map/ppermute | solution.py:149

commit v3 on v2

--- a/solution.py
+++ b/solution.py
@@ -1,7 +1,6 @@
-import functools
-
 import jax
 import jax.numpy as jnp
+import numpy as np
 from jax import lax
 from jax.experimental import pallas as pl
 from jax.experimental.pallas import tpu as pltpu
@@ -11,7 +10,6 @@
 F32 = jnp.float32
 FEAT = ("zl", "y", "x")
 TGT = ("zh", "core")
-PLANE = ("y", "x")
 TN = (((0,), (0,)), ((), ()))
 NT = (((1,), (1,)), ((), ()))
 
@@ -19,6 +17,24 @@
 COUNT = J * ROWS * DEPTH
 CHUNK = D // J
 WIDE = D // 4
+STEP = 4
+
+
+def position(y, x):
+    return 4 * y + x + (y % 2) * (3 - 2 * x)
+
+
+def plane_groups(shape):
+    ids = np.arange(np.prod(shape)).reshape(shape)
+    order = sorted(np.ndindex(shape[1], shape[2]), key=lambda p: position(*p))
+    return [
+        [int(ids[z, y, x, zh, core]) for y, x in order]
+        for z, zh, core in np.ndindex(shape[0], *shape[3:])
+    ]
+
+
+def exchange(x):
+    return lax.all_to_all(x, FEAT + TGT, 0, 0, axis_index_groups=plane_groups((4, 4, 4, 2, 2)), tiled=True)
 
 
 def in_vmem(x):
@@ -33,6 +49,17 @@
         compiler_params=pltpu.CompilerParams(vmem_limit_bytes=40 * 1024 * 1024),
         **kwargs,
     )(*args)
+
+
+def load_kernel(tokens_ref, enc_ref, tokens_out, enc_out, sems):
+    copies = [
+        pltpu.make_async_copy(tokens_ref, tokens_out, sems.at[0]),
+        pltpu.make_async_copy(enc_ref, enc_out, sems.at[1]),
+    ]
+    for copy in copies:
+        copy.start()
+    for copy in copies:
+        copy.wait()
 
 
 def pack_kernel(own_ref, below_ref, above_ref, far_ref, out_ref):
@@ -54,7 +81,7 @@
 
 def forward_kernel(own_ref, other_ref, enc_ref, enc_bias_ref, dec_ref, target_ref, out_ref, pos_ref, feats_ref, acc_ref):
     core, zl = lax.axis_index("core"), lax.axis_index("zl")
-    member = lax.axis_index(PLANE)
+    member = position(lax.axis_index("y"), lax.axis_index("x"))
     sums = []
     for h in range(2):
         mine = pl.multiple_of(core * (D // 2) + h * WIDE, WIDE)
@@ -94,7 +121,7 @@
 
 
 def error_kernel(a_ref, b_ref, c_ref, d_ref, bias_ref, out_ref):
-    member = lax.axis_index(PLANE)
+    member = position(lax.axis_index("y"), lax.axis_index("x"))
     a, b, c, d = [ref[...].astype(F32) for ref in (a_ref, b_ref, c_ref, d_ref)]
     bias = bias_ref[:, pl.ds(pl.multiple_of(member * CHUNK, CHUNK), CHUNK)]
     error = (((a + b) + (c + d)) + bias).astype(BF16)
@@ -114,16 +141,22 @@
     send_ref[...] = jnp.where(zh == 0, total[:, half:], total[:, :half]).astype(BF16)
 
 
-def decoder_kernel(error_ref, feats_ref, grad_ref, bias_ref):
-    grad_ref[...] = lax.dot_general(feats_ref[...], error_ref[0], TN, preferred_element_type=F32)
-    bias_ref[...] = jnp.sum(error_ref[0].astype(F32), axis=0, keepdims=True)
-
-
-def encoder_kernel(own_ref, other_ref, keep_ref, near_ref, far_ref, cross_ref, pos_ref, grad_ref, bias_ref):
+def decoder_kernel(error_ref, feats_ref, grad_ref, bias_ref, done_ref):
+    error = jnp.concatenate([error_ref[j] for j in range(STEP)], axis=1)
+    grad_ref[...] = lax.dot_general(feats_ref[...], error, TN, preferred_element_type=F32)
+    bias_ref[...] = jnp.sum(error.astype(F32), axis=0, keepdims=True)
+    done_ref[...] = jnp.zeros_like(done_ref)
+
+
+def pair_kernel(keep_ref, peer_ref, after_ref, out_ref):
+    out_ref[...] = keep_ref[...] + peer_ref[...].astype(F32)
+
+
+def encoder_kernel(own_ref, other_ref, pair_ref, near_ref, pos_ref, grad_ref, bias_ref):
     core, zh = lax.axis_index("core"), lax.axis_index("zh")
     quarter = FEATS // 4
     half = pl.multiple_of(zh * (FEATS // 2), FEATS // 2)
-    share = (keep_ref[...] + near_ref[...]) + (far_ref[...].astype(F32) + cross_ref[...].astype(F32))
+    share = pair_ref[...] + near_ref[...]
     act = share * (2.0 * pos_ref[:, pl.ds(half, FEATS // 2)])
     act = jnp.where(core == 0, act[:, :quarter], act[:, quarter:])
     bias_ref[...] = jnp.sum(act, axis=0, keepdims=True)
@@ -152,8 +185,15 @@
 def body(tokens, encoder_weight, encoder_bias, decoder_weight, decoder_bias, targets):
     sds = jax.ShapeDtypeStruct
     below, above, far = [lax.ppermute(tokens, ("zl", "zh"), ring(step)) for step in (1, 7, 2)]
+    tokens, encoder_weight = call(
+        load_kernel,
+        (pltpu.VMEM(tokens.shape, BF16), pltpu.VMEM(encoder_weight.shape, BF16)),
+        tokens, encoder_weight,
+        in_specs=[pl.BlockSpec(memory_space=pl.ANY)] * 2,
+        scratch_shapes=[pltpu.SemaphoreType.DMA((2,))],
+    )
     packed = call(pack_kernel, pltpu.VMEM((J, ROWS, 8, WIDE), BF16), tokens, below, above, far)
-    own = lax.all_to_all(packed, PLANE, 0, 0, tiled=True).reshape(2 * COUNT, WIDE)
+    own = exchange(packed).reshape(2 * COUNT, WIDE)
     other = mirror("core", 2, 1)(own)
     dec = decoder_weight[0]
     pieces, positive, feats = call(
@@ -163,36 +203,41 @@
         vmem=(0, 1, 2, 4),
         scratch_shapes=[pltpu.VMEM((2, COUNT, CHUNK), F32)],
     )
-    pieces = lax.all_to_all(pieces, PLANE, 0, 0, tiled=True)
+    pieces = exchange(pieces)
     part = call(sum_kernel, pltpu.VMEM((COUNT, CHUNK), BF16), pieces, vmem=(0,))
     peers = [mirror("zl", DEPTH, key)(part) for key in (1, 2, 3)]
     copies = call(error_kernel, pltpu.VMEM((J, COUNT, CHUNK), BF16), part, *peers, decoder_bias, vmem=(0, 1, 2, 3))
-    errors = lax.all_to_all(copies, PLANE, 0, 0, tiled=True)
+    errors = exchange(copies)
     keep, send = call(
         back_kernel,
         (pltpu.VMEM((COUNT, FEATS // 2), F32), pltpu.VMEM((COUNT, FEATS // 2), BF16)),
         errors, dec,
         vmem=(0, 1),
     )
-    near = mirror(TGT, 4, 1)(keep)
-    back = [mirror(TGT, 4, key)(send) for key in (2, 3)]
-    decoder_grad, bias_grad = call(
+    peer = mirror("zh", 2, 1)(send)
+    decoder_grad, bias_grad, done = call(
         decoder_kernel,
-        (sds((FEATS, D), F32), sds((1, D), F32)),
+        (sds((FEATS, D), F32), sds((1, D), F32), pltpu.VMEM((8, 128), F32)),
         errors, feats,
         vmem=(0, 1),
-        grid=(J,),
+        grid=(J // STEP,),
         in_specs=[
-            pl.BlockSpec((1, COUNT, CHUNK), lambda j: (j, 0, 0)),
+            pl.BlockSpec((STEP, COUNT, CHUNK), lambda j: (j, 0, 0)),
             pl.BlockSpec((COUNT, FEATS), lambda j: (0, 0)),
         ],
-        out_specs=(pl.BlockSpec((FEATS, CHUNK), lambda j: (0, j)), pl.BlockSpec((1, CHUNK), lambda j: (0, j))),
-    )
+        out_specs=(
+            pl.BlockSpec((FEATS, STEP * CHUNK), lambda j: (0, j)),
+            pl.BlockSpec((1, STEP * CHUNK), lambda j: (0, j)),
+            pl.BlockSpec((8, 128), lambda j: (0, 0)),
+        ),
+    )
+    pair = call(pair_kernel, pltpu.VMEM((COUNT, FEATS // 2), F32), keep, peer, done, vmem=(0, 1, 2))
+    near = mirror("core", 2, 1)(pair)
     encoder_grad, encoder_bias_grad = call(
         encoder_kernel,
         (sds((FEATS // 4, D), F32), sds((1, FEATS // 4), F32)),
-        own, other, keep, near, *back, positive,
-        vmem=(0, 1, 2, 3, 4, 5, 6),
+        own, other, pair, near, positive,
+        vmem=(0, 1, 2, 3, 4),
     )
     return encoder_grad.T, encoder_bias_grad[0], decoder_grad[None], bias_grad
 

time: 118 us -> 110 us (0.932); the launches traced: 118 us -> 109 us
  blocking collectives: 68 us -> 62.9 us
  Pallas kernels: 12.5 us -> 8.03 us
  starting transfers between devices: 22.1 us -> 23.6 us
    all_to_all x3, blocking collectives: 68 us -> 62.9 us  [exchange(): lax.all_to_all(x, FEAT + TGT, 0, 0, axis_index_groups=plane_groups((4, 4,...]
    pallas_call x7 -> x9, Pallas kernels: 12.5 us -> 8.03 us  [call(): pl.pallas_call(kernel, out_shape=outs, compiler_params=pltpu.CompilerPara...]
    ppermute x3, waiting for transfers between devices: 5.18 us -> 2.75 us  [body(): lax.ppermute(tokens, ('zl', 'zh'), ring(step))]
    ppermute x7 -> x6, starting transfers between devices: 15.7 us -> 17.1 us  [mirror(): return lambda x: lax.ppermute(x, axes, [(i, i ^ key) for i in range(size)])]
    ppermute x7 -> x6, waiting for transfers between devices: 6.94 us -> 8.21 us  [mirror(): return lambda x: lax.ppermute(x, axes, [(i, i ^ key) for i in range(size)])]
  transfers between devices with their start and end apart: 10 -> 9, of which waited for: 6 -> 6; matrix products, arithmetic and copies ran while one was open for 0% -> 0% of each run, Pallas kernels for 7% -> 3%
where the time goes in v3:
time: 110 us; the launch traced here: 109 us
  blocking collectives  62.9 us (57%)
  starting transfers between devices  23.6 us (21%)
  waiting for transfers between devices  11 us (10%)
  Pallas kernels  8.03 us (7%)
  local copies, waits for them, and re-layouts  2.37 us (2%)
    all_to_all x3, blocking collectives, exchange(): lax.all_to_all(x, FEAT + TGT, 0, 0, axis_index_groups=plane_groups((4, 4,...  62.9 us
    ppermute x6, starting transfers between devices, mirror(): return lambda x: lax.ppermute(x, axes, [(i, i ^ key) for i in range(size)])  17.1 us
    ppermute x6, waiting for transfers between devices, mirror(): return lambda x: lax.ppermute(x, axes, [(i, i ^ key) for i in range(size)])  8.21 us
    pallas_call x9, Pallas kernels, call(): pl.pallas_call(kernel, out_shape=outs, compiler_params=pltpu.CompilerPara...  8.03 us
    ppermute x3, starting transfers between devices, body(): lax.ppermute(tokens, ('zl', 'zh'), ring(step))  6.57 us
    ppermute x3, waiting for transfers between devices, body(): lax.ppermute(tokens, ('zl', 'zh'), ring(step))  2.75 us
    unnamed x12, local copies, waits for them, and re-layouts  2.37 us
  transfers between devices with their start and end apart: 9, of which 6 were waited for; matrix products, arithmetic and copies ran while one was open for 0% of the time, Pallas kernels for 3%

profile of v3, /device:TPU:1, one launch (start us, length us, event | category | flops | bytes accessed | tf_op | source)
XLA Modules:
  0.0 108.6 jit_solution(173059956317249035)
XLA Ops:
  0.6 2.5 %collective-permute-start = (bf16[3,4096]{1,0:T(4,128)(2,1)}, bf16[3,4096]{1,0:T(4,128)(2,1)S(1)}, u32[]{:S(2)}, u32[]{:S(2)}) collective-permute-start(bf16[3,4096]{1,0:T(4,128)(2,1)} %tokens_ref.1), channel_id=1, source_target_pairs={{0,64},{64,128},{128,192},{192,2},{2,66},{66,130},{130,194},{194,0... | collective-permute-start | bytes 73736 | tf_op jit(solution)/shard_map/ppermute | solution.py:187
  3.2 4.0 %collective-permute-start.1 = (bf16[3,4096]{1,0:T(4,128)(2,1)}, bf16[3,4096]{1,0:T(4,128)(2,1)S(1)}, u32[]{:S(2)}, u32[]{:S(2)}) collective-permute-start(bf16[3,4096]{1,0:T(4,128)(2,1)} %tokens_ref.1), channel_id=1, source_target_pairs={{0,194},{64,0},{128,64},{192,128},{2,192},{66,2},{130,66},{194,130... | collective-permute-start | bytes 73736 | tf_op jit(solution)/shard_map/ppermute | solution.py:187
  7.2 1.6 %copy-done.1 = bf16[4096,256]{1,0:T(8,128)(2,1)S(1)} copy-done((bf16[4096,256]{1,0:T(8,128)(2,1)S(1)}, bf16[4096,256]{1,0:T(8,128)(2,1)}, u32[]{:S(2)}) %copy-start.1) | copy-done | bytes 2097176
  8.8 0.8 copy-done.2
  9.6 0.2 shard_map.93
  9.8 2.7 %collective-permute-done.2.far_ref = bf16[3,4096]{1,0:T(4,128)(2,1)S(1)} collective-permute-done((bf16[3,4096]{1,0:T(4,128)(2,1)}, bf16[3,4096]{1,0:T(4,128)(2,1)S(1)}, u32[]{:S(2)}, u32[]{:S(2)}) %collective-permute-start.2) | collective-permute-done | bytes 24608 | tf_op jit(solution)/shard_map/ppermute | solution.py:187
  12.7 17.2 %all_to_all.15 = bf16[16,3,8,1024]{3,2,1,0:T(8,128)(2,1)S(1)} all-to-all(bf16[16,3,8,1024]{3,2,1,0:T(8,128)(2,1)S(1)} %shard_map.94), channel_id=1, replica_groups={{0,4,8,12,28,24,20,16,32,36,40,44,60,56,52,48},{1,5,9,13,29,25,21,17,33..., dimensions={0} | all-to-all | bytes 1572864 | tf_op jit(solution)/shard_map/all_to_all | solution.py:37
  29.9 4.1 %collective-permute-start.3 = (bf16[384,1024]{1,0:T(8,128)(2,1)S(1)}, bf16[384,1024]{1,0:T(8,128)(2,1)S(1)}, u32[]{:S(2)}, u32[]{:S(2)}) collective-permute-start(bf16[384,1024]{1,0:T(8,128)(2,1)S(1)} %bitcast.9), channel_id=1, source_target_pairs={{0,1},{1,0},{2,3},{3,2},{4,5},{5,4},{6,7},{7,6},{8,9},{9,8},{10,11... | collective-permute-start | bytes 2359304 | tf_op jit(solution)/shard_map/ppermute | solution.py:182
  33.9 1.9 %collective-permute-done.3.other_ref = bf16[384,1024]{1,0:T(8,128)(2,1)S(1)} collective-permute-done((bf16[384,1024]{1,0:T(8,128)(2,1)S(1)}, bf16[384,1024]{1,0:T(8,128)(2,1)S(1)}, u32[]{:S(2)}, u32[]{:S(2)}) %collective-permute-start.3) | collective-permute-done | bytes 786464 | tf_op jit(solution)/shard_map/ppermute | solution.py:182
  35.9 1.8 %shard_map.95 = (bf16[16,192,256]{2,1,0:T(8,128)(2,1)S(1)}, f32[192,256]{1,0:T(8,128)S(1)}, bf16[192,256]{1,0:T(8,128)(2,1)S(1)}) custom-call(bf16[384,1024]{1,0:T(8,128)(2,1)S(1)} %bitcast.10, bf16[384,1024]{1,0:T(8,128)(2,1)S(1)} %collective-permute-done.3.other_ref, bf16[4096,256]{1,0:T(8,128)(2,1)S(1)} %get-tuple-element.17.enc_ref, ...), custom_call_target="tpu_custom_call" | custom-call | tf_op jit(solution)/shard_map/pallas_call | solution.py:46
  37.7 24.0 %all_to_all.16.pieces_ref = bf16[16,192,256]{2,1,0:T(8,128)(2,1)S(1)} all-to-all(bf16[16,192,256]{2,1,0:T(8,128)(2,1)S(1)} %get-tuple-element.18), channel_id=1, replica_groups={{0,4,8,12,28,24,20,16,32,36,40,44,60,56,52,48},{1,5,9,13,29,25,21,17,33..., dimensions={0} | all-to-all | bytes 3145728 | tf_op jit(solution)/shard_map/all_to_all | solution.py:37
  61.6 0.2 shard_map.96.a_ref
  62.0 1.5 %collective-permute-start.5 = (bf16[192,256]{1,0:T(8,128)(2,1)S(1)}, bf16[192,256]{1,0:T(8,128)(2,1)S(1)}, u32[]{:S(2)}, u32[]{:S(2)}) collective-permute-start(bf16[192,256]{1,0:T(8,128)(2,1)S(1)} %shard_map.96.a_ref), channel_id=1, source_target_pairs={{0,128},{64,192},{128,0},{192,64},{1,129},{65,193},{129,1},{193,65... | collective-permute-start | bytes 294920 | tf_op jit(solution)/shard_map/ppermute | solution.py:182
  63.5 2.0 %collective-permute-start.6 = (bf16[192,256]{1,0:T(8,128)(2,1)S(1)}, bf16[192,256]{1,0:T(8,128)(2,1)S(1)}, u32[]{:S(2)}, u32[]{:S(2)}) collective-permute-start(bf16[192,256]{1,0:T(8,128)(2,1)S(1)} %shard_map.96.a_ref), channel_id=1, source_target_pairs={{0,192},{64,128},{128,64},{192,0},{1,193},{65,129},{129,65},{193,1... | collective-permute-start | bytes 294920 | tf_op jit(solution)/shard_map/ppermute | solution.py:182
  65.5 1.0 collective-permute-done.5.c_ref
  66.5 2.7 %collective-permute-done.6.d_ref = bf16[192,256]{1,0:T(8,128)(2,1)S(1)} collective-permute-done((bf16[192,256]{1,0:T(8,128)(2,1)S(1)}, bf16[192,256]{1,0:T(8,128)(2,1)S(1)}, u32[]{:S(2)}, u32[]{:S(2)}) %collective-permute-start.6) | collective-permute-done | bytes 98336 | tf_op jit(solution)/shard_map/ppermute | solution.py:182
  69.4 21.7 %all_to_all.17.error_ref = bf16[16,192,256]{2,1,0:T(8,128)(2,1)S(1)} all-to-all(bf16[16,192,256]{2,1,0:T(8,128)(2,1)S(1)} %shard_map.97), channel_id=1, replica_groups={{0,4,8,12,28,24,20,16,32,36,40,44,60,56,52,48},{1,5,9,13,29,25,21,17,33..., dimensions={0} | all-to-all | bytes 3145728 | tf_op jit(solution)/shard_map/all_to_all | solution.py:37
  91.1 0.9 shard_map.98
  92.0 2.4 %collective-permute-start.7 = (bf16[192,128]{1,0:T(8,128)(2,1)S(1)}, bf16[192,128]{1,0:T(8,128)(2,1)S(1)}, u32[]{:S(2)}, u32[]{:S(2)}) collective-permute-start(bf16[192,128]{1,0:T(8,128)(2,1)S(1)} %get-tuple-element.20), channel_id=1, source_target_pairs={{0,2},{2,0},{1,3},{3,1},{4,6},{6,4},{5,7},{7,5},{8,10},{10,8},{9,1... | collective-permute-start | bytes 147464 | tf_op jit(solution)/shard_map/ppermute | solution.py:182
  94.3 2.9 %shard_map.99 = (f32[256,4096]{1,0:T(8,128)}, f32[1,4096]{1,0:T(1,128)}, f32[8,128]{1,0:T(8,128)S(1)}) custom-call(bf16[16,192,256]{2,1,0:T(8,128)(2,1)S(1)} %all_to_all.17.error_ref, bf16[192,256]{1,0:T(8,128)(2,1)S(1)} %get-tuple-element.21.feats_ref), custom_call_target="tpu_custom_call" | custom-call | tf_op jit(solution)/shard_map/pallas_call | solution.py:46
  97.2 1.6 %collective-permute-done.7.peer_ref = bf16[192,128]{1,0:T(8,128)(2,1)S(1)} collective-permute-done((bf16[192,128]{1,0:T(8,128)(2,1)S(1)}, bf16[192,128]{1,0:T(8,128)(2,1)S(1)}, u32[]{:S(2)}, u32[]{:S(2)}) %collective-permute-start.7) | collective-permute-done | bytes 49184 | tf_op jit(solution)/shard_map/ppermute | solution.py:182
  98.9 7.0 %collective-permute-start.8 = (f32[192,128]{1,0:T(8,128)S(1)}, f32[192,128]{1,0:T(8,128)S(1)}, u32[]{:S(2)}, u32[]{:S(2)}) collective-permute-start(f32[192,128]{1,0:T(8,128)S(1)} %shard_map.100.pair_ref), channel_id=1, source_target_pairs={{0,1},{1,0},{2,3},{3,2},{4,5},{5,4},{6,7},{7,6},{8,9},{9,8},{10,11... | collective-permute-start | bytes 294920 | tf_op jit(solution)/shard_map/ppermute | solution.py:182
  105.9 0.9 collective-permute-done.8.near_ref
  106.9 1.7 %shard_map.101 = (f32[64,4096]{1,0:T(8,128)}, f32[1,64]{1,0:T(1,128)}) custom-call(bf16[384,1024]{1,0:T(8,128)(2,1)S(1)} %bitcast.11, bf16[384,1024]{1,0:T(8,128)(2,1)S(1)} %collective-permute-done.3.other_ref, f32[192,128]{1,0:T(8,128)S(1)} %shard_map.100.pair_ref, f32[192,128]{1,0:T(8,128)S(1)} %collective-permute-done.8.near_ref, ...), custom_call_target="tpu_custom_call" | custom-call | tf_op jit(solution)/shard_map/pallas_call | solution.py:46
  (18 shorter events, 0.4 us)
Async XLA Ops:
  0.6 35.2 %copy-start = (bf16[1,256,4096]{2,1,0:T(8,128)(2,1)S(1)}, bf16[1,256,4096]{2,1,0:T(8,128)(2,1)}, u32[]{:S(2)}) copy-start(bf16[1,256,4096]{2,1,0:T(8,128)(2,1)} %param.9) | copy-start | bytes 6291460
  0.6 9.1 %collective-permute-start = (bf16[3,4096]{1,0:T(4,128)(2,1)}, bf16[3,4096]{1,0:T(4,128)(2,1)S(1)}, u32[]{:S(2)}, u32[]{:S(2)}) collective-permute-start(bf16[3,4096]{1,0:T(4,128)(2,1)} %tokens_ref.1), channel_id=1, source_target_pairs={{0,64},{64,128},{128,192},{192,2},{2,66},{66,130},{130,194},{194,0... | collective-permute-start | bytes 73736 | tf_op jit(solution)/shard_map/ppermute | solution.py:187
  3.2 6.6 %collective-permute-start.1 = (bf16[3,4096]{1,0:T(4,128)(2,1)}, bf16[3,4096]{1,0:T(4,128)(2,1)S(1)}, u32[]{:S(2)}, u32[]{:S(2)}) collective-permute-start(bf16[3,4096]{1,0:T(4,128)(2,1)} %tokens_ref.1), channel_id=1, source_target_pairs={{0,194},{64,0},{128,64},{192,128},{2,192},{66,2},{130,66},{194,130... | collective-permute-start | bytes 73736 | tf_op jit(solution)/shard_map/ppermute | solution.py:187
  7.2 5.3 %collective-permute-start.2 = (bf16[3,4096]{1,0:T(4,128)(2,1)}, bf16[3,4096]{1,0:T(4,128)(2,1)S(1)}, u32[]{:S(2)}, u32[]{:S(2)}) collective-permute-start(bf16[3,4096]{1,0:T(4,128)(2,1)} %tokens_ref.1), channel_id=1, source_target_pairs={{0,128},{64,192},{128,2},{192,66},{2,130},{66,194},{130,0},{194,64... | collective-permute-start | bytes 73736 | tf_op jit(solution)/shard_map/ppermute | solution.py:187
  7.2 1.6 %copy-start.1 = (bf16[4096,256]{1,0:T(8,128)(2,1)S(1)}, bf16[4096,256]{1,0:T(8,128)(2,1)}, u32[]{:S(2)}) copy-start(bf16[4096,256]{1,0:T(8,128)(2,1)} %enc_ref.1) | copy-start | bytes 6291460
  8.8 0.8 copy-start.2
  9.6 26.3 %copy-start.3 = (bf16[1,3,4096]{2,1,0:T(4,128)(2,1)S(1)}, bf16[1,3,4096]{2,1,0:T(4,128)(2,1)}, u32[]{:S(2)}) copy-start(bf16[1,3,4096]{2,1,0:T(4,128)(2,1)} %param.11) | copy-start | bytes 73732
  9.6 26.3 %copy-start.5 = (f32[256]{0:T(256)S(1)}, f32[256]{0:T(256)}, u32[]{:S(2)}) copy-start(f32[256]{0:T(256)} %param.8) | copy-start | bytes 3076
  29.9 6.0 %collective-permute-start.3 = (bf16[384,1024]{1,0:T(8,128)(2,1)S(1)}, bf16[384,1024]{1,0:T(8,128)(2,1)S(1)}, u32[]{:S(2)}, u32[]{:S(2)}) collective-permute-start(bf16[384,1024]{1,0:T(8,128)(2,1)S(1)} %bitcast.9), channel_id=1, source_target_pairs={{0,1},{1,0},{2,3},{3,2},{4,5},{5,4},{6,7},{7,6},{8,9},{9,8},{10,11... | collective-permute-start | bytes 2359304 | tf_op jit(solution)/shard_map/ppermute | solution.py:182
  37.7 31.5 %copy-start.4 = (f32[1,4096]{1,0:T(1,128)S(1)}, f32[1,4096]{1,0:T(1,128)}, u32[]{:S(2)}) copy-start(f32[1,4096]{1,0:T(1,128)} %bias_ref.1) | copy-start | bytes 49156
  61.9 3.6 %collective-permute-start.4 = (bf16[192,256]{1,0:T(8,128)(2,1)S(1)}, bf16[192,256]{1,0:T(8,128)(2,1)S(1)}, u32[]{:S(2)}, u32[]{:S(2)}) collective-permute-start(bf16[192,256]{1,0:T(8,128)(2,1)S(1)} %shard_map.96.a_ref), channel_id=1, source_target_pairs={{0,64},{64,0},{128,192},{192,128},{1,65},{65,1},{129,193},{193,129... | collective-permute-start | bytes 294920 | tf_op jit(solution)/shard_map/ppermute | solution.py:182
  62.0 4.5 %collective-permute-start.5 = (bf16[192,256]{1,0:T(8,128)(2,1)S(1)}, bf16[192,256]{1,0:T(8,128)(2,1)S(1)}, u32[]{:S(2)}, u32[]{:S(2)}) collective-permute-start(bf16[192,256]{1,0:T(8,128)(2,1)S(1)} %shard_map.96.a_ref), channel_id=1, source_target_pairs={{0,128},{64,192},{128,0},{192,64},{1,129},{65,193},{129,1},{193,65... | collective-permute-start | bytes 294920 | tf_op jit(solution)/shard_map/ppermute | solution.py:182
  63.5 5.7 %collective-permute-start.6 = (bf16[192,256]{1,0:T(8,128)(2,1)S(1)}, bf16[192,256]{1,0:T(8,128)(2,1)S(1)}, u32[]{:S(2)}, u32[]{:S(2)}) collective-permute-start(bf16[192,256]{1,0:T(8,128)(2,1)S(1)} %shard_map.96.a_ref), channel_id=1, source_target_pairs={{0,192},{64,128},{128,64},{192,0},{1,193},{65,129},{129,65},{193,1... | collective-permute-start | bytes 294920 | tf_op jit(solution)/shard_map/ppermute | solution.py:182
  92.0 6.9 %collective-permute-start.7 = (bf16[192,128]{1,0:T(8,128)(2,1)S(1)}, bf16[192,128]{1,0:T(8,128)(2,1)S(1)}, u32[]{:S(2)}, u32[]{:S(2)}) collective-permute-start(bf16[192,128]{1,0:T(8,128)(2,1)S(1)} %get-tuple-element.20), channel_id=1, source_target_pairs={{0,2},{2,0},{1,3},{3,1},{4,6},{6,4},{5,7},{7,5},{8,10},{10,8},{9,1... | collective-permute-start | bytes 147464 | tf_op jit(solution)/shard_map/ppermute | solution.py:182
  98.9 8.0 %collective-permute-start.8 = (f32[192,128]{1,0:T(8,128)S(1)}, f32[192,128]{1,0:T(8,128)S(1)}, u32[]{:S(2)}, u32[]{:S(2)}) collective-permute-start(f32[192,128]{1,0:T(8,128)S(1)} %shard_map.100.pair_ref), channel_id=1, source_target_pairs={{0,1},{1,0},{2,3},{3,2},{4,5},{5,4},{6,7},{7,6},{8,9},{9,8},{10,11... | collective-permute-start | bytes 294920 | tf_op jit(solution)/shard_map/ppermute | solution.py:182

commit v4 on v3

v4 whole, which is shorter than its diff:
```python
import jax
import jax.numpy as jnp
import numpy as np
from jax import lax
from jax.experimental import pallas as pl
from jax.experimental.pallas import tpu as pltpu
from jax.sharding import Mesh, PartitionSpec as P

BF16 = jnp.bfloat16
F32 = jnp.float32
FEAT = ("zl", "y", "x")
TGT = ("zh", "core")
TN = (((0,), (0,)), ((), ()))
NT = (((1,), (1,)), ((), ()))
KEYS = (1, 2, 3)

J, ROWS, DEPTH, D, FEATS = 16, 3, 4, 4096, 256
COUNT = J * ROWS * DEPTH
WIDE, PIECE = D // 4, D // 16
HALF = D // 2


def call(kernel, outs, *args, vmem=(), **kwargs):
    args = [pltpu.with_memory_space_constraint(a, pltpu.VMEM) if i in vmem else a for i, a in enumerate(args)]
    return pl.pallas_call(
        kernel,
        out_shape=outs,
        compiler_params=pltpu.CompilerParams(vmem_limit_bytes=40 * 1024 * 1024),
        **kwargs,
    )(*args)


def coordinates():
    core, y, x = lax.axis_index("core"), lax.axis_index("y"), lax.axis_index("x")
    return jnp.where(core == 0, x, y), jnp.where(core == 0, y, x)


def columns(at, width):
    return pl.ds(pl.multiple_of(at * width, width), width)


def load_kernel(tokens_ref, enc_ref, tokens_out, enc_out, sems):
    copies = [
        pltpu.make_async_copy(tokens_ref, tokens_out, sems.at[0]),
        pltpu.make_async_copy(enc_ref, enc_out, sems.at[1]),
    ]
    for copy in copies:
        copy.start()
    for copy in copies:
        copy.wait()


def pack_kernel(own_ref, below_ref, above_ref, far_ref, out_ref):
    zl = lax.axis_index("zl")
    sub = lax.broadcasted_iota(jnp.int32, (8, WIDE), 0)
    sources = [(own_ref, 0), (below_ref, 3), (above_ref, 1), (far_ref, 2)]
    half = columns(lax.axis_index("core"), HALF)
    blocks = [(ref[:, half].astype(F32), (zl + step) % 4) for ref, step in sources]
    for i in range(ROWS):
        tile = jnp.zeros((8, WIDE), F32)
        for block, depth in blocks:
            for h in range(2):
                row = block[i : i + 1, h * WIDE : (h + 1) * WIDE]
                tile = jnp.where(sub == depth + 4 * h, row, tile)
        tile = tile.astype(BF16)
        for j in range(J):
            out_ref[j, 8 * i : 8 * i + 8, :] = tile


def forward_kernel(
    own_ref, other_ref, enc_ref, enc_bias_ref, dec_ref, target_ref,
    keep_ref, send1_ref, send2_ref, send3_ref, pos_ref, feats_ref, acc_ref,
):
    core, zl = lax.axis_index("core"), lax.axis_index("zl")
    member = lax.axis_index("y") * 4 + lax.axis_index("x")
    a, _ = coordinates()
    sums = []
    for h in range(2):
        sums.append(
            jnp.dot(own_ref[...], enc_ref[columns(2 * core + h, WIDE), :], preferred_element_type=F32)
            + jnp.dot(other_ref[...], enc_ref[columns(2 - 2 * core + h, WIDE), :], preferred_element_type=F32)
        )
    low, high = [s.reshape(COUNT // 8, 2, 8, FEATS) for s in sums]
    sub = lax.broadcasted_iota(jnp.int32, (COUNT // 8, 8, FEATS), 1)
    both = []
    for g in range(2):
        part = jnp.where(sub < 4, low[:, g], high[:, g])
        both.append(part + pltpu.roll(part, 4, 1))
    pre = jnp.where(sub < 4, both[0], both[1]).reshape(COUNT, FEATS) + enc_bias_ref[...]
    positive = jnp.maximum(pre, 0.0)
    pos_ref[...] = positive
    feats = (positive * positive).astype(BF16)
    feats_ref[...] = feats
    lane_sub = lax.broadcasted_iota(jnp.int32, (8, WIDE), 0)
    for key in (2, 1, 3, 0):
        out_ref = (keep_ref, send1_ref, send2_ref, send3_ref)[key]
        place = columns(a ^ key, WIDE)
        acc = keep_ref if key == 0 else acc_ref.at[key % 2]
        acc[...] = jnp.dot(feats, dec_ref[:, place], preferred_element_type=F32)
        values = target_ref[:, place].astype(F32)
        for i in range(ROWS):
            group = ROWS * member + i
            tile = pl.ds(pl.multiple_of(8 * (group // 2), 8), 8)
            row = 4 * (group % 2) + zl
            acc[tile, :] = acc[tile, :] - jnp.where(lane_sub == row, values[i : i + 1], 0.0)
        if key:
            out_ref[...] = acc[...].astype(BF16)


def middle_kernel(keep_ref, r1_ref, r2_ref, r3_ref, out_ref, send1_ref, send2_ref, send3_ref):
    _, b = coordinates()
    for key, ref in enumerate((out_ref, send1_ref, send2_ref, send3_ref)):
        place = columns(b ^ key, PIECE)
        total = (keep_ref[:, place] + r1_ref[:, place].astype(F32)) + (
            r2_ref[:, place].astype(F32) + r3_ref[:, place].astype(F32)
        )
        ref[...] = total.astype(ref.dtype)


def sum_kernel(keep_ref, r1_ref, r2_ref, r3_ref, out_ref):
    r1, r2, r3 = [ref[...].astype(F32) for ref in (r1_ref, r2_ref, r3_ref)]
    out_ref[...] = ((keep_ref[...] + r1) + (r2 + r3)).astype(BF16)


def error_kernel(own_ref, r1_ref, r2_ref, r3_ref, bias_ref, out_ref):
    a, b = coordinates()
    own, r1, r2, r3 = [ref[...].astype(F32) for ref in (own_ref, r1_ref, r2_ref, r3_ref)]
    bias = bias_ref[:, columns(4 * a + b, PIECE)]
    error = (((own + r1) + (r2 + r3)) + bias).astype(BF16)
    for j in range(J):
        out_ref[j] = error


def back_kernel(error_ref, dec_ref, keep_ref, send_ref):
    zh = lax.axis_index("zh")
    total = jnp.zeros((COUNT, FEATS), F32)
    for j in range(J):
        total = total + lax.dot_general(
            error_ref[j], dec_ref[:, j * PIECE : (j + 1) * PIECE], NT, preferred_element_type=F32
        )
    half = FEATS // 2
    keep_ref[...] = jnp.where(zh == 0, total[:, :half], total[:, half:])
    send_ref[...] = jnp.where(zh == 0, total[:, half:], total[:, :half]).astype(BF16)


def decoder_kernel(error_ref, feats_ref, grad_ref, bias_ref, done_ref, part_ref, sems):
    feats = feats_ref[...]
    copies = []
    for k in range(4):
        error = jnp.concatenate([error_ref[4 * k + j] for j in range(4)], axis=1)
        place = slice(k * WIDE, (k + 1) * WIDE)
        part_ref[k] = lax.dot_general(feats, error, TN, preferred_element_type=F32)
        copy = pltpu.make_async_copy(part_ref.at[k], grad_ref.at[:, place], sems.at[k])
        copy.start()
        copies.append(copy)
        bias_ref[:, place] = jnp.sum(error.astype(F32), axis=0, keepdims=True)
    done_ref[...] = jnp.zeros_like(done_ref)
    for copy in copies:
        copy.wait()


def pair_kernel(keep_ref, peer_ref, after_ref, out_ref):
    out_ref[...] = keep_ref[...] + peer_ref[...].astype(F32)


def encoder_kernel(own_ref, other_ref, pair_ref, near_ref, pos_ref, grad_ref, bias_ref):
    core, zh = lax.axis_index("core"), lax.axis_index("zh")
    quarter = FEATS // 4
    share = pair_ref[...] + near_ref[...]
    act = share * (2.0 * pos_ref[:, columns(zh, FEATS // 2)])
    act = jnp.where(core == 0, act[:, :quarter], act[:, quarter:])
    bias_ref[...] = jnp.sum(act, axis=0, keepdims=True)
    tiles = act.astype(BF16).astype(F32).reshape(COUNT // 8, 8, quarter)
    turned = pltpu.roll(tiles, 4, 1)
    sub = lax.broadcasted_iota(jnp.int32, tiles.shape, 1)
    zero = jnp.zeros_like(tiles)
    low = jnp.stack([jnp.where(sub < 4, tiles, zero), jnp.where(sub < 4, turned, zero)], axis=1)
    high = jnp.stack([jnp.where(sub < 4, zero, turned), jnp.where(sub < 4, zero, tiles)], axis=1)
    for h, side in enumerate((low, high)):
        side = side.reshape(2 * COUNT, quarter).astype(BF16)
        for ref, owner in ((own_ref, core), (other_ref, 1 - core)):
            grad_ref[:, columns(2 * owner + h, WIDE)] = lax.dot_general(
                side, ref[...], TN, preferred_element_type=F32
            )


def ring(step):
    index = lambda z: (z % 4) * 2 + z // 4
    return [(index(z), index((z + step) % 8)) for z in range(8)]


def mirror(x, axes, size, key):
    return lax.ppermute(x, axes, [(i, i ^ key) for i in range(size)])


def plane_swap(x, wide, key):
    pairs = []
    for i in range(32):
        y, x_at, core = i // 8, i // 2 % 4, i % 2
        along_x = wide == (core == 0)
        there = (y, x_at ^ key) if along_x else (y ^ key, x_at)
        pairs.append((i, 8 * there[0] + 2 * there[1] + core))
    return lax.ppermute(x, ("y", "x", "core"), pairs)


def plane_groups():
    ids = np.arange(256).reshape(4, 4, 4, 2, 2)
    return [
        [int(ids[(z, c % 4, c // 4) if core == 0 else (z, c // 4, c % 4)][zh, core]) for c in range(J)]
        for z, zh, core in np.ndindex(4, 2, 2)
    ]


def body(tokens, encoder_weight, encoder_bias, decoder_weight, decoder_bias, targets):
    sds, vmem = jax.ShapeDtypeStruct, pltpu.VMEM
    dec = decoder_weight[0]

    near_rows = [lax.ppermute(tokens, ("zl", "zh"), ring(step)) for step in (1, 7, 2)]
    tokens, encoder_weight = call(
        load_kernel,
        (vmem(tokens.shape, BF16), vmem(encoder_weight.shape, BF16)),
        tokens, encoder_weight,
        in_specs=[pl.BlockSpec(memory_space=pl.ANY)] * 2,
        scratch_shapes=[pltpu.SemaphoreType.DMA((2,))],
    )
    packed = call(pack_kernel, vmem((J, 8 * ROWS, WIDE), BF16), tokens, *near_rows, vmem=range(4))
    own = lax.all_to_all(packed, ("y", "x"), 0, 0, tiled=True)
    own = own.reshape(2 * COUNT, WIDE)
    other = mirror(own, "core", 2, 1)

    wide, piece = (COUNT, WIDE), (COUNT, PIECE)
    keep, *sends, positive, feats = call(
        forward_kernel,
        (vmem(wide, F32),) + (vmem(wide, BF16),) * 3 + (vmem((COUNT, FEATS), F32), vmem((COUNT, FEATS), BF16)),
        own, other, encoder_weight, encoder_bias[None], dec, targets[0],
        vmem=(0, 1, 2, 4),
        scratch_shapes=[vmem((2,) + wide, F32)],
    )
    moved = [plane_swap(sends[key - 1], True, key) for key in KEYS]
    keep, *sends = call(middle_kernel, (vmem(piece, F32),) + (vmem(piece, BF16),) * 3, keep, *moved, vmem=range(4))
    moved = [plane_swap(sends[key - 1], False, key) for key in KEYS]
    part = call(sum_kernel, vmem(piece, BF16), keep, *moved, vmem=range(4))
    moved = [mirror(part, "zl", DEPTH, key) for key in KEYS]
    copies = call(error_kernel, vmem((J,) + piece, BF16), part, *moved, decoder_bias, vmem=range(4))
    errors = lax.all_to_all(copies, FEAT + TGT, 0, 0, axis_index_groups=plane_groups(), tiled=True)

    half = (COUNT, FEATS // 2)
    keep, send = call(back_kernel, (vmem(half, F32), vmem(half, BF16)), errors, dec, vmem=range(2))
    peer = mirror(send, "zh", 2, 1)
    decoder_grad, bias_grad, done = call(
        decoder_kernel,
        (sds((FEATS, D), F32), sds((1, D), F32), vmem((8, 128), F32)),
        errors, feats,
        vmem=range(2),
        out_specs=(
            pl.BlockSpec(memory_space=pl.ANY),
            pl.BlockSpec(memory_space=pltpu.VMEM),
            pl.BlockSpec(memory_space=pltpu.VMEM),
        ),
        scratch_shapes=[vmem((4, FEATS, WIDE), F32), pltpu.SemaphoreType.DMA((4,))],
    )
    pair = call(pair_kernel, vmem(half, F32), keep, peer, done, vmem=range(3))
    near = mirror(pair, "core", 2, 1)
    encoder_grad, encoder_bias_grad = call(
        encoder_kernel,
        (sds((FEATS // 4, D), F32), sds((1, FEATS // 4), F32)),
        own, other, pair, near, positive,
        vmem=range(5),
    )
    return encoder_grad.T, encoder_bias_grad[0], decoder_grad[None], bias_grad


def solution(mesh):
    split = Mesh(mesh.devices.reshape(4, 4, 4, 2, 2), FEAT + TGT)
    return jax.shard_map(
        body,
        mesh=split,
        in_specs=(
            P(FEAT, None),
            P(None, FEAT),
            P(FEAT),
            P(TGT, FEAT, None),
            P(TGT, None),
            P(TGT, FEAT, None),
        ),
        out_specs=(
            P(None, FEAT + TGT),
            P(FEAT + TGT),
            P(TGT, FEAT, None),
            P(TGT, None),
        ),
        check_vma=False,
    )
```

time: 110 us -> 108 us (0.982)
  blocking collectives: 62.9 us -> 41.4 us
  waiting for transfers between devices: 11 us -> 22.3 us
  starting transfers between devices: 23.6 us -> 32.2 us
    all_to_all x3 -> x2, blocking collectives: 62.9 us -> 41.4 us  [the longest x1 22.9 us: body(): lax.all_to_all(copies, FEAT + TGT, 0, 0, axis_index_groups=plane_groups()...]
    ppermute x6 -> x12, waiting for transfers between devices: 8.21 us -> 19.5 us  [the longest x6 13.3 us: plane_swap(): return lax.ppermute(x, ('y', 'x', 'core'), pairs)]
    ppermute x6 -> x12, starting transfers between devices: 17.1 us -> 25.6 us  [the longest x6 17.8 us: mirror(): return lax.ppermute(x, axes, [(i, i ^ key) for i in range(size)])]
    pallas_call x9 -> x10, Pallas kernels: 8.03 us -> 7.9 us  [call(): pl.pallas_call(kernel, out_shape=outs, compiler_params=pltpu.CompilerPara...]
  transfers between devices with their start and end apart: 9 -> 15, of which waited for: 6 -> 10; matrix products, arithmetic and copies ran while one was open for 0% -> 0% of each run, Pallas kernels for 3% -> 3%
where the time goes in v4:
time: 108 us; the launch traced here: 107 us
  blocking collectives  41.4 us (38%)
  starting transfers between devices  32.2 us (30%)
  waiting for transfers between devices  22.3 us (21%)
  Pallas kernels  7.9 us (7%)
  local copies, waits for them, and re-layouts  2.37 us (2%)
    all_to_all x1, blocking collectives, body(): lax.all_to_all(copies, FEAT + TGT, 0, 0, axis_index_groups=plane_groups()...  22.9 us
    all_to_all x1, blocking collectives, body(): own = lax.all_to_all(packed, ('y', 'x'), 0, 0, tiled=True)  18.5 us
    ppermute x6, starting transfers between devices, mirror(): return lax.ppermute(x, axes, [(i, i ^ key) for i in range(size)])  17.8 us
    ppermute x6, waiting for transfers between devices, plane_swap(): return lax.ppermute(x, ('y', 'x', 'core'), pairs)  13.3 us
    pallas_call x10, Pallas kernels, call(): pl.pallas_call(kernel, out_shape=outs, compiler_params=pltpu.CompilerPara...  7.9 us
    ppermute x6, starting transfers between devices, plane_swap(): return lax.ppermute(x, ('y', 'x', 'core'), pairs)  7.88 us
    ppermute x3, starting transfers between devices, body(): lax.ppermute(tokens, ('zl', 'zh'), ring(step))  6.57 us
    ppermute x6, waiting for transfers between devices, mirror(): return lax.ppermute(x, axes, [(i, i ^ key) for i in range(size)])  6.26 us
  transfers between devices with their start and end apart: 15, of which 10 were waited for; matrix products, arithmetic and copies ran while one was open for 0% of the time, Pallas kernels for 3%

profile of v4, /device:TPU:1, one launch (start us, length us, event | category | flops | bytes accessed | tf_op | source)
XLA Modules:
  0.0 106.9 jit_solution(16239534998952488043)
XLA Ops:
  0.6 2.5 %collective-permute-start = (bf16[3,4096]{1,0:T(4,128)(2,1)}, bf16[3,4096]{1,0:T(4,128)(2,1)S(1)}, u32[]{:S(2)}, u32[]{:S(2)}) collective-permute-start(bf16[3,4096]{1,0:T(4,128)(2,1)} %tokens_ref.1), channel_id=1, source_target_pairs={{0,64},{64,128},{128,192},{192,2},{2,66},{66,130},{130,194},{194,0... | collective-permute-start | bytes 73736 | tf_op jit(solution)/shard_map/ppermute | solution.py:218
  3.2 4.0 %collective-permute-start.1 = (bf16[3,4096]{1,0:T(4,128)(2,1)}, bf16[3,4096]{1,0:T(4,128)(2,1)S(1)}, u32[]{:S(2)}, u32[]{:S(2)}) collective-permute-start(bf16[3,4096]{1,0:T(4,128)(2,1)} %tokens_ref.1), channel_id=1, source_target_pairs={{0,194},{64,0},{128,64},{192,128},{2,192},{66,2},{130,66},{194,130... | collective-permute-start | bytes 73736 | tf_op jit(solution)/shard_map/ppermute | solution.py:218
  7.2 1.6 %copy-done.1 = bf16[4096,256]{1,0:T(8,128)(2,1)S(1)} copy-done((bf16[4096,256]{1,0:T(8,128)(2,1)S(1)}, bf16[4096,256]{1,0:T(8,128)(2,1)}, u32[]{:S(2)}) %copy-start.1) | copy-done | bytes 2097176
  9.8 2.7 %collective-permute-done.2.far_ref = bf16[3,4096]{1,0:T(4,128)(2,1)S(1)} collective-permute-done((bf16[3,4096]{1,0:T(4,128)(2,1)}, bf16[3,4096]{1,0:T(4,128)(2,1)S(1)}, u32[]{:S(2)}, u32[]{:S(2)}) %collective-permute-start.2) | collective-permute-done | bytes 24608 | tf_op jit(solution)/shard_map/ppermute | solution.py:218
  12.7 18.5 %all_to_all.10 = bf16[16,24,1024]{2,1,0:T(8,128)(2,1)S(1)} all-to-all(bf16[16,24,1024]{2,1,0:T(8,128)(2,1)S(1)} %shard_map.94), channel_id=1, replica_groups=mesh['zl'=4,'y'=4,'x'=4,'zh'=2,'core'=2] {'y','x'}, dimensions={0} | all-to-all | bytes 1572864 | tf_op jit(solution)/shard_map/all_to_all | solution.py:227
  31.2 3.4 %collective-permute-start.3 = (bf16[384,1024]{1,0:T(8,128)(2,1)S(1)}, bf16[384,1024]{1,0:T(8,128)(2,1)S(1)}, u32[]{:S(2)}, u32[]{:S(2)}) collective-permute-start(bf16[384,1024]{1,0:T(8,128)(2,1)S(1)} %bitcast.9), channel_id=1, source_target_pairs={{0,1},{1,0},{2,3},{3,2},{4,5},{5,4},{6,7},{7,6},{8,9},{9,8},{10,11... | collective-permute-start | bytes 2359304 | tf_op jit(solution)/shard_map/ppermute | solution.py:193
  34.6 1.9 %collective-permute-done.3.other_ref = bf16[384,1024]{1,0:T(8,128)(2,1)S(1)} collective-permute-done((bf16[384,1024]{1,0:T(8,128)(2,1)S(1)}, bf16[384,1024]{1,0:T(8,128)(2,1)S(1)}, u32[]{:S(2)}, u32[]{:S(2)}) %collective-permute-start.3) | collective-permute-done | bytes 786464 | tf_op jit(solution)/shard_map/ppermute | solution.py:193
  36.5 1.6 %shard_map.95 = (f32[192,1024]{1,0:T(8,128)S(1)}, bf16[192,1024]{1,0:T(8,128)(2,1)S(1)}, bf16[192,1024]{1,0:T(8,128)(2,1)S(1)}, bf16[192,1024]{1,0:T(8,128)(2,1)...) custom-call(bf16[384,1024]{1,0:T(8,128)(2,1)S(1)} %bitcast.10, ...), custom_call_target="tpu_custom_call" | custom-call | tf_op jit(solution)/shard_map/pallas_call | solution.py:25
  38.2 1.7 %collective-permute-start.5 = (bf16[192,1024]{1,0:T(8,128)(2,1)S(1)}, bf16[192,1024]{1,0:T(8,128)(2,1)S(1)}, u32[]{:S(2)}, u32[]{:S(2)}) collective-permute-start(bf16[192,1024]{1,0:T(8,128)(2,1)S(1)} %get-tuple-element.27), channel_id=1, source_target_pairs={{0,8},{1,33},{4,12},{5,37},{8,0},{9,41},{12,4},{13,45},{16,24},{17... | collective-permute-start | bytes 1179656 | tf_op jit(solution)/shard_map/ppermute | solution.py:203
  39.9 2.1 %collective-permute-start.6 = (bf16[192,1024]{1,0:T(8,128)(2,1)S(1)}, bf16[192,1024]{1,0:T(8,128)(2,1)S(1)}, u32[]{:S(2)}, u32[]{:S(2)}) collective-permute-start(bf16[192,1024]{1,0:T(8,128)(2,1)S(1)} %get-tuple-element.28), channel_id=1, source_target_pairs={{0,12},{1,49},{4,8},{5,53},{8,4},{9,57},{12,0},{13,61},{16,28},{17... | collective-permute-start | bytes 1179656 | tf_op jit(solution)/shard_map/ppermute | solution.py:203
  42.0 3.1 %collective-permute-done.4.r1_ref = bf16[192,1024]{1,0:T(8,128)(2,1)S(1)} collective-permute-done((bf16[192,1024]{1,0:T(8,128)(2,1)S(1)}, bf16[192,1024]{1,0:T(8,128)(2,1)S(1)}, u32[]{:S(2)}, u32[]{:S(2)}) %collective-permute-start.4) | collective-permute-done | bytes 393248 | tf_op jit(solution)/shard_map/ppermute | solution.py:203
  45.1 4.6 %collective-permute-done.5.r2_ref = bf16[192,1024]{1,0:T(8,128)(2,1)S(1)} collective-permute-done((bf16[192,1024]{1,0:T(8,128)(2,1)S(1)}, bf16[192,1024]{1,0:T(8,128)(2,1)S(1)}, u32[]{:S(2)}, u32[]{:S(2)}) %collective-permute-start.5) | collective-permute-done | bytes 393248 | tf_op jit(solution)/shard_map/ppermute | solution.py:203
  49.6 2.6 %collective-permute-done.6.r3_ref = bf16[192,1024]{1,0:T(8,128)(2,1)S(1)} collective-permute-done((bf16[192,1024]{1,0:T(8,128)(2,1)S(1)}, bf16[192,1024]{1,0:T(8,128)(2,1)S(1)}, u32[]{:S(2)}, u32[]{:S(2)}) %collective-permute-start.6) | collective-permute-done | bytes 393248 | tf_op jit(solution)/shard_map/ppermute | solution.py:203
  52.6 1.9 %collective-permute-start.8 = (bf16[192,256]{1,0:T(8,128)(2,1)S(1)}, bf16[192,256]{1,0:T(8,128)(2,1)S(1)}, u32[]{:S(2)}, u32[]{:S(2)}) collective-permute-start(bf16[192,256]{1,0:T(8,128)(2,1)S(1)} %get-tuple-element.31), channel_id=1, source_target_pairs={{0,32},{1,9},{4,36},{5,13},{8,40},{9,1},{12,44},{13,5},{16,48},{17... | collective-permute-start | bytes 294920 | tf_op jit(solution)/shard_map/ppermute | solution.py:203
  54.5 2.0 %collective-permute-start.9 = (bf16[192,256]{1,0:T(8,128)(2,1)S(1)}, bf16[192,256]{1,0:T(8,128)(2,1)S(1)}, u32[]{:S(2)}, u32[]{:S(2)}) collective-permute-start(bf16[192,256]{1,0:T(8,128)(2,1)S(1)} %get-tuple-element.32), channel_id=1, source_target_pairs={{0,48},{1,13},{4,52},{5,9},{8,56},{9,5},{12,60},{13,1},{16,32},{17... | collective-permute-start | bytes 294920 | tf_op jit(solution)/shard_map/ppermute | solution.py:203
  57.6 1.8 %collective-permute-done.9.r3_ref = bf16[192,256]{1,0:T(8,128)(2,1)S(1)} collective-permute-done((bf16[192,256]{1,0:T(8,128)(2,1)S(1)}, bf16[192,256]{1,0:T(8,128)(2,1)S(1)}, u32[]{:S(2)}, u32[]{:S(2)}) %collective-permute-start.9) | collective-permute-done | bytes 98336 | tf_op jit(solution)/shard_map/ppermute | solution.py:203
  59.6 1.6 %collective-permute-start.11 = (bf16[192,256]{1,0:T(8,128)(2,1)S(1)}, bf16[192,256]{1,0:T(8,128)(2,1)S(1)}, u32[]{:S(2)}, u32[]{:S(2)}) collective-permute-start(bf16[192,256]{1,0:T(8,128)(2,1)S(1)} %shard_map.97.own_ref), channel_id=1, source_target_pairs={{0,128},{64,192},{128,0},{192,64},{1,129},{65,193},{129,1},{193,65... | collective-permute-start | bytes 294920 | tf_op jit(solution)/shard_map/ppermute | solution.py:193
  61.1 2.0 %collective-permute-start.12 = (bf16[192,256]{1,0:T(8,128)(2,1)S(1)}, bf16[192,256]{1,0:T(8,128)(2,1)S(1)}, u32[]{:S(2)}, u32[]{:S(2)}) collective-permute-start(bf16[192,256]{1,0:T(8,128)(2,1)S(1)} %shard_map.97.own_ref), channel_id=1, source_target_pairs={{0,192},{64,128},{128,64},{192,0},{1,193},{65,129},{129,65},{193,1... | collective-permute-start | bytes 294920 | tf_op jit(solution)/shard_map/ppermute | solution.py:193
  64.1 2.4 %collective-permute-done.12.r3_ref = bf16[192,256]{1,0:T(8,128)(2,1)S(1)} collective-permute-done((bf16[192,256]{1,0:T(8,128)(2,1)S(1)}, bf16[192,256]{1,0:T(8,128)(2,1)S(1)}, u32[]{:S(2)}, u32[]{:S(2)}) %collective-permute-start.12) | collective-permute-done | bytes 98336 | tf_op jit(solution)/shard_map/ppermute | solution.py:193
  66.7 22.9 %all_to_all.11.error_ref = bf16[16,192,256]{2,1,0:T(8,128)(2,1)S(1)} all-to-all(bf16[16,192,256]{2,1,0:T(8,128)(2,1)S(1)} %shard_map.98), channel_id=1, replica_groups={{0,16,32,48,4,20,36,52,8,24,40,56,12,28,44,60},{1,5,9,13,17,21,25,29,33..., dimensions={0} | all-to-all | bytes 3145728 | tf_op jit(solution)/shard_map/all_to_all | solution.py:245
  90.5 5.7 %collective-permute-start.13 = (bf16[192,128]{1,0:T(8,128)(2,1)S(1)}, bf16[192,128]{1,0:T(8,128)(2,1)S(1)}, u32[]{:S(2)}, u32[]{:S(2)}) collective-permute-start(bf16[192,128]{1,0:T(8,128)(2,1)S(1)} %get-tuple-element.34), channel_id=1, source_target_pairs={{0,2},{2,0},{1,3},{3,1},{4,6},{6,4},{5,7},{7,5},{8,10},{10,8},{9,1... | collective-permute-start | bytes 147464 | tf_op jit(solution)/shard_map/ppermute | solution.py:193
  96.2 3.0 %shard_map.100 = (f32[256,4096]{1,0:T(8,128)}, f32[1,4096]{1,0:T(1,128)}, f32[8,128]{1,0:T(8,128)S(1)}) custom-call(bf16[16,192,256]{2,1,0:T(8,128)(2,1)S(1)} %all_to_all.11.error_ref, bf16[192,256]{1,0:T(8,128)(2,1)S(1)} %get-tuple-element.35.feats_ref), custom_call_target="tpu_custom_call" | custom-call | tf_op jit(solution)/shard_map/pallas_call | solution.py:25
  99.2 5.1 %collective-permute-start.14 = (f32[192,128]{1,0:T(8,128)S(1)}, f32[192,128]{1,0:T(8,128)S(1)}, u32[]{:S(2)}, u32[]{:S(2)}) collective-permute-start(f32[192,128]{1,0:T(8,128)S(1)} %shard_map.101.pair_ref), channel_id=1, source_target_pairs={{0,1},{1,0},{2,3},{3,2},{4,5},{5,4},{6,7},{7,6},{8,9},{9,8},{10,11... | collective-permute-start | bytes 294920 | tf_op jit(solution)/shard_map/ppermute | solution.py:193
  105.2 1.8 %shard_map.102 = (f32[64,4096]{1,0:T(8,128)}, f32[1,64]{1,0:T(1,128)}) custom-call(bf16[384,1024]{1,0:T(8,128)(2,1)S(1)} %bitcast.11, bf16[384,1024]{1,0:T(8,128)(2,1)S(1)} %collective-permute-done.3.other_ref, f32[192,128]{1,0:T(8,128)S(1)} %shard_map.101.pair_ref, f32[192,128]{1,0:T(8,128)S(1)} %collective-permute-done.14.near_ref, ...), custom_call_target="tpu_custom_call" | custom-call | tf_op jit(solution)/shard_map/pallas_call | solution.py:25
  (30 shorter events, 5.8 us)
Async XLA Ops:
  0.6 35.8 %copy-start = (bf16[1,256,4096]{2,1,0:T(8,128)(2,1)S(1)}, bf16[1,256,4096]{2,1,0:T(8,128)(2,1)}, u32[]{:S(2)}) copy-start(bf16[1,256,4096]{2,1,0:T(8,128)(2,1)} %param.9) | copy-start | bytes 6291460
  0.6 9.1 %collective-permute-start = (bf16[3,4096]{1,0:T(4,128)(2,1)}, bf16[3,4096]{1,0:T(4,128)(2,1)S(1)}, u32[]{:S(2)}, u32[]{:S(2)}) collective-permute-start(bf16[3,4096]{1,0:T(4,128)(2,1)} %tokens_ref.1), channel_id=1, source_target_pairs={{0,64},{64,128},{128,192},{192,2},{2,66},{66,130},{130,194},{194,0... | collective-permute-start | bytes 73736 | tf_op jit(solution)/shard_map/ppermute | solution.py:218
  3.2 6.6 %collective-permute-start.1 = (bf16[3,4096]{1,0:T(4,128)(2,1)}, bf16[3,4096]{1,0:T(4,128)(2,1)S(1)}, u32[]{:S(2)}, u32[]{:S(2)}) collective-permute-start(bf16[3,4096]{1,0:T(4,128)(2,1)} %tokens_ref.1), channel_id=1, source_target_pairs={{0,194},{64,0},{128,64},{192,128},{2,192},{66,2},{130,66},{194,130... | collective-permute-start | bytes 73736 | tf_op jit(solution)/shard_map/ppermute | solution.py:218
  7.2 5.3 %collective-permute-start.2 = (bf16[3,4096]{1,0:T(4,128)(2,1)}, bf16[3,4096]{1,0:T(4,128)(2,1)S(1)}, u32[]{:S(2)}, u32[]{:S(2)}) collective-permute-start(bf16[3,4096]{1,0:T(4,128)(2,1)} %tokens_ref.1), channel_id=1, source_target_pairs={{0,128},{64,192},{128,2},{192,66},{2,130},{66,194},{130,0},{194,64... | collective-permute-start | bytes 73736 | tf_op jit(solution)/shard_map/ppermute | solution.py:218
  7.2 1.6 %copy-start.1 = (bf16[4096,256]{1,0:T(8,128)(2,1)S(1)}, bf16[4096,256]{1,0:T(8,128)(2,1)}, u32[]{:S(2)}) copy-start(bf16[4096,256]{1,0:T(8,128)(2,1)} %enc_ref.1) | copy-start | bytes 6291460
  8.8 0.8 copy-start.2
  9.6 26.9 %copy-start.3 = (bf16[1,3,4096]{2,1,0:T(4,128)(2,1)S(1)}, bf16[1,3,4096]{2,1,0:T(4,128)(2,1)}, u32[]{:S(2)}) copy-start(bf16[1,3,4096]{2,1,0:T(4,128)(2,1)} %param.11) | copy-start | bytes 73732
  9.6 26.9 %copy-start.5 = (f32[256]{0:T(256)S(1)}, f32[256]{0:T(256)}, u32[]{:S(2)}) copy-start(f32[256]{0:T(256)} %param.8) | copy-start | bytes 3076
  31.2 5.3 %collective-permute-start.3 = (bf16[384,1024]{1,0:T(8,128)(2,1)S(1)}, bf16[384,1024]{1,0:T(8,128)(2,1)S(1)}, u32[]{:S(2)}, u32[]{:S(2)}) collective-permute-start(bf16[384,1024]{1,0:T(8,128)(2,1)S(1)} %bitcast.9), channel_id=1, source_target_pairs={{0,1},{1,0},{2,3},{3,2},{4,5},{5,4},{6,7},{7,6},{8,9},{9,8},{10,11... | collective-permute-start | bytes 2359304 | tf_op jit(solution)/shard_map/ppermute | solution.py:193
  38.0 28.5 %copy-start.4 = (f32[1,4096]{1,0:T(1,128)S(1)}, f32[1,4096]{1,0:T(1,128)}, u32[]{:S(2)}) copy-start(f32[1,4096]{1,0:T(1,128)} %bias_ref.1) | copy-start | bytes 49156
  38.1 7.0 %collective-permute-start.4 = (bf16[192,1024]{1,0:T(8,128)(2,1)S(1)}, bf16[192,1024]{1,0:T(8,128)(2,1)S(1)}, u32[]{:S(2)}, u32[]{:S(2)}) collective-permute-start(bf16[192,1024]{1,0:T(8,128)(2,1)S(1)} %get-tuple-element.26), channel_id=1, source_target_pairs={{0,4},{1,17},{4,0},{5,21},{8,12},{9,25},{12,8},{13,29},{16,20},{17... | collective-permute-start | bytes 1179656 | tf_op jit(solution)/shard_map/ppermute | solution.py:203
  38.2 11.5 %collective-permute-start.5 = (bf16[192,1024]{1,0:T(8,128)(2,1)S(1)}, bf16[192,1024]{1,0:T(8,128)(2,1)S(1)}, u32[]{:S(2)}, u32[]{:S(2)}) collective-permute-start(bf16[192,1024]{1,0:T(8,128)(2,1)S(1)} %get-tuple-element.27), channel_id=1, source_target_pairs={{0,8},{1,33},{4,12},{5,37},{8,0},{9,41},{12,4},{13,45},{16,24},{17... | collective-permute-start | bytes 1179656 | tf_op jit(solution)/shard_map/ppermute | solution.py:203
  39.9 12.3 %collective-permute-start.6 = (bf16[192,1024]{1,0:T(8,128)(2,1)S(1)}, bf16[192,1024]{1,0:T(8,128)(2,1)S(1)}, u32[]{:S(2)}, u32[]{:S(2)}) collective-permute-start(bf16[192,1024]{1,0:T(8,128)(2,1)S(1)} %get-tuple-element.28), channel_id=1, source_target_pairs={{0,12},{1,49},{4,8},{5,53},{8,4},{9,57},{12,0},{13,61},{16,28},{17... | collective-permute-start | bytes 1179656 | tf_op jit(solution)/shard_map/ppermute | solution.py:203
  52.5 3.9 %collective-permute-start.7 = (bf16[192,256]{1,0:T(8,128)(2,1)S(1)}, bf16[192,256]{1,0:T(8,128)(2,1)S(1)}, u32[]{:S(2)}, u32[]{:S(2)}) collective-permute-start(bf16[192,256]{1,0:T(8,128)(2,1)S(1)} %get-tuple-element.30), channel_id=1, source_target_pairs={{0,16},{1,5},{4,20},{5,1},{8,24},{9,13},{12,28},{13,9},{16,0},{17,... | collective-permute-start | bytes 294920 | tf_op jit(solution)/shard_map/ppermute | solution.py:203
  52.6 5.1 %collective-permute-start.8 = (bf16[192,256]{1,0:T(8,128)(2,1)S(1)}, bf16[192,256]{1,0:T(8,128)(2,1)S(1)}, u32[]{:S(2)}, u32[]{:S(2)}) collective-permute-start(bf16[192,256]{1,0:T(8,128)(2,1)S(1)} %get-tuple-element.31), channel_id=1, source_target_pairs={{0,32},{1,9},{4,36},{5,13},{8,40},{9,1},{12,44},{13,5},{16,48},{17... | collective-permute-start | bytes 294920 | tf_op jit(solution)/shard_map/ppermute | solution.py:203
  54.5 5.0 %collective-permute-start.9 = (bf16[192,256]{1,0:T(8,128)(2,1)S(1)}, bf16[192,256]{1,0:T(8,128)(2,1)S(1)}, u32[]{:S(2)}, u32[]{:S(2)}) collective-permute-start(bf16[192,256]{1,0:T(8,128)(2,1)S(1)} %get-tuple-element.32), channel_id=1, source_target_pairs={{0,48},{1,13},{4,52},{5,9},{8,56},{9,5},{12,60},{13,1},{16,32},{17... | collective-permute-start | bytes 294920 | tf_op jit(solution)/shard_map/ppermute | solution.py:203
  59.5 3.6 %collective-permute-start.10 = (bf16[192,256]{1,0:T(8,128)(2,1)S(1)}, bf16[192,256]{1,0:T(8,128)(2,1)S(1)}, u32[]{:S(2)}, u32[]{:S(2)}) collective-permute-start(bf16[192,256]{1,0:T(8,128)(2,1)S(1)} %shard_map.97.own_ref), channel_id=1, source_target_pairs={{0,64},{64,0},{128,192},{192,128},{1,65},{65,1},{129,193},{193,129... | collective-permute-start | bytes 294920 | tf_op jit(solution)/shard_map/ppermute | solution.py:193
  59.6 4.5 %collective-permute-start.11 = (bf16[192,256]{1,0:T(8,128)(2,1)S(1)}, bf16[192,256]{1,0:T(8,128)(2,1)S(1)}, u32[]{:S(2)}, u32[]{:S(2)}) collective-permute-start(bf16[192,256]{1,0:T(8,128)(2,1)S(1)} %shard_map.97.own_ref), channel_id=1, source_target_pairs={{0,128},{64,192},{128,0},{192,64},{1,129},{65,193},{129,1},{193,65... | collective-permute-start | bytes 294920 | tf_op jit(solution)/shard_map/ppermute | solution.py:193
  61.1 5.4 %collective-permute-start.12 = (bf16[192,256]{1,0:T(8,128)(2,1)S(1)}, bf16[192,256]{1,0:T(8,128)(2,1)S(1)}, u32[]{:S(2)}, u32[]{:S(2)}) collective-permute-start(bf16[192,256]{1,0:T(8,128)(2,1)S(1)} %shard_map.97.own_ref), channel_id=1, source_target_pairs={{0,192},{64,128},{128,64},{192,0},{1,193},{65,129},{129,65},{193,1... | collective-permute-start | bytes 294920 | tf_op jit(solution)/shard_map/ppermute | solution.py:193
  90.5 8.7 %collective-permute-start.13 = (bf16[192,128]{1,0:T(8,128)(2,1)S(1)}, bf16[192,128]{1,0:T(8,128)(2,1)S(1)}, u32[]{:S(2)}, u32[]{:S(2)}) collective-permute-start(bf16[192,128]{1,0:T(8,128)(2,1)S(1)} %get-tuple-element.34), channel_id=1, source_target_pairs={{0,2},{2,0},{1,3},{3,1},{4,6},{6,4},{5,7},{7,5},{8,10},{10,8},{9,1... | collective-permute-start | bytes 147464 | tf_op jit(solution)/shard_map/ppermute | solution.py:193
  99.2 6.0 %collective-permute-start.14 = (f32[192,128]{1,0:T(8,128)S(1)}, f32[192,128]{1,0:T(8,128)S(1)}, u32[]{:S(2)}, u32[]{:S(2)}) collective-permute-start(f32[192,128]{1,0:T(8,128)S(1)} %shard_map.101.pair_ref), channel_id=1, source_target_pairs={{0,1},{1,0},{2,3},{3,2},{4,5},{5,4},{6,7},{7,6},{8,9},{9,8},{10,11... | collective-permute-start | bytes 294920 | tf_op jit(solution)/shard_map/ppermute | solution.py:193

commit v5 on v4

--- a/solution.py
+++ b/solution.py
@@ -69,10 +69,9 @@
 
 def forward_kernel(
     own_ref, other_ref, enc_ref, enc_bias_ref, dec_ref, target_ref,
-    keep_ref, send1_ref, send2_ref, send3_ref, pos_ref, feats_ref, acc_ref,
+    send2_ref, pos_ref, feats_ref, acc_ref,
 ):
-    core, zl = lax.axis_index("core"), lax.axis_index("zl")
-    member = lax.axis_index("y") * 4 + lax.axis_index("x")
+    core = lax.axis_index("core")
     a, _ = coordinates()
     sums = []
     for h in range(2):
@@ -91,20 +90,29 @@
     pos_ref[...] = positive
     feats = (positive * positive).astype(BF16)
     feats_ref[...] = feats
+    product(feats, dec_ref, target_ref, a ^ 2, acc_ref)
+    send2_ref[...] = acc_ref[...].astype(BF16)
+
+
+def product(feats, dec_ref, target_ref, at, acc_ref):
+    zl, member = lax.axis_index("zl"), lax.axis_index("y") * 4 + lax.axis_index("x")
     lane_sub = lax.broadcasted_iota(jnp.int32, (8, WIDE), 0)
-    for key in (2, 1, 3, 0):
-        out_ref = (keep_ref, send1_ref, send2_ref, send3_ref)[key]
-        place = columns(a ^ key, WIDE)
-        acc = keep_ref if key == 0 else acc_ref.at[key % 2]
-        acc[...] = jnp.dot(feats, dec_ref[:, place], preferred_element_type=F32)
-        values = target_ref[:, place].astype(F32)
-        for i in range(ROWS):
-            group = ROWS * member + i
-            tile = pl.ds(pl.multiple_of(8 * (group // 2), 8), 8)
-            row = 4 * (group % 2) + zl
-            acc[tile, :] = acc[tile, :] - jnp.where(lane_sub == row, values[i : i + 1], 0.0)
-        if key:
-            out_ref[...] = acc[...].astype(BF16)
+    place = columns(at, WIDE)
+    acc_ref[...] = jnp.dot(feats, dec_ref[:, place], preferred_element_type=F32)
+    values = target_ref[:, place].astype(F32)
+    for i in range(ROWS):
+        group = ROWS * member + i
+        tile = pl.ds(pl.multiple_of(8 * (group // 2), 8), 8)
+        row = 4 * (group % 2) + zl
+        acc_ref[tile, :] = acc_ref[tile, :] - jnp.where(lane_sub == row, values[i : i + 1], 0.0)
+
+
+def rest_kernel(feats_ref, dec_ref, target_ref, keep_ref, send1_ref, send3_ref, acc_ref):
+    a, _ = coordinates()
+    for key, out_ref in ((1, send1_ref), (3, send3_ref)):
+        product(feats_ref[...], dec_ref, target_ref, a ^ key, acc_ref.at[key // 2])
+        out_ref[...] = acc_ref[key // 2].astype(BF16)
+    product(feats_ref[...], dec_ref, target_ref, a, keep_ref)
 
 
 def middle_kernel(keep_ref, r1_ref, r2_ref, r3_ref, out_ref, send1_ref, send2_ref, send3_ref):
@@ -117,12 +125,12 @@
         ref[...] = total.astype(ref.dtype)
 
 
-def sum_kernel(keep_ref, r1_ref, r2_ref, r3_ref, out_ref):
+def sum_kernel(keep_ref, r2_ref, r1_ref, r3_ref, out_ref):
     r1, r2, r3 = [ref[...].astype(F32) for ref in (r1_ref, r2_ref, r3_ref)]
     out_ref[...] = ((keep_ref[...] + r1) + (r2 + r3)).astype(BF16)
 
 
-def error_kernel(own_ref, r1_ref, r2_ref, r3_ref, bias_ref, out_ref):
+def error_kernel(own_ref, r2_ref, r3_ref, r1_ref, bias_ref, out_ref):
     a, b = coordinates()
     own, r1, r2, r3 = [ref[...].astype(F32) for ref in (own_ref, r1_ref, r2_ref, r3_ref)]
     bias = bias_ref[:, columns(4 * a + b, PIECE)]
@@ -131,16 +139,22 @@
         out_ref[j] = error
 
 
-def back_kernel(error_ref, dec_ref, keep_ref, send_ref):
-    zh = lax.axis_index("zh")
-    total = jnp.zeros((COUNT, FEATS), F32)
+def back_half(error_ref, dec_ref, side):
+    rows = columns(side, FEATS // 2)
+    total = jnp.zeros((COUNT, FEATS // 2), F32)
     for j in range(J):
         total = total + lax.dot_general(
-            error_ref[j], dec_ref[:, j * PIECE : (j + 1) * PIECE], NT, preferred_element_type=F32
+            error_ref[j], dec_ref[rows, j * PIECE : (j + 1) * PIECE], NT, preferred_element_type=F32
         )
-    half = FEATS // 2
-    keep_ref[...] = jnp.where(zh == 0, total[:, :half], total[:, half:])
-    send_ref[...] = jnp.where(zh == 0, total[:, half:], total[:, :half]).astype(BF16)
+    return total
+
+
+def send_kernel(error_ref, dec_ref, out_ref):
+    out_ref[...] = back_half(error_ref, dec_ref, 1 - lax.axis_index("zh")).astype(BF16)
+
+
+def keep_kernel(error_ref, dec_ref, out_ref):
+    out_ref[...] = back_half(error_ref, dec_ref, lax.axis_index("zh"))
 
 
 def decoder_kernel(error_ref, feats_ref, grad_ref, bias_ref, done_ref, part_ref, sems):
@@ -215,7 +229,7 @@
     sds, vmem = jax.ShapeDtypeStruct, pltpu.VMEM
     dec = decoder_weight[0]
 
-    near_rows = [lax.ppermute(tokens, ("zl", "zh"), ring(step)) for step in (1, 7, 2)]
+    far_rows, *near_rows = [lax.ppermute(tokens, ("zl", "zh"), ring(step)) for step in (2, 1, 7)]
     tokens, encoder_weight = call(
         load_kernel,
         (vmem(tokens.shape, BF16), vmem(encoder_weight.shape, BF16)),
@@ -223,30 +237,39 @@
         in_specs=[pl.BlockSpec(memory_space=pl.ANY)] * 2,
         scratch_shapes=[pltpu.SemaphoreType.DMA((2,))],
     )
-    packed = call(pack_kernel, vmem((J, 8 * ROWS, WIDE), BF16), tokens, *near_rows, vmem=range(4))
+    packed = call(pack_kernel, vmem((J, 8 * ROWS, WIDE), BF16), tokens, *near_rows, far_rows, vmem=range(4))
     own = lax.all_to_all(packed, ("y", "x"), 0, 0, tiled=True)
     own = own.reshape(2 * COUNT, WIDE)
     other = mirror(own, "core", 2, 1)
 
     wide, piece = (COUNT, WIDE), (COUNT, PIECE)
-    keep, *sends, positive, feats = call(
+    send2, positive, feats = call(
         forward_kernel,
-        (vmem(wide, F32),) + (vmem(wide, BF16),) * 3 + (vmem((COUNT, FEATS), F32), vmem((COUNT, FEATS), BF16)),
+        (vmem(wide, BF16), vmem((COUNT, FEATS), F32), vmem((COUNT, FEATS), BF16)),
         own, other, encoder_weight, encoder_bias[None], dec, targets[0],
-        vmem=(0, 1, 2, 4),
+        vmem=(0, 1, 2, 4, 5),
+        scratch_shapes=[vmem(wide, F32)],
+    )
+    moved2 = plane_swap(send2, True, 2)
+    keep, send1, send3 = call(
+        rest_kernel,
+        (vmem(wide, F32), vmem(wide, BF16), vmem(wide, BF16)),
+        feats, dec, targets[0],
+        vmem=range(3),
         scratch_shapes=[vmem((2,) + wide, F32)],
     )
-    moved = [plane_swap(sends[key - 1], True, key) for key in KEYS]
+    moved = [plane_swap(send1, True, 1), moved2, plane_swap(send3, True, 3)]
     keep, *sends = call(middle_kernel, (vmem(piece, F32),) + (vmem(piece, BF16),) * 3, keep, *moved, vmem=range(4))
-    moved = [plane_swap(sends[key - 1], False, key) for key in KEYS]
+    moved = [plane_swap(sends[key - 1], False, key) for key in (2, 1, 3)]
     part = call(sum_kernel, vmem(piece, BF16), keep, *moved, vmem=range(4))
-    moved = [mirror(part, "zl", DEPTH, key) for key in KEYS]
+    moved = [mirror(part, "zl", DEPTH, key) for key in (2, 3, 1)]
     copies = call(error_kernel, vmem((J,) + piece, BF16), part, *moved, decoder_bias, vmem=range(4))
     errors = lax.all_to_all(copies, FEAT + TGT, 0, 0, axis_index_groups=plane_groups(), tiled=True)
 
     half = (COUNT, FEATS // 2)
-    keep, send = call(back_kernel, (vmem(half, F32), vmem(half, BF16)), errors, dec, vmem=range(2))
+    send = call(send_kernel, vmem(half, BF16), errors, dec, vmem=range(2))
     peer = mirror(send, "zh", 2, 1)
+    keep = call(keep_kernel, vmem(half, F32), errors, dec, vmem=range(2))
     decoder_grad, bias_grad, done = call(
         decoder_kernel,
         (sds((FEATS, D), F32), sds((1, D), F32), vmem((8, 128), F32)),

time: 108 us -> 104 us (0.963); the launches traced: 107 us -> 104 us
  starting transfers between devices: 32.2 us -> 26.9 us
  waiting for transfers between devices: 22.3 us -> 24.4 us
    ppermute x6, starting transfers between devices: 17.8 us -> 13.6 us  [mirror(): return lax.ppermute(x, axes, [(i, i ^ key) for i in range(size)])]
    ppermute x6, waiting for transfers between devices: 6.26 us -> 9.71 us  [mirror(): return lax.ppermute(x, axes, [(i, i ^ key) for i in range(size)])]
    ppermute x6, waiting for transfers between devices: 13.3 us -> 12 us  [plane_swap(): return lax.ppermute(x, ('y', 'x', 'core'), pairs)]
    ppermute x6, starting transfers between devices: 7.88 us -> 6.67 us  [plane_swap(): return lax.ppermute(x, ('y', 'x', 'core'), pairs)]
    pallas_call x10 -> x12, Pallas kernels: 7.9 us -> 8.4 us  [call(): pl.pallas_call(kernel, out_shape=outs, compiler_params=pltpu.CompilerPara...]
  transfers between devices with their start and end apart: 15 -> 15, of which waited for: 10 -> 10; matrix products, arithmetic and copies ran while one was open for 0% -> 0% of each run, Pallas kernels for 3% -> 4%
where the time goes in v5:
time: 104 us
  blocking collectives  41.3 us (40%)
  starting transfers between devices  26.9 us (26%)
  waiting for transfers between devices  24.4 us (23%)
  Pallas kernels  8.4 us (8%)
  local copies, waits for them, and re-layouts  2.37 us (2%)
    all_to_all x1, blocking collectives, body(): lax.all_to_all(copies, FEAT + TGT, 0, 0, axis_index_groups=plane_groups()...  22.7 us
    all_to_all x1, blocking collectives, body(): own = lax.all_to_all(packed, ('y', 'x'), 0, 0, tiled=True)  18.5 us
    ppermute x6, starting transfers between devices, mirror(): return lax.ppermute(x, axes, [(i, i ^ key) for i in range(size)])  13.6 us
    ppermute x6, waiting for transfers between devices, plane_swap(): return lax.ppermute(x, ('y', 'x', 'core'), pairs)  12 us
    ppermute x6, waiting for transfers between devices, mirror(): return lax.ppermute(x, axes, [(i, i ^ key) for i in range(size)])  9.71 us
    pallas_call x12, Pallas kernels, call(): pl.pallas_call(kernel, out_shape=outs, compiler_params=pltpu.CompilerPara...  8.4 us
    ppermute x6, starting transfers between devices, plane_swap(): return lax.ppermute(x, ('y', 'x', 'core'), pairs)  6.67 us
    ppermute x3, starting transfers between devices, body(): lax.ppermute(tokens, ('zl', 'zh'), ring(step))  6.57 us
  transfers between devices with their start and end apart: 15, of which 10 were waited for; matrix products, arithmetic and copies ran while one was open for 0% of the time, Pallas kernels for 4%

profile of v5, /device:TPU:1, one launch (start us, length us, event | category | flops | bytes accessed | tf_op | source)
XLA Modules:
  0.0 104.1 jit_solution(17678153259770190554)
XLA Ops:
  0.6 2.5 %collective-permute-start = (bf16[3,4096]{1,0:T(4,128)(2,1)}, bf16[3,4096]{1,0:T(4,128)(2,1)S(1)}, u32[]{:S(2)}, u32[]{:S(2)}) collective-permute-start(bf16[3,4096]{1,0:T(4,128)(2,1)} %tokens_ref.1), channel_id=1, source_target_pairs={{0,64},{64,128},{128,192},{192,2},{2,66},{66,130},{130,194},{194,0... | collective-permute-start | bytes 73736 | tf_op jit(solution)/shard_map/ppermute | solution.py:232
  3.2 4.0 %collective-permute-start.1 = (bf16[3,4096]{1,0:T(4,128)(2,1)}, bf16[3,4096]{1,0:T(4,128)(2,1)S(1)}, u32[]{:S(2)}, u32[]{:S(2)}) collective-permute-start(bf16[3,4096]{1,0:T(4,128)(2,1)} %tokens_ref.1), channel_id=1, source_target_pairs={{0,194},{64,0},{128,64},{192,128},{2,192},{66,2},{130,66},{194,130... | collective-permute-start | bytes 73736 | tf_op jit(solution)/shard_map/ppermute | solution.py:232
  7.2 1.6 %copy-done.1 = bf16[4096,256]{1,0:T(8,128)(2,1)S(1)} copy-done((bf16[4096,256]{1,0:T(8,128)(2,1)S(1)}, bf16[4096,256]{1,0:T(8,128)(2,1)}, u32[]{:S(2)}) %copy-start.1) | copy-done | bytes 2097176
  9.8 2.7 %collective-permute-done.2.far_ref = bf16[3,4096]{1,0:T(4,128)(2,1)S(1)} collective-permute-done((bf16[3,4096]{1,0:T(4,128)(2,1)}, bf16[3,4096]{1,0:T(4,128)(2,1)S(1)}, u32[]{:S(2)}, u32[]{:S(2)}) %collective-permute-start.2) | collective-permute-done | bytes 24608 | tf_op jit(solution)/shard_map/ppermute | solution.py:232
  12.7 18.5 %all_to_all.10 = bf16[16,24,1024]{2,1,0:T(8,128)(2,1)S(1)} all-to-all(bf16[16,24,1024]{2,1,0:T(8,128)(2,1)S(1)} %shard_map.94), channel_id=1, replica_groups=mesh['zl'=4,'y'=4,'x'=4,'zh'=2,'core'=2] {'y','x'}, dimensions={0} | all-to-all | bytes 1572864 | tf_op jit(solution)/shard_map/all_to_all | solution.py:241
  31.2 3.4 %collective-permute-start.3 = (bf16[384,1024]{1,0:T(8,128)(2,1)S(1)}, bf16[384,1024]{1,0:T(8,128)(2,1)S(1)}, u32[]{:S(2)}, u32[]{:S(2)}) collective-permute-start(bf16[384,1024]{1,0:T(8,128)(2,1)S(1)} %bitcast.11), channel_id=1, source_target_pairs={{0,1},{1,0},{2,3},{3,2},{4,5},{5,4},{6,7},{7,6},{8,9},{9,8},{10,11... | collective-permute-start | bytes 2359304 | tf_op jit(solution)/shard_map/ppermute | solution.py:207
  34.6 1.9 %collective-permute-done.3.other_ref = bf16[384,1024]{1,0:T(8,128)(2,1)S(1)} collective-permute-done((bf16[384,1024]{1,0:T(8,128)(2,1)S(1)}, bf16[384,1024]{1,0:T(8,128)(2,1)S(1)}, u32[]{:S(2)}, u32[]{:S(2)}) %collective-permute-start.3) | collective-permute-done | bytes 786464 | tf_op jit(solution)/shard_map/ppermute | solution.py:207
  36.5 1.2 %shard_map.95 = (bf16[192,1024]{1,0:T(8,128)(2,1)S(1)}, f32[192,256]{1,0:T(8,128)S(1)}, bf16[192,256]{1,0:T(8,128)(2,1)S(1)}) custom-call(bf16[384,1024]{1,0:T(8,128)(2,1)S(1)} %bitcast.12, bf16[384,1024]{1,0:T(8,128)(2,1)S(1)} %collective-permute-done.3.other_ref, bf16[4096,256]{1,0:T(8,128)(2,1)S(1)} %get-tuple-element.22.enc_ref, f32[1,256]{1,0:T(1,128)S(1)} %bitcast.16, ...), custom_call_target="tpu_custom_call" | custom-call | tf_op jit(solution)/shard_map/pallas_call | solution.py:25
  39.2 2.4 %collective-permute-start.5 = (bf16[192,1024]{1,0:T(8,128)(2,1)S(1)}, bf16[192,1024]{1,0:T(8,128)(2,1)S(1)}, u32[]{:S(2)}, u32[]{:S(2)}) collective-permute-start(bf16[192,1024]{1,0:T(8,128)(2,1)S(1)} %get-tuple-element.26), channel_id=1, source_target_pairs={{0,8},{1,33},{4,12},{5,37},{8,0},{9,41},{12,4},{13,45},{16,24},{17... | collective-permute-start | bytes 1179656 | tf_op jit(solution)/shard_map/ppermute | solution.py:217
  41.6 3.7 %collective-permute-done.4.r1_ref = bf16[192,1024]{1,0:T(8,128)(2,1)S(1)} collective-permute-done((bf16[192,1024]{1,0:T(8,128)(2,1)S(1)}, bf16[192,1024]{1,0:T(8,128)(2,1)S(1)}, u32[]{:S(2)}, u32[]{:S(2)}) %collective-permute-start.4) | collective-permute-done | bytes 393248 | tf_op jit(solution)/shard_map/ppermute | solution.py:217
  45.3 5.5 %collective-permute-done.6.r3_ref = bf16[192,1024]{1,0:T(8,128)(2,1)S(1)} collective-permute-done((bf16[192,1024]{1,0:T(8,128)(2,1)S(1)}, bf16[192,1024]{1,0:T(8,128)(2,1)S(1)}, u32[]{:S(2)}, u32[]{:S(2)}) %collective-permute-start.6) | collective-permute-done | bytes 393248 | tf_op jit(solution)/shard_map/ppermute | solution.py:217
  52.3 2.1 %collective-permute-start.9 = (bf16[192,256]{1,0:T(8,128)(2,1)S(1)}, bf16[192,256]{1,0:T(8,128)(2,1)S(1)}, u32[]{:S(2)}, u32[]{:S(2)}) collective-permute-start(bf16[192,256]{1,0:T(8,128)(2,1)S(1)} %get-tuple-element.31), channel_id=1, source_target_pairs={{0,48},{1,13},{4,52},{5,9},{8,56},{9,5},{12,60},{13,1},{16,32},{17... | collective-permute-start | bytes 294920 | tf_op jit(solution)/shard_map/ppermute | solution.py:217
  54.4 1.7 %collective-permute-done.7.r2_ref = bf16[192,256]{1,0:T(8,128)(2,1)S(1)} collective-permute-done((bf16[192,256]{1,0:T(8,128)(2,1)S(1)}, bf16[192,256]{1,0:T(8,128)(2,1)S(1)}, u32[]{:S(2)}, u32[]{:S(2)}) %collective-permute-start.7) | collective-permute-done | bytes 98336 | tf_op jit(solution)/shard_map/ppermute | solution.py:217
  56.1 1.0 collective-permute-done.9.r3_ref
  57.2 1.6 %collective-permute-start.10 = (bf16[192,256]{1,0:T(8,128)(2,1)S(1)}, bf16[192,256]{1,0:T(8,128)(2,1)S(1)}, u32[]{:S(2)}, u32[]{:S(2)}) collective-permute-start(bf16[192,256]{1,0:T(8,128)(2,1)S(1)} %shard_map.98.own_ref), channel_id=1, source_target_pairs={{0,128},{64,192},{128,0},{192,64},{1,129},{65,193},{129,1},{193,65... | collective-permute-start | bytes 294920 | tf_op jit(solution)/shard_map/ppermute | solution.py:207
  58.8 1.2 %collective-permute-start.12 = (bf16[192,256]{1,0:T(8,128)(2,1)S(1)}, bf16[192,256]{1,0:T(8,128)(2,1)S(1)}, u32[]{:S(2)}, u32[]{:S(2)}) collective-permute-start(bf16[192,256]{1,0:T(8,128)(2,1)S(1)} %shard_map.98.own_ref), channel_id=1, source_target_pairs={{0,64},{64,0},{128,192},{192,128},{1,65},{65,1},{129,193},{193,129... | collective-permute-start | bytes 294920 | tf_op jit(solution)/shard_map/ppermute | solution.py:207
  59.9 1.8 %collective-permute-done.10.r2_ref = bf16[192,256]{1,0:T(8,128)(2,1)S(1)} collective-permute-done((bf16[192,256]{1,0:T(8,128)(2,1)S(1)}, bf16[192,256]{1,0:T(8,128)(2,1)S(1)}, u32[]{:S(2)}, u32[]{:S(2)}) %collective-permute-start.10) | collective-permute-done | bytes 98336 | tf_op jit(solution)/shard_map/ppermute | solution.py:207
  61.7 3.3 %collective-permute-done.11.r3_ref = bf16[192,256]{1,0:T(8,128)(2,1)S(1)} collective-permute-done((bf16[192,256]{1,0:T(8,128)(2,1)S(1)}, bf16[192,256]{1,0:T(8,128)(2,1)S(1)}, u32[]{:S(2)}, u32[]{:S(2)}) %collective-permute-start.11) | collective-permute-done | bytes 98336 | tf_op jit(solution)/shard_map/ppermute | solution.py:207
  65.2 22.7 %all_to_all.11.error_ref = bf16[16,192,256]{2,1,0:T(8,128)(2,1)S(1)} all-to-all(bf16[16,192,256]{2,1,0:T(8,128)(2,1)S(1)} %shard_map.99), channel_id=1, replica_groups={{0,16,32,48,4,20,36,52,8,24,40,56,12,28,44,60},{1,5,9,13,17,21,25,29,33..., dimensions={0} | all-to-all | bytes 3145728 | tf_op jit(solution)/shard_map/all_to_all | solution.py:267
  88.5 1.6 %collective-permute-start.13 = (bf16[192,128]{1,0:T(8,128)(2,1)S(1)}, bf16[192,128]{1,0:T(8,128)(2,1)S(1)}, u32[]{:S(2)}, u32[]{:S(2)}) collective-permute-start(bf16[192,128]{1,0:T(8,128)(2,1)S(1)} %shard_map.101), channel_id=1, source_target_pairs={{0,2},{2,0},{1,3},{3,1},{4,6},{6,4},{5,7},{7,5},{8,10},{10,8},{9,1... | collective-permute-start | bytes 147464 | tf_op jit(solution)/shard_map/ppermute | solution.py:207
  90.2 3.0 %shard_map.102 = (f32[256,4096]{1,0:T(8,128)}, f32[1,4096]{1,0:T(1,128)}, f32[8,128]{1,0:T(8,128)S(1)}) custom-call(bf16[16,192,256]{2,1,0:T(8,128)(2,1)S(1)} %all_to_all.11.error_ref, bf16[192,256]{1,0:T(8,128)(2,1)S(1)} %get-tuple-element.23.feats_ref), custom_call_target="tpu_custom_call" | custom-call | tf_op jit(solution)/shard_map/pallas_call | solution.py:25
  93.7 1.8 %collective-permute-done.13.peer_ref = bf16[192,128]{1,0:T(8,128)(2,1)S(1)} collective-permute-done((bf16[192,128]{1,0:T(8,128)(2,1)S(1)}, bf16[192,128]{1,0:T(8,128)(2,1)S(1)}, u32[]{:S(2)}, u32[]{:S(2)}) %collective-permute-start.13) | collective-permute-done | bytes 49184 | tf_op jit(solution)/shard_map/ppermute | solution.py:207
  95.5 5.9 %collective-permute-start.14 = (f32[192,128]{1,0:T(8,128)S(1)}, f32[192,128]{1,0:T(8,128)S(1)}, u32[]{:S(2)}, u32[]{:S(2)}) collective-permute-start(f32[192,128]{1,0:T(8,128)S(1)} %shard_map.103.pair_ref), channel_id=1, source_target_pairs={{0,1},{1,0},{2,3},{3,2},{4,5},{5,4},{6,7},{7,6},{8,9},{9,8},{10,11... | collective-permute-start | bytes 294920 | tf_op jit(solution)/shard_map/ppermute | solution.py:207
  102.3 1.7 %shard_map.104 = (f32[64,4096]{1,0:T(8,128)}, f32[1,64]{1,0:T(1,128)}) custom-call(bf16[384,1024]{1,0:T(8,128)(2,1)S(1)} %bitcast.13, bf16[384,1024]{1,0:T(8,128)(2,1)S(1)} %collective-permute-done.3.other_ref, f32[192,128]{1,0:T(8,128)S(1)} %shard_map.103.pair_ref, f32[192,128]{1,0:T(8,128)S(1)} %collective-permute-done.14.near_ref, ...), custom_call_target="tpu_custom_call" | custom-call | tf_op jit(solution)/shard_map/pallas_call | solution.py:25
  (32 shorter events, 6.4 us)
Async XLA Ops:
  0.6 35.8 %copy-start = (bf16[1,256,4096]{2,1,0:T(8,128)(2,1)S(1)}, bf16[1,256,4096]{2,1,0:T(8,128)(2,1)}, u32[]{:S(2)}) copy-start(bf16[1,256,4096]{2,1,0:T(8,128)(2,1)} %param.9) | copy-start | bytes 6291460
  0.6 9.1 %collective-permute-start = (bf16[3,4096]{1,0:T(4,128)(2,1)}, bf16[3,4096]{1,0:T(4,128)(2,1)S(1)}, u32[]{:S(2)}, u32[]{:S(2)}) collective-permute-start(bf16[3,4096]{1,0:T(4,128)(2,1)} %tokens_ref.1), channel_id=1, source_target_pairs={{0,64},{64,128},{128,192},{192,2},{2,66},{66,130},{130,194},{194,0... | collective-permute-start | bytes 73736 | tf_op jit(solution)/shard_map/ppermute | solution.py:232
  3.2 6.6 %collective-permute-start.1 = (bf16[3,4096]{1,0:T(4,128)(2,1)}, bf16[3,4096]{1,0:T(4,128)(2,1)S(1)}, u32[]{:S(2)}, u32[]{:S(2)}) collective-permute-start(bf16[3,4096]{1,0:T(4,128)(2,1)} %tokens_ref.1), channel_id=1, source_target_pairs={{0,194},{64,0},{128,64},{192,128},{2,192},{66,2},{130,66},{194,130... | collective-permute-start | bytes 73736 | tf_op jit(solution)/shard_map/ppermute | solution.py:232
  7.2 5.3 %collective-permute-start.2 = (bf16[3,4096]{1,0:T(4,128)(2,1)}, bf16[3,4096]{1,0:T(4,128)(2,1)S(1)}, u32[]{:S(2)}, u32[]{:S(2)}) collective-permute-start(bf16[3,4096]{1,0:T(4,128)(2,1)} %tokens_ref.1), channel_id=1, source_target_pairs={{0,128},{64,192},{128,2},{192,66},{2,130},{66,194},{130,0},{194,64... | collective-permute-start | bytes 73736 | tf_op jit(solution)/shard_map/ppermute | solution.py:232
  7.2 1.6 %copy-start.1 = (bf16[4096,256]{1,0:T(8,128)(2,1)S(1)}, bf16[4096,256]{1,0:T(8,128)(2,1)}, u32[]{:S(2)}) copy-start(bf16[4096,256]{1,0:T(8,128)(2,1)} %enc_ref.1) | copy-start | bytes 6291460
  8.8 0.8 copy-start.3
  9.6 26.9 %copy-start.2 = (bf16[1,3,4096]{2,1,0:T(4,128)(2,1)S(1)}, bf16[1,3,4096]{2,1,0:T(4,128)(2,1)}, u32[]{:S(2)}) copy-start(bf16[1,3,4096]{2,1,0:T(4,128)(2,1)} %param.11) | copy-start | bytes 73732
  9.6 26.9 %copy-start.5 = (f32[256]{0:T(256)S(1)}, f32[256]{0:T(256)}, u32[]{:S(2)}) copy-start(f32[256]{0:T(256)} %param.8) | copy-start | bytes 3076
  31.2 5.3 %collective-permute-start.3 = (bf16[384,1024]{1,0:T(8,128)(2,1)S(1)}, bf16[384,1024]{1,0:T(8,128)(2,1)S(1)}, u32[]{:S(2)}, u32[]{:S(2)}) collective-permute-start(bf16[384,1024]{1,0:T(8,128)(2,1)S(1)} %bitcast.11), channel_id=1, source_target_pairs={{0,1},{1,0},{2,3},{3,2},{4,5},{5,4},{6,7},{7,6},{8,9},{9,8},{10,11... | collective-permute-start | bytes 2359304 | tf_op jit(solution)/shard_map/ppermute | solution.py:207
  37.7 27.3 %copy-start.4 = (f32[1,4096]{1,0:T(1,128)S(1)}, f32[1,4096]{1,0:T(1,128)}, u32[]{:S(2)}) copy-start(f32[1,4096]{1,0:T(1,128)} %bias_ref.1) | copy-start | bytes 49156
  38.3 7.0 %collective-permute-start.4 = (bf16[192,1024]{1,0:T(8,128)(2,1)S(1)}, bf16[192,1024]{1,0:T(8,128)(2,1)S(1)}, u32[]{:S(2)}, u32[]{:S(2)}) collective-permute-start(bf16[192,1024]{1,0:T(8,128)(2,1)S(1)} %get-tuple-element.25), channel_id=1, source_target_pairs={{0,4},{1,17},{4,0},{5,21},{8,12},{9,25},{12,8},{13,29},{16,20},{17... | collective-permute-start | bytes 1179656 | tf_op jit(solution)/shard_map/ppermute | solution.py:217
  38.4 12.4 %collective-permute-start.6 = (bf16[192,1024]{1,0:T(8,128)(2,1)S(1)}, bf16[192,1024]{1,0:T(8,128)(2,1)S(1)}, u32[]{:S(2)}, u32[]{:S(2)}) collective-permute-start(bf16[192,1024]{1,0:T(8,128)(2,1)S(1)} %get-tuple-element.27), channel_id=1, source_target_pairs={{0,12},{1,49},{4,8},{5,53},{8,4},{9,57},{12,0},{13,61},{16,28},{17... | collective-permute-start | bytes 1179656 | tf_op jit(solution)/shard_map/ppermute | solution.py:217
  39.2 11.6 %collective-permute-start.5 = (bf16[192,1024]{1,0:T(8,128)(2,1)S(1)}, bf16[192,1024]{1,0:T(8,128)(2,1)S(1)}, u32[]{:S(2)}, u32[]{:S(2)}) collective-permute-start(bf16[192,1024]{1,0:T(8,128)(2,1)S(1)} %get-tuple-element.26), channel_id=1, source_target_pairs={{0,8},{1,33},{4,12},{5,37},{8,0},{9,41},{12,4},{13,45},{16,24},{17... | collective-permute-start | bytes 1179656 | tf_op jit(solution)/shard_map/ppermute | solution.py:217
  51.0 5.1 %collective-permute-start.7 = (bf16[192,256]{1,0:T(8,128)(2,1)S(1)}, bf16[192,256]{1,0:T(8,128)(2,1)S(1)}, u32[]{:S(2)}, u32[]{:S(2)}) collective-permute-start(bf16[192,256]{1,0:T(8,128)(2,1)S(1)} %get-tuple-element.29), channel_id=1, source_target_pairs={{0,32},{1,9},{4,36},{5,13},{8,40},{9,1},{12,44},{13,5},{16,48},{17... | collective-permute-start | bytes 294920 | tf_op jit(solution)/shard_map/ppermute | solution.py:217
  51.8 4.3 %collective-permute-start.8 = (bf16[192,256]{1,0:T(8,128)(2,1)S(1)}, bf16[192,256]{1,0:T(8,128)(2,1)S(1)}, u32[]{:S(2)}, u32[]{:S(2)}) collective-permute-start(bf16[192,256]{1,0:T(8,128)(2,1)S(1)} %get-tuple-element.30), channel_id=1, source_target_pairs={{0,16},{1,5},{4,20},{5,1},{8,24},{9,13},{12,28},{13,9},{16,0},{17,... | collective-permute-start | bytes 294920 | tf_op jit(solution)/shard_map/ppermute | solution.py:217
  52.3 4.9 %collective-permute-start.9 = (bf16[192,256]{1,0:T(8,128)(2,1)S(1)}, bf16[192,256]{1,0:T(8,128)(2,1)S(1)}, u32[]{:S(2)}, u32[]{:S(2)}) collective-permute-start(bf16[192,256]{1,0:T(8,128)(2,1)S(1)} %get-tuple-element.31), channel_id=1, source_target_pairs={{0,48},{1,13},{4,52},{5,9},{8,56},{9,5},{12,60},{13,1},{16,32},{17... | collective-permute-start | bytes 294920 | tf_op jit(solution)/shard_map/ppermute | solution.py:217
  57.2 4.5 %collective-permute-start.10 = (bf16[192,256]{1,0:T(8,128)(2,1)S(1)}, bf16[192,256]{1,0:T(8,128)(2,1)S(1)}, u32[]{:S(2)}, u32[]{:S(2)}) collective-permute-start(bf16[192,256]{1,0:T(8,128)(2,1)S(1)} %shard_map.98.own_ref), channel_id=1, source_target_pairs={{0,128},{64,192},{128,0},{192,64},{1,129},{65,193},{129,1},{193,65... | collective-permute-start | bytes 294920 | tf_op jit(solution)/shard_map/ppermute | solution.py:207
  58.8 6.3 %collective-permute-start.11 = (bf16[192,256]{1,0:T(8,128)(2,1)S(1)}, bf16[192,256]{1,0:T(8,128)(2,1)S(1)}, u32[]{:S(2)}, u32[]{:S(2)}) collective-permute-start(bf16[192,256]{1,0:T(8,128)(2,1)S(1)} %shard_map.98.own_ref), channel_id=1, source_target_pairs={{0,192},{64,128},{128,64},{192,0},{1,193},{65,129},{129,65},{193,1... | collective-permute-start | bytes 294920 | tf_op jit(solution)/shard_map/ppermute | solution.py:207
  58.8 6.3 %collective-permute-start.12 = (bf16[192,256]{1,0:T(8,128)(2,1)S(1)}, bf16[192,256]{1,0:T(8,128)(2,1)S(1)}, u32[]{:S(2)}, u32[]{:S(2)}) collective-permute-start(bf16[192,256]{1,0:T(8,128)(2,1)S(1)} %shard_map.98.own_ref), channel_id=1, source_target_pairs={{0,64},{64,0},{128,192},{192,128},{1,65},{65,1},{129,193},{193,129... | collective-permute-start | bytes 294920 | tf_op jit(solution)/shard_map/ppermute | solution.py:207
  88.5 6.9 %collective-permute-start.13 = (bf16[192,128]{1,0:T(8,128)(2,1)S(1)}, bf16[192,128]{1,0:T(8,128)(2,1)S(1)}, u32[]{:S(2)}, u32[]{:S(2)}) collective-permute-start(bf16[192,128]{1,0:T(8,128)(2,1)S(1)} %shard_map.101), channel_id=1, source_target_pairs={{0,2},{2,0},{1,3},{3,1},{4,6},{6,4},{5,7},{7,5},{8,10},{10,8},{9,1... | collective-permute-start | bytes 147464 | tf_op jit(solution)/shard_map/ppermute | solution.py:207
  95.5 6.8 %collective-permute-start.14 = (f32[192,128]{1,0:T(8,128)S(1)}, f32[192,128]{1,0:T(8,128)S(1)}, u32[]{:S(2)}, u32[]{:S(2)}) collective-permute-start(f32[192,128]{1,0:T(8,128)S(1)} %shard_map.103.pair_ref), channel_id=1, source_target_pairs={{0,1},{1,0},{2,3},{3,2},{4,5},{5,4},{6,7},{7,6},{8,9},{9,8},{10,11... | collective-permute-start | bytes 294920 | tf_op jit(solution)/shard_map/ppermute | solution.py:207

commit v6 on v5

--- a/solution.py
+++ b/solution.py
@@ -1,6 +1,5 @@
 import jax
 import jax.numpy as jnp
-import numpy as np
 from jax import lax
 from jax.experimental import pallas as pl
 from jax.experimental.pallas import tpu as pltpu
@@ -50,7 +49,7 @@
         copy.wait()
 
 
-def pack_kernel(own_ref, below_ref, above_ref, far_ref, out_ref):
+def pack_kernel(own_ref, far_ref, below_ref, above_ref, out_ref):
     zl = lax.axis_index("zl")
     sub = lax.broadcasted_iota(jnp.int32, (8, WIDE), 0)
     sources = [(own_ref, 0), (below_ref, 3), (above_ref, 1), (far_ref, 2)]
@@ -134,40 +133,49 @@
     a, b = coordinates()
     own, r1, r2, r3 = [ref[...].astype(F32) for ref in (own_ref, r1_ref, r2_ref, r3_ref)]
     bias = bias_ref[:, columns(4 * a + b, PIECE)]
-    error = (((own + r1) + (r2 + r3)) + bias).astype(BF16)
-    for j in range(J):
-        out_ref[j] = error
-
-
-def back_half(error_ref, dec_ref, side):
+    out_ref[...] = (((own + r1) + (r2 + r3)) + bias).astype(BF16)
+
+
+def widen_kernel(own_ref, r2_ref, r1_ref, r3_ref, out_ref):
+    _, b = coordinates()
+    for key, ref in ((0, own_ref), (1, r1_ref), (2, r2_ref), (3, r3_ref)):
+        out_ref[:, columns(b ^ key, PIECE)] = ref[...]
+
+
+def back_half(blocks, dec_ref, side):
+    a, _ = coordinates()
     rows = columns(side, FEATS // 2)
     total = jnp.zeros((COUNT, FEATS // 2), F32)
-    for j in range(J):
+    for key, ref in zip((0, 1, 3, 2), blocks):
         total = total + lax.dot_general(
-            error_ref[j], dec_ref[rows, j * PIECE : (j + 1) * PIECE], NT, preferred_element_type=F32
+            ref[...], dec_ref[rows, columns(a ^ key, WIDE)], NT, preferred_element_type=F32
         )
     return total
 
 
-def send_kernel(error_ref, dec_ref, out_ref):
-    out_ref[...] = back_half(error_ref, dec_ref, 1 - lax.axis_index("zh")).astype(BF16)
-
-
-def keep_kernel(error_ref, dec_ref, out_ref):
-    out_ref[...] = back_half(error_ref, dec_ref, lax.axis_index("zh"))
-
-
-def decoder_kernel(error_ref, feats_ref, grad_ref, bias_ref, done_ref, part_ref, sems):
+def send_kernel(own_ref, r1_ref, r3_ref, r2_ref, dec_ref, out_ref):
+    blocks = (own_ref, r1_ref, r3_ref, r2_ref)
+    out_ref[...] = back_half(blocks, dec_ref, 1 - lax.axis_index("zh")).astype(BF16)
+
+
+def keep_kernel(own_ref, r1_ref, r3_ref, r2_ref, dec_ref, out_ref):
+    out_ref[...] = back_half((own_ref, r1_ref, r3_ref, r2_ref), dec_ref, lax.axis_index("zh"))
+
+
+def decoder_kernel(own_ref, r1_ref, r3_ref, r2_ref, feats_ref, grad_ref, bias_ref, done_ref, part_ref, row_ref, sems):
+    a, _ = coordinates()
     feats = feats_ref[...]
     copies = []
-    for k in range(4):
-        error = jnp.concatenate([error_ref[4 * k + j] for j in range(4)], axis=1)
-        place = slice(k * WIDE, (k + 1) * WIDE)
-        part_ref[k] = lax.dot_general(feats, error, TN, preferred_element_type=F32)
-        copy = pltpu.make_async_copy(part_ref.at[k], grad_ref.at[:, place], sems.at[k])
+    for key, ref in ((0, own_ref), (1, r1_ref), (3, r3_ref), (2, r2_ref)):
+        place = columns(a ^ key, WIDE)
+        part_ref[key] = lax.dot_general(feats, ref[...], TN, preferred_element_type=F32)
+        copy = pltpu.make_async_copy(part_ref.at[key], grad_ref.at[:, place], sems.at[key])
         copy.start()
         copies.append(copy)
-        bias_ref[:, place] = jnp.sum(error.astype(F32), axis=0, keepdims=True)
+        row_ref[:, place] = jnp.sum(ref[...].astype(F32), axis=0, keepdims=True)
+    copy = pltpu.make_async_copy(row_ref, bias_ref, sems.at[4])
+    copy.start()
+    copies.append(copy)
     done_ref[...] = jnp.zeros_like(done_ref)
     for copy in copies:
         copy.wait()
@@ -217,14 +225,6 @@
     return lax.ppermute(x, ("y", "x", "core"), pairs)
 
 
-def plane_groups():
-    ids = np.arange(256).reshape(4, 4, 4, 2, 2)
-    return [
-        [int(ids[(z, c % 4, c // 4) if core == 0 else (z, c // 4, c % 4)][zh, core]) for c in range(J)]
-        for z, zh, core in np.ndindex(4, 2, 2)
-    ]
-
-
 def body(tokens, encoder_weight, encoder_bias, decoder_weight, decoder_bias, targets):
     sds, vmem = jax.ShapeDtypeStruct, pltpu.VMEM
     dec = decoder_weight[0]
@@ -237,7 +237,7 @@
         in_specs=[pl.BlockSpec(memory_space=pl.ANY)] * 2,
         scratch_shapes=[pltpu.SemaphoreType.DMA((2,))],
     )
-    packed = call(pack_kernel, vmem((J, 8 * ROWS, WIDE), BF16), tokens, *near_rows, far_rows, vmem=range(4))
+    packed = call(pack_kernel, vmem((J, 8 * ROWS, WIDE), BF16), tokens, far_rows, *near_rows, vmem=range(4))
     own = lax.all_to_all(packed, ("y", "x"), 0, 0, tiled=True)
     own = own.reshape(2 * COUNT, WIDE)
     other = mirror(own, "core", 2, 1)
@@ -263,24 +263,26 @@
     moved = [plane_swap(sends[key - 1], False, key) for key in (2, 1, 3)]
     part = call(sum_kernel, vmem(piece, BF16), keep, *moved, vmem=range(4))
     moved = [mirror(part, "zl", DEPTH, key) for key in (2, 3, 1)]
-    copies = call(error_kernel, vmem((J,) + piece, BF16), part, *moved, decoder_bias, vmem=range(4))
-    errors = lax.all_to_all(copies, FEAT + TGT, 0, 0, axis_index_groups=plane_groups(), tiled=True)
+    error = call(error_kernel, vmem(piece, BF16), part, *moved, decoder_bias, vmem=range(4))
+    moved = [plane_swap(error, False, key) for key in (2, 1, 3)]
+    block = call(widen_kernel, vmem(wide, BF16), error, *moved, vmem=range(4))
+    errors = [block] + [plane_swap(block, True, key) for key in (1, 3, 2)]
 
     half = (COUNT, FEATS // 2)
-    send = call(send_kernel, vmem(half, BF16), errors, dec, vmem=range(2))
+    send = call(send_kernel, vmem(half, BF16), *errors, dec, vmem=range(5))
     peer = mirror(send, "zh", 2, 1)
-    keep = call(keep_kernel, vmem(half, F32), errors, dec, vmem=range(2))
+    keep = call(keep_kernel, vmem(half, F32), *errors, dec, vmem=range(5))
     decoder_grad, bias_grad, done = call(
         decoder_kernel,
         (sds((FEATS, D), F32), sds((1, D), F32), vmem((8, 128), F32)),
-        errors, feats,
-        vmem=range(2),
+        *errors, feats,
+        vmem=range(5),
         out_specs=(
             pl.BlockSpec(memory_space=pl.ANY),
-            pl.BlockSpec(memory_space=pltpu.VMEM),
+            pl.BlockSpec(memory_space=pl.ANY),
             pl.BlockSpec(memory_space=pltpu.VMEM),
         ),
-        scratch_shapes=[vmem((4, FEATS, WIDE), F32), pltpu.SemaphoreType.DMA((4,))],
+        scratch_shapes=[vmem((4, FEATS, WIDE), F32), vmem((1, D), F32), pltpu.SemaphoreType.DMA((5,))],
     )
     pair = call(pair_kernel, vmem(half, F32), keep, peer, done, vmem=range(3))
     near = mirror(pair, "core", 2, 1)

time: 104 us -> 104 us (level)
  blocking collectives: 41.3 us -> 18.7 us
  waiting for transfers between devices: 24.4 us -> 36.1 us
  starting transfers between devices: 26.9 us -> 38.1 us
    all_to_all x1 -> x0, blocking collectives: 22.7 us -> none  [body(): lax.all_to_all(copies, FEAT + TGT, 0, 0, axis_index_groups=plane_groups()...]
    ppermute x6 -> x12, waiting for transfers between devices: 12 us -> 26.2 us  [plane_swap(): return lax.ppermute(x, ('y', 'x', 'core'), pairs)]
    ppermute x6 -> x12, starting transfers between devices: 6.67 us -> 13.5 us  [plane_swap(): return lax.ppermute(x, ('y', 'x', 'core'), pairs)]
    ppermute x6, starting transfers between devices: 13.6 us -> 17.9 us  [mirror(): return lax.ppermute(x, axes, [(i, i ^ key) for i in range(size)])]
    ppermute x3, waiting for transfers between devices: 2.75 us -> 0.82 us  [body(): lax.ppermute(tokens, ('zl', 'zh'), ring(step))]
    pallas_call x12 -> x13, Pallas kernels: 8.4 us -> 7.75 us  [call(): pl.pallas_call(kernel, out_shape=outs, compiler_params=pltpu.CompilerPara...]
  transfers between devices with their start and end apart: 15 -> 21, of which waited for: 10 -> 16; matrix products, arithmetic and copies ran while one was open for 0% -> 0% of each run, Pallas kernels for 4% -> 3%
where the time goes in v6:
time: 104 us
  starting transfers between devices  38.1 us (37%)
  waiting for transfers between devices  36.1 us (35%)
  blocking collectives  18.7 us (18%)
  Pallas kernels  7.75 us (7%)
  local copies, waits for them, and re-layouts  2.37 us (2%)
    ppermute x12, waiting for transfers between devices, plane_swap(): return lax.ppermute(x, ('y', 'x', 'core'), pairs)  26.2 us
    all_to_all x1, blocking collectives, body(): own = lax.all_to_all(packed, ('y', 'x'), 0, 0, tiled=True)  18.7 us
    ppermute x6, starting transfers between devices, mirror(): return lax.ppermute(x, axes, [(i, i ^ key) for i in range(size)])  17.9 us
    ppermute x12, starting transfers between devices, plane_swap(): return lax.ppermute(x, ('y', 'x', 'core'), pairs)  13.5 us
    ppermute x6, waiting for transfers between devices, mirror(): return lax.ppermute(x, axes, [(i, i ^ key) for i in range(size)])  9.06 us
    pallas_call x13, Pallas kernels, call(): pl.pallas_call(kernel, out_shape=outs, compiler_params=pltpu.CompilerPara...  7.75 us
    ppermute x3, starting transfers between devices, body(): lax.ppermute(tokens, ('zl', 'zh'), ring(step))  6.66 us
    unnamed x12, local copies, waits for them, and re-layouts  2.37 us
  transfers between devices with their start and end apart: 21, of which 16 were waited for; matrix products, arithmetic and copies ran while one was open for 0% of the time, Pallas kernels for 3%

profile of v6, /device:TPU:1, one launch (start us, length us, event | category | flops | bytes accessed | tf_op | source)
XLA Modules:
  0.0 103.9 jit_solution(15380988449676280057)
XLA Ops:
  0.6 3.9 %collective-permute-start = (bf16[3,4096]{1,0:T(4,128)(2,1)}, bf16[3,4096]{1,0:T(4,128)(2,1)S(1)}, u32[]{:S(2)}, u32[]{:S(2)}) collective-permute-start(bf16[3,4096]{1,0:T(4,128)(2,1)} %tokens_ref.1), channel_id=1, source_target_pairs={{0,128},{64,192},{128,2},{192,66},{2,130},{66,194},{130,0},{194,64... | collective-permute-start | bytes 73736 | tf_op jit(solution)/shard_map/ppermute | solution.py:232
  4.5 1.6 %collective-permute-start.1 = (bf16[3,4096]{1,0:T(4,128)(2,1)}, bf16[3,4096]{1,0:T(4,128)(2,1)S(1)}, u32[]{:S(2)}, u32[]{:S(2)}) collective-permute-start(bf16[3,4096]{1,0:T(4,128)(2,1)} %tokens_ref.1), channel_id=1, source_target_pairs={{0,64},{64,128},{128,192},{192,2},{2,66},{66,130},{130,194},{194,0... | collective-permute-start | bytes 73736 | tf_op jit(solution)/shard_map/ppermute | solution.py:232
  7.3 1.6 %copy-done.1 = bf16[4096,256]{1,0:T(8,128)(2,1)S(1)} copy-done((bf16[4096,256]{1,0:T(8,128)(2,1)S(1)}, bf16[4096,256]{1,0:T(8,128)(2,1)}, u32[]{:S(2)}) %copy-start.1) | copy-done | bytes 2097176
  10.8 18.7 %all_to_all.5 = bf16[16,24,1024]{2,1,0:T(8,128)(2,1)S(1)} all-to-all(bf16[16,24,1024]{2,1,0:T(8,128)(2,1)S(1)} %shard_map.94), channel_id=1, replica_groups=mesh['zl'=4,'y'=4,'x'=4,'zh'=2,'core'=2] {'y','x'}, dimensions={0} | all-to-all | bytes 1572864 | tf_op jit(solution)/shard_map/all_to_all | solution.py:241
  29.6 3.1 %collective-permute-start.3 = (bf16[384,1024]{1,0:T(8,128)(2,1)S(1)}, bf16[384,1024]{1,0:T(8,128)(2,1)S(1)}, u32[]{:S(2)}, u32[]{:S(2)}) collective-permute-start(bf16[384,1024]{1,0:T(8,128)(2,1)S(1)} %bitcast.11), channel_id=1, source_target_pairs={{0,1},{1,0},{2,3},{3,2},{4,5},{5,4},{6,7},{7,6},{8,9},{9,8},{10,11... | collective-permute-start | bytes 2359304 | tf_op jit(solution)/shard_map/ppermute | solution.py:215
  32.7 1.9 %collective-permute-done.3.other_ref = bf16[384,1024]{1,0:T(8,128)(2,1)S(1)} collective-permute-done((bf16[384,1024]{1,0:T(8,128)(2,1)S(1)}, bf16[384,1024]{1,0:T(8,128)(2,1)S(1)}, u32[]{:S(2)}, u32[]{:S(2)}) %collective-permute-start.3) | collective-permute-done | bytes 786464 | tf_op jit(solution)/shard_map/ppermute | solution.py:215
  37.4 2.4 %collective-permute-start.5 = (bf16[192,1024]{1,0:T(8,128)(2,1)S(1)}, bf16[192,1024]{1,0:T(8,128)(2,1)S(1)}, u32[]{:S(2)}, u32[]{:S(2)}) collective-permute-start(bf16[192,1024]{1,0:T(8,128)(2,1)S(1)} %get-tuple-element.26), channel_id=1, source_target_pairs={{0,8},{1,33},{4,12},{5,37},{8,0},{9,41},{12,4},{13,45},{16,24},{17... | collective-permute-start | bytes 1179656 | tf_op jit(solution)/shard_map/ppermute | solution.py:225
  39.8 3.7 %collective-permute-done.4.r1_ref = bf16[192,1024]{1,0:T(8,128)(2,1)S(1)} collective-permute-done((bf16[192,1024]{1,0:T(8,128)(2,1)S(1)}, bf16[192,1024]{1,0:T(8,128)(2,1)S(1)}, u32[]{:S(2)}, u32[]{:S(2)}) %collective-permute-start.4) | collective-permute-done | bytes 393248 | tf_op jit(solution)/shard_map/ppermute | solution.py:225
  43.5 5.5 %collective-permute-done.6.r3_ref = bf16[192,1024]{1,0:T(8,128)(2,1)S(1)} collective-permute-done((bf16[192,1024]{1,0:T(8,128)(2,1)S(1)}, bf16[192,1024]{1,0:T(8,128)(2,1)S(1)}, u32[]{:S(2)}, u32[]{:S(2)}) %collective-permute-start.6) | collective-permute-done | bytes 393248 | tf_op jit(solution)/shard_map/ppermute | solution.py:225
  50.5 2.1 %collective-permute-start.9 = (bf16[192,256]{1,0:T(8,128)(2,1)S(1)}, bf16[192,256]{1,0:T(8,128)(2,1)S(1)}, u32[]{:S(2)}, u32[]{:S(2)}) collective-permute-start(bf16[192,256]{1,0:T(8,128)(2,1)S(1)} %get-tuple-element.31), channel_id=1, source_target_pairs={{0,48},{1,13},{4,52},{5,9},{8,56},{9,5},{12,60},{13,1},{16,32},{17... | collective-permute-start | bytes 294920 | tf_op jit(solution)/shard_map/ppermute | solution.py:225
  52.6 1.7 %collective-permute-done.7.r2_ref = bf16[192,256]{1,0:T(8,128)(2,1)S(1)} collective-permute-done((bf16[192,256]{1,0:T(8,128)(2,1)S(1)}, bf16[192,256]{1,0:T(8,128)(2,1)S(1)}, u32[]{:S(2)}, u32[]{:S(2)}) %collective-permute-start.7) | collective-permute-done | bytes 98336 | tf_op jit(solution)/shard_map/ppermute | solution.py:225
  55.4 2.2 %collective-permute-start.10 = (bf16[192,256]{1,0:T(8,128)(2,1)S(1)}, bf16[192,256]{1,0:T(8,128)(2,1)S(1)}, u32[]{:S(2)}, u32[]{:S(2)}) collective-permute-start(bf16[192,256]{1,0:T(8,128)(2,1)S(1)} %shard_map.98.own_ref), channel_id=1, source_target_pairs={{0,128},{64,192},{128,0},{192,64},{1,129},{65,193},{129,1},{193,65... | collective-permute-start | bytes 294920 | tf_op jit(solution)/shard_map/ppermute | solution.py:215
  57.6 1.4 %collective-permute-start.11 = (bf16[192,256]{1,0:T(8,128)(2,1)S(1)}, bf16[192,256]{1,0:T(8,128)(2,1)S(1)}, u32[]{:S(2)}, u32[]{:S(2)}) collective-permute-start(bf16[192,256]{1,0:T(8,128)(2,1)S(1)} %shard_map.98.own_ref), channel_id=1, source_target_pairs={{0,192},{64,128},{128,64},{192,0},{1,193},{65,129},{129,65},{193,1... | collective-permute-start | bytes 294920 | tf_op jit(solution)/shard_map/ppermute | solution.py:215
  59.8 3.2 %collective-permute-done.11.r3_ref = bf16[192,256]{1,0:T(8,128)(2,1)S(1)} collective-permute-done((bf16[192,256]{1,0:T(8,128)(2,1)S(1)}, bf16[192,256]{1,0:T(8,128)(2,1)S(1)}, u32[]{:S(2)}, u32[]{:S(2)}) %collective-permute-start.11) | collective-permute-done | bytes 98336 | tf_op jit(solution)/shard_map/ppermute | solution.py:215
  65.5 1.4 %collective-permute-start.14 = (bf16[192,256]{1,0:T(8,128)(2,1)S(1)}, bf16[192,256]{1,0:T(8,128)(2,1)S(1)}, u32[]{:S(2)}, u32[]{:S(2)}) collective-permute-start(bf16[192,256]{1,0:T(8,128)(2,1)S(1)} %shard_map.99.own_ref), channel_id=1, source_target_pairs={{0,16},{1,5},{4,20},{5,1},{8,24},{9,13},{12,28},{13,9},{16,0},{17,... | collective-permute-start | bytes 294920 | tf_op jit(solution)/shard_map/ppermute | solution.py:225
  67.6 1.7 %collective-permute-done.13.r2_ref = bf16[192,256]{1,0:T(8,128)(2,1)S(1)} collective-permute-done((bf16[192,256]{1,0:T(8,128)(2,1)S(1)}, bf16[192,256]{1,0:T(8,128)(2,1)S(1)}, u32[]{:S(2)}, u32[]{:S(2)}) %collective-permute-start.13) | collective-permute-done | bytes 98336 | tf_op jit(solution)/shard_map/ppermute | solution.py:225
  69.9 1.6 %collective-permute-done.15.r3_ref = bf16[192,256]{1,0:T(8,128)(2,1)S(1)} collective-permute-done((bf16[192,256]{1,0:T(8,128)(2,1)S(1)}, bf16[192,256]{1,0:T(8,128)(2,1)S(1)}, u32[]{:S(2)}, u32[]{:S(2)}) %collective-permute-start.15) | collective-permute-done | bytes 98336 | tf_op jit(solution)/shard_map/ppermute | solution.py:225
  72.9 2.3 %collective-permute-start.18 = (bf16[192,1024]{1,0:T(8,128)(2,1)S(1)}, bf16[192,1024]{1,0:T(8,128)(2,1)S(1)}, u32[]{:S(2)}, u32[]{:S(2)}) collective-permute-start(bf16[192,1024]{1,0:T(8,128)(2,1)S(1)} %shard_map.100.own_ref), channel_id=1, source_target_pairs={{0,8},{1,33},{4,12},{5,37},{8,0},{9,41},{12,4},{13,45},{16,24},{17... | collective-permute-start | bytes 1179656 | tf_op jit(solution)/shard_map/ppermute | solution.py:225
  75.2 3.7 %collective-permute-done.16.r1_ref = bf16[192,1024]{1,0:T(8,128)(2,1)S(1)} collective-permute-done((bf16[192,1024]{1,0:T(8,128)(2,1)S(1)}, bf16[192,1024]{1,0:T(8,128)(2,1)S(1)}, u32[]{:S(2)}, u32[]{:S(2)}) %collective-permute-start.16) | collective-permute-done | bytes 393248 | tf_op jit(solution)/shard_map/ppermute | solution.py:225
  78.8 6.6 %collective-permute-done.17.r3_ref = bf16[192,1024]{1,0:T(8,128)(2,1)S(1)} collective-permute-done((bf16[192,1024]{1,0:T(8,128)(2,1)S(1)}, bf16[192,1024]{1,0:T(8,128)(2,1)S(1)}, u32[]{:S(2)}, u32[]{:S(2)}) %collective-permute-start.17) | collective-permute-done | bytes 393248 | tf_op jit(solution)/shard_map/ppermute | solution.py:225
  86.0 2.8 %collective-permute-start.19 = (bf16[192,128]{1,0:T(8,128)(2,1)S(1)}, bf16[192,128]{1,0:T(8,128)(2,1)S(1)}, u32[]{:S(2)}, u32[]{:S(2)}) collective-permute-start(bf16[192,128]{1,0:T(8,128)(2,1)S(1)} %shard_map.102), channel_id=1, source_target_pairs={{0,2},{2,0},{1,3},{3,1},{4,6},{6,4},{5,7},{7,5},{8,10},{10,8},{9,1... | collective-permute-start | bytes 147464 | tf_op jit(solution)/shard_map/ppermute | solution.py:215
  88.7 2.4 %shard_map.103 = (f32[256,4096]{1,0:T(8,128)}, f32[1,4096]{1,0:T(1,128)}, f32[8,128]{1,0:T(8,128)S(1)}) custom-call(bf16[192,1024]{1,0:T(8,128)(2,1)S(1)} %shard_map.100.own_ref, bf16[192,1024]{1,0:T(8,128)(2,1)S(1)} %collective-permute-done.16.r1_ref, bf16[192,1024]{1,0:T(8,128)(2,1)S(1)} %collective-permute-done.17.r3_ref, ...), custom_call_target="tpu_custom_call" | custom-call | tf_op jit(solution)/shard_map/pallas_call | solution.py:24
  92.9 8.2 %collective-permute-start.20 = (f32[192,128]{1,0:T(8,128)S(1)}, f32[192,128]{1,0:T(8,128)S(1)}, u32[]{:S(2)}, u32[]{:S(2)}) collective-permute-start(f32[192,128]{1,0:T(8,128)S(1)} %shard_map.104.pair_ref), channel_id=1, source_target_pairs={{0,1},{1,0},{2,3},{3,2},{4,5},{5,4},{6,7},{7,6},{8,9},{9,8},{10,11... | collective-permute-start | bytes 294920 | tf_op jit(solution)/shard_map/ppermute | solution.py:215
  102.1 1.8 %shard_map.105 = (f32[64,4096]{1,0:T(8,128)}, f32[1,64]{1,0:T(1,128)}) custom-call(bf16[384,1024]{1,0:T(8,128)(2,1)S(1)} %bitcast.13, bf16[384,1024]{1,0:T(8,128)(2,1)S(1)} %collective-permute-done.3.other_ref, f32[192,128]{1,0:T(8,128)S(1)} %shard_map.104.pair_ref, f32[192,128]{1,0:T(8,128)S(1)} %collective-permute-done.20.near_ref, ...), custom_call_target="tpu_custom_call" | custom-call | tf_op jit(solution)/shard_map/pallas_call | solution.py:24
  (44 shorter events, 17.6 us)
Async XLA Ops:
  0.6 34.0 %copy-start = (bf16[1,256,4096]{2,1,0:T(8,128)(2,1)S(1)}, bf16[1,256,4096]{2,1,0:T(8,128)(2,1)}, u32[]{:S(2)}) copy-start(bf16[1,256,4096]{2,1,0:T(8,128)(2,1)} %param.9) | copy-start | bytes 6291460
  0.6 9.2 %collective-permute-start = (bf16[3,4096]{1,0:T(4,128)(2,1)}, bf16[3,4096]{1,0:T(4,128)(2,1)S(1)}, u32[]{:S(2)}, u32[]{:S(2)}) collective-permute-start(bf16[3,4096]{1,0:T(4,128)(2,1)} %tokens_ref.1), channel_id=1, source_target_pairs={{0,128},{64,192},{128,2},{192,66},{2,130},{66,194},{130,0},{194,64... | collective-permute-start | bytes 73736 | tf_op jit(solution)/shard_map/ppermute | solution.py:232
  4.5 5.3 %collective-permute-start.1 = (bf16[3,4096]{1,0:T(4,128)(2,1)}, bf16[3,4096]{1,0:T(4,128)(2,1)S(1)}, u32[]{:S(2)}, u32[]{:S(2)}) collective-permute-start(bf16[3,4096]{1,0:T(4,128)(2,1)} %tokens_ref.1), channel_id=1, source_target_pairs={{0,64},{64,128},{128,192},{192,2},{2,66},{66,130},{130,194},{194,0... | collective-permute-start | bytes 73736 | tf_op jit(solution)/shard_map/ppermute | solution.py:232
  6.2 4.5 %collective-permute-start.2 = (bf16[3,4096]{1,0:T(4,128)(2,1)}, bf16[3,4096]{1,0:T(4,128)(2,1)S(1)}, u32[]{:S(2)}, u32[]{:S(2)}) collective-permute-start(bf16[3,4096]{1,0:T(4,128)(2,1)} %tokens_ref.1), channel_id=1, source_target_pairs={{0,194},{64,0},{128,64},{192,128},{2,192},{66,2},{130,66},{194,130... | collective-permute-start | bytes 73736 | tf_op jit(solution)/shard_map/ppermute | solution.py:232
  9.7 25.0 %copy-start.5 = (f32[256]{0:T(256)S(1)}, f32[256]{0:T(256)}, u32[]{:S(2)}) copy-start(f32[256]{0:T(256)} %param.8) | copy-start | bytes 3076
  29.6 5.1 %collective-permute-start.3 = (bf16[384,1024]{1,0:T(8,128)(2,1)S(1)}, bf16[384,1024]{1,0:T(8,128)(2,1)S(1)}, u32[]{:S(2)}, u32[]{:S(2)}) collective-permute-start(bf16[384,1024]{1,0:T(8,128)(2,1)S(1)} %bitcast.11), channel_id=1, source_target_pairs={{0,1},{1,0},{2,3},{3,2},{4,5},{5,4},{6,7},{7,6},{8,9},{9,8},{10,11... | collective-permute-start | bytes 2359304 | tf_op jit(solution)/shard_map/ppermute | solution.py:215
  35.9 28.3 %copy-start.4 = (f32[1,4096]{1,0:T(1,128)S(1)}, f32[1,4096]{1,0:T(1,128)}, u32[]{:S(2)}) copy-start(f32[1,4096]{1,0:T(1,128)} %bias_ref.1) | copy-start | bytes 49156
  36.5 7.0 %collective-permute-start.4 = (bf16[192,1024]{1,0:T(8,128)(2,1)S(1)}, bf16[192,1024]{1,0:T(8,128)(2,1)S(1)}, u32[]{:S(2)}, u32[]{:S(2)}) collective-permute-start(bf16[192,1024]{1,0:T(8,128)(2,1)S(1)} %get-tuple-element.25), channel_id=1, source_target_pairs={{0,4},{1,17},{4,0},{5,21},{8,12},{9,25},{12,8},{13,29},{16,20},{17... | collective-permute-start | bytes 1179656 | tf_op jit(solution)/shard_map/ppermute | solution.py:225
  36.6 12.4 %collective-permute-start.6 = (bf16[192,1024]{1,0:T(8,128)(2,1)S(1)}, bf16[192,1024]{1,0:T(8,128)(2,1)S(1)}, u32[]{:S(2)}, u32[]{:S(2)}) collective-permute-start(bf16[192,1024]{1,0:T(8,128)(2,1)S(1)} %get-tuple-element.27), channel_id=1, source_target_pairs={{0,12},{1,49},{4,8},{5,53},{8,4},{9,57},{12,0},{13,61},{16,28},{17... | collective-permute-start | bytes 1179656 | tf_op jit(solution)/shard_map/ppermute | solution.py:225
  37.4 11.6 %collective-permute-start.5 = (bf16[192,1024]{1,0:T(8,128)(2,1)S(1)}, bf16[192,1024]{1,0:T(8,128)(2,1)S(1)}, u32[]{:S(2)}, u32[]{:S(2)}) collective-permute-start(bf16[192,1024]{1,0:T(8,128)(2,1)S(1)} %get-tuple-element.26), channel_id=1, source_target_pairs={{0,8},{1,33},{4,12},{5,37},{8,0},{9,41},{12,4},{13,45},{16,24},{17... | collective-permute-start | bytes 1179656 | tf_op jit(solution)/shard_map/ppermute | solution.py:225
  49.2 5.1 %collective-permute-start.7 = (bf16[192,256]{1,0:T(8,128)(2,1)S(1)}, bf16[192,256]{1,0:T(8,128)(2,1)S(1)}, u32[]{:S(2)}, u32[]{:S(2)}) collective-permute-start(bf16[192,256]{1,0:T(8,128)(2,1)S(1)} %get-tuple-element.29), channel_id=1, source_target_pairs={{0,32},{1,9},{4,36},{5,13},{8,40},{9,1},{12,44},{13,5},{16,48},{17... | collective-permute-start | bytes 294920 | tf_op jit(solution)/shard_map/ppermute | solution.py:225
  50.0 4.3 %collective-permute-start.8 = (bf16[192,256]{1,0:T(8,128)(2,1)S(1)}, bf16[192,256]{1,0:T(8,128)(2,1)S(1)}, u32[]{:S(2)}, u32[]{:S(2)}) collective-permute-start(bf16[192,256]{1,0:T(8,128)(2,1)S(1)} %get-tuple-element.30), channel_id=1, source_target_pairs={{0,16},{1,5},{4,20},{5,1},{8,24},{9,13},{12,28},{13,9},{16,0},{17,... | collective-permute-start | bytes 294920 | tf_op jit(solution)/shard_map/ppermute | solution.py:225
  50.5 4.9 %collective-permute-start.9 = (bf16[192,256]{1,0:T(8,128)(2,1)S(1)}, bf16[192,256]{1,0:T(8,128)(2,1)S(1)}, u32[]{:S(2)}, u32[]{:S(2)}) collective-permute-start(bf16[192,256]{1,0:T(8,128)(2,1)S(1)} %get-tuple-element.31), channel_id=1, source_target_pairs={{0,48},{1,13},{4,52},{5,9},{8,56},{9,5},{12,60},{13,1},{16,32},{17... | collective-permute-start | bytes 294920 | tf_op jit(solution)/shard_map/ppermute | solution.py:225
  55.4 4.5 %collective-permute-start.10 = (bf16[192,256]{1,0:T(8,128)(2,1)S(1)}, bf16[192,256]{1,0:T(8,128)(2,1)S(1)}, u32[]{:S(2)}, u32[]{:S(2)}) collective-permute-start(bf16[192,256]{1,0:T(8,128)(2,1)S(1)} %shard_map.98.own_ref), channel_id=1, source_target_pairs={{0,128},{64,192},{128,0},{192,64},{1,129},{65,193},{129,1},{193,65... | collective-permute-start | bytes 294920 | tf_op jit(solution)/shard_map/ppermute | solution.py:215
  57.6 5.4 %collective-permute-start.11 = (bf16[192,256]{1,0:T(8,128)(2,1)S(1)}, bf16[192,256]{1,0:T(8,128)(2,1)S(1)}, u32[]{:S(2)}, u32[]{:S(2)}) collective-permute-start(bf16[192,256]{1,0:T(8,128)(2,1)S(1)} %shard_map.98.own_ref), channel_id=1, source_target_pairs={{0,192},{64,128},{128,64},{192,0},{1,193},{65,129},{129,65},{193,1... | collective-permute-start | bytes 294920 | tf_op jit(solution)/shard_map/ppermute | solution.py:215
  59.0 5.2 %collective-permute-start.12 = (bf16[192,256]{1,0:T(8,128)(2,1)S(1)}, bf16[192,256]{1,0:T(8,128)(2,1)S(1)}, u32[]{:S(2)}, u32[]{:S(2)}) collective-permute-start(bf16[192,256]{1,0:T(8,128)(2,1)S(1)} %shard_map.98.own_ref), channel_id=1, source_target_pairs={{0,64},{64,0},{128,192},{192,128},{1,65},{65,1},{129,193},{193,129... | collective-permute-start | bytes 294920 | tf_op jit(solution)/shard_map/ppermute | solution.py:215
  64.2 5.1 %collective-permute-start.13 = (bf16[192,256]{1,0:T(8,128)(2,1)S(1)}, bf16[192,256]{1,0:T(8,128)(2,1)S(1)}, u32[]{:S(2)}, u32[]{:S(2)}) collective-permute-start(bf16[192,256]{1,0:T(8,128)(2,1)S(1)} %shard_map.99.own_ref), channel_id=1, source_target_pairs={{0,32},{1,9},{4,36},{5,13},{8,40},{9,1},{12,44},{13,5},{16,48},{17... | collective-permute-start | bytes 294920 | tf_op jit(solution)/shard_map/ppermute | solution.py:225
  65.5 4.4 %collective-permute-start.14 = (bf16[192,256]{1,0:T(8,128)(2,1)S(1)}, bf16[192,256]{1,0:T(8,128)(2,1)S(1)}, u32[]{:S(2)}, u32[]{:S(2)}) collective-permute-start(bf16[192,256]{1,0:T(8,128)(2,1)S(1)} %shard_map.99.own_ref), channel_id=1, source_target_pairs={{0,16},{1,5},{4,20},{5,1},{8,24},{9,13},{12,28},{13,9},{16,0},{17,... | collective-permute-start | bytes 294920 | tf_op jit(solution)/shard_map/ppermute | solution.py:225
  66.9 4.7 %collective-permute-start.15 = (bf16[192,256]{1,0:T(8,128)(2,1)S(1)}, bf16[192,256]{1,0:T(8,128)(2,1)S(1)}, u32[]{:S(2)}, u32[]{:S(2)}) collective-permute-start(bf16[192,256]{1,0:T(8,128)(2,1)S(1)} %shard_map.99.own_ref), channel_id=1, source_target_pairs={{0,48},{1,13},{4,52},{5,9},{8,56},{9,5},{12,60},{13,1},{16,32},{17... | collective-permute-start | bytes 294920 | tf_op jit(solution)/shard_map/ppermute | solution.py:225
  71.6 7.2 %collective-permute-start.16 = (bf16[192,1024]{1,0:T(8,128)(2,1)S(1)}, bf16[192,1024]{1,0:T(8,128)(2,1)S(1)}, u32[]{:S(2)}, u32[]{:S(2)}) collective-permute-start(bf16[192,1024]{1,0:T(8,128)(2,1)S(1)} %shard_map.100.own_ref), channel_id=1, source_target_pairs={{0,4},{1,17},{4,0},{5,21},{8,12},{9,25},{12,8},{13,29},{16,20},{17... | collective-permute-start | bytes 1179656 | tf_op jit(solution)/shard_map/ppermute | solution.py:225
  72.0 13.4 %collective-permute-start.17 = (bf16[192,1024]{1,0:T(8,128)(2,1)S(1)}, bf16[192,1024]{1,0:T(8,128)(2,1)S(1)}, u32[]{:S(2)}, u32[]{:S(2)}) collective-permute-start(bf16[192,1024]{1,0:T(8,128)(2,1)S(1)} %shard_map.100.own_ref), channel_id=1, source_target_pairs={{0,12},{1,49},{4,8},{5,53},{8,4},{9,57},{12,0},{13,61},{16,28},{17... | collective-permute-start | bytes 1179656 | tf_op jit(solution)/shard_map/ppermute | solution.py:225
  72.9 12.5 %collective-permute-start.18 = (bf16[192,1024]{1,0:T(8,128)(2,1)S(1)}, bf16[192,1024]{1,0:T(8,128)(2,1)S(1)}, u32[]{:S(2)}, u32[]{:S(2)}) collective-permute-start(bf16[192,1024]{1,0:T(8,128)(2,1)S(1)} %shard_map.100.own_ref), channel_id=1, source_target_pairs={{0,8},{1,33},{4,12},{5,37},{8,0},{9,41},{12,4},{13,45},{16,24},{17... | collective-permute-start | bytes 1179656 | tf_op jit(solution)/shard_map/ppermute | solution.py:225
  86.0 6.9 %collective-permute-start.19 = (bf16[192,128]{1,0:T(8,128)(2,1)S(1)}, bf16[192,128]{1,0:T(8,128)(2,1)S(1)}, u32[]{:S(2)}, u32[]{:S(2)}) collective-permute-start(bf16[192,128]{1,0:T(8,128)(2,1)S(1)} %shard_map.102), channel_id=1, source_target_pairs={{0,2},{2,0},{1,3},{3,1},{4,6},{6,4},{5,7},{7,5},{8,10},{10,8},{9,1... | collective-permute-start | bytes 147464 | tf_op jit(solution)/shard_map/ppermute | solution.py:215
  92.9 9.2 %collective-permute-start.20 = (f32[192,128]{1,0:T(8,128)S(1)}, f32[192,128]{1,0:T(8,128)S(1)}, u32[]{:S(2)}, u32[]{:S(2)}) collective-permute-start(f32[192,128]{1,0:T(8,128)S(1)} %shard_map.104.pair_ref), channel_id=1, source_target_pairs={{0,1},{1,0},{2,3},{3,2},{4,5},{5,4},{6,7},{7,6},{8,9},{9,8},{10,11... | collective-permute-start | bytes 294920 | tf_op jit(solution)/shard_map/ppermute | solution.py:215
  (3 other events, 27.3 us)

commit v7 on v5

--- a/solution.py
+++ b/solution.py
@@ -50,7 +50,7 @@
         copy.wait()
 
 
-def pack_kernel(own_ref, below_ref, above_ref, far_ref, out_ref):
+def pack_kernel(own_ref, far_ref, below_ref, above_ref, out_ref):
     zl = lax.axis_index("zl")
     sub = lax.broadcasted_iota(jnp.int32, (8, WIDE), 0)
     sources = [(own_ref, 0), (below_ref, 3), (above_ref, 1), (far_ref, 2)]
@@ -237,7 +237,7 @@
         in_specs=[pl.BlockSpec(memory_space=pl.ANY)] * 2,
         scratch_shapes=[pltpu.SemaphoreType.DMA((2,))],
     )
-    packed = call(pack_kernel, vmem((J, 8 * ROWS, WIDE), BF16), tokens, *near_rows, far_rows, vmem=range(4))
+    packed = call(pack_kernel, vmem((J, 8 * ROWS, WIDE), BF16), tokens, far_rows, *near_rows, vmem=range(4))
     own = lax.all_to_all(packed, ("y", "x"), 0, 0, tiled=True)
     own = own.reshape(2 * COUNT, WIDE)
     other = mirror(own, "core", 2, 1)

time: 104 us -> 104 us (level)
  waiting for transfers between devices: 24.4 us -> 22.2 us
  starting transfers between devices: 26.9 us -> 28.4 us
    ppermute x3, waiting for transfers between devices: 2.75 us -> 0.82 us  [body(): lax.ppermute(tokens, ('zl', 'zh'), ring(step))]
    ppermute x6, starting transfers between devices: 13.6 us -> 15 us  [mirror(): return lax.ppermute(x, axes, [(i, i ^ key) for i in range(size)])]
  transfers between devices with their start and end apart: 15 -> 15, of which waited for: 10 -> 11; matrix products, arithmetic and copies ran while one was open for 0% -> 0% of each run, Pallas kernels for 4% -> 4%
where the time goes in v7:
time: 104 us; the launch traced here: 103 us
  blocking collectives  41 us (39%)
  starting transfers between devices  28.4 us (27%)
  waiting for transfers between devices  22.2 us (21%)
  Pallas kernels  8.39 us (8%)
  local copies, waits for them, and re-layouts  2.37 us (2%)
    all_to_all x1, blocking collectives, body(): lax.all_to_all(copies, FEAT + TGT, 0, 0, axis_index_groups=plane_groups()...  22.2 us
    all_to_all x1, blocking collectives, body(): own = lax.all_to_all(packed, ('y', 'x'), 0, 0, tiled=True)  18.7 us
    ppermute x6, starting transfers between devices, mirror(): return lax.ppermute(x, axes, [(i, i ^ key) for i in range(size)])  15 us
    ppermute x6, waiting for transfers between devices, plane_swap(): return lax.ppermute(x, ('y', 'x', 'core'), pairs)  12 us
    ppermute x6, waiting for transfers between devices, mirror(): return lax.ppermute(x, axes, [(i, i ^ key) for i in range(size)])  9.39 us
    pallas_call x12, Pallas kernels, call(): pl.pallas_call(kernel, out_shape=outs, compiler_params=pltpu.CompilerPara...  8.39 us
    ppermute x6, starting transfers between devices, plane_swap(): return lax.ppermute(x, ('y', 'x', 'core'), pairs)  6.67 us
    ppermute x3, starting transfers between devices, body(): lax.ppermute(tokens, ('zl', 'zh'), ring(step))  6.66 us
  transfers between devices with their start and end apart: 15, of which 11 were waited for; matrix products, arithmetic and copies ran while one was open for 0% of the time, Pallas kernels for 4%

profile of v7, /device:TPU:1, one launch (start us, length us, event | category | flops | bytes accessed | tf_op | source)
XLA Modules:
  0.0 103.0 jit_solution(1441428774738278312)
XLA Ops:
  0.6 3.9 %collective-permute-start = (bf16[3,4096]{1,0:T(4,128)(2,1)}, bf16[3,4096]{1,0:T(4,128)(2,1)S(1)}, u32[]{:S(2)}, u32[]{:S(2)}) collective-permute-start(bf16[3,4096]{1,0:T(4,128)(2,1)} %tokens_ref.1), channel_id=1, source_target_pairs={{0,128},{64,192},{128,2},{192,66},{2,130},{66,194},{130,0},{194,64... | collective-permute-start | bytes 73736 | tf_op jit(solution)/shard_map/ppermute | solution.py:232
  4.5 1.6 %collective-permute-start.1 = (bf16[3,4096]{1,0:T(4,128)(2,1)}, bf16[3,4096]{1,0:T(4,128)(2,1)S(1)}, u32[]{:S(2)}, u32[]{:S(2)}) collective-permute-start(bf16[3,4096]{1,0:T(4,128)(2,1)} %tokens_ref.1), channel_id=1, source_target_pairs={{0,64},{64,128},{128,192},{192,2},{2,66},{66,130},{130,194},{194,0... | collective-permute-start | bytes 73736 | tf_op jit(solution)/shard_map/ppermute | solution.py:232
  6.2 1.1 %collective-permute-start.2 = (bf16[3,4096]{1,0:T(4,128)(2,1)}, bf16[3,4096]{1,0:T(4,128)(2,1)S(1)}, u32[]{:S(2)}, u32[]{:S(2)}) collective-permute-start(bf16[3,4096]{1,0:T(4,128)(2,1)} %tokens_ref.1), channel_id=1, source_target_pairs={{0,194},{64,0},{128,64},{192,128},{2,192},{66,2},{130,66},{194,130... | collective-permute-start | bytes 73736 | tf_op jit(solution)/shard_map/ppermute | solution.py:232
  7.3 1.6 %copy-done.1 = bf16[4096,256]{1,0:T(8,128)(2,1)S(1)} copy-done((bf16[4096,256]{1,0:T(8,128)(2,1)S(1)}, bf16[4096,256]{1,0:T(8,128)(2,1)}, u32[]{:S(2)}) %copy-start.1) | copy-done | bytes 2097176
  10.8 18.7 %all_to_all.10 = bf16[16,24,1024]{2,1,0:T(8,128)(2,1)S(1)} all-to-all(bf16[16,24,1024]{2,1,0:T(8,128)(2,1)S(1)} %shard_map.94), channel_id=1, replica_groups=mesh['zl'=4,'y'=4,'x'=4,'zh'=2,'core'=2] {'y','x'}, dimensions={0} | all-to-all | bytes 1572864 | tf_op jit(solution)/shard_map/all_to_all | solution.py:241
  29.6 3.1 %collective-permute-start.3 = (bf16[384,1024]{1,0:T(8,128)(2,1)S(1)}, bf16[384,1024]{1,0:T(8,128)(2,1)S(1)}, u32[]{:S(2)}, u32[]{:S(2)}) collective-permute-start(bf16[384,1024]{1,0:T(8,128)(2,1)S(1)} %bitcast.11), channel_id=1, source_target_pairs={{0,1},{1,0},{2,3},{3,2},{4,5},{5,4},{6,7},{7,6},{8,9},{9,8},{10,11... | collective-permute-start | bytes 2359304 | tf_op jit(solution)/shard_map/ppermute | solution.py:207
  32.7 1.9 %collective-permute-done.3.other_ref = bf16[384,1024]{1,0:T(8,128)(2,1)S(1)} collective-permute-done((bf16[384,1024]{1,0:T(8,128)(2,1)S(1)}, bf16[384,1024]{1,0:T(8,128)(2,1)S(1)}, u32[]{:S(2)}, u32[]{:S(2)}) %collective-permute-start.3) | collective-permute-done | bytes 786464 | tf_op jit(solution)/shard_map/ppermute | solution.py:207
  34.6 1.2 %shard_map.95 = (bf16[192,1024]{1,0:T(8,128)(2,1)S(1)}, f32[192,256]{1,0:T(8,128)S(1)}, bf16[192,256]{1,0:T(8,128)(2,1)S(1)}) custom-call(bf16[384,1024]{1,0:T(8,128)(2,1)S(1)} %bitcast.12, bf16[384,1024]{1,0:T(8,128)(2,1)S(1)} %collective-permute-done.3.other_ref, bf16[4096,256]{1,0:T(8,128)(2,1)S(1)} %get-tuple-element.22.enc_ref, f32[1,256]{1,0:T(1,128)S(1)} %bitcast.16, ...), custom_call_target="tpu_custom_call" | custom-call | tf_op jit(solution)/shard_map/pallas_call | solution.py:25
  37.4 2.4 %collective-permute-start.5 = (bf16[192,1024]{1,0:T(8,128)(2,1)S(1)}, bf16[192,1024]{1,0:T(8,128)(2,1)S(1)}, u32[]{:S(2)}, u32[]{:S(2)}) collective-permute-start(bf16[192,1024]{1,0:T(8,128)(2,1)S(1)} %get-tuple-element.26), channel_id=1, source_target_pairs={{0,8},{1,33},{4,12},{5,37},{8,0},{9,41},{12,4},{13,45},{16,24},{17... | collective-permute-start | bytes 1179656 | tf_op jit(solution)/shard_map/ppermute | solution.py:217
  39.8 3.7 %collective-permute-done.4.r1_ref = bf16[192,1024]{1,0:T(8,128)(2,1)S(1)} collective-permute-done((bf16[192,1024]{1,0:T(8,128)(2,1)S(1)}, bf16[192,1024]{1,0:T(8,128)(2,1)S(1)}, u32[]{:S(2)}, u32[]{:S(2)}) %collective-permute-start.4) | collective-permute-done | bytes 393248 | tf_op jit(solution)/shard_map/ppermute | solution.py:217
  43.5 5.5 %collective-permute-done.6.r3_ref = bf16[192,1024]{1,0:T(8,128)(2,1)S(1)} collective-permute-done((bf16[192,1024]{1,0:T(8,128)(2,1)S(1)}, bf16[192,1024]{1,0:T(8,128)(2,1)S(1)}, u32[]{:S(2)}, u32[]{:S(2)}) %collective-permute-start.6) | collective-permute-done | bytes 393248 | tf_op jit(solution)/shard_map/ppermute | solution.py:217
  50.5 2.1 %collective-permute-start.9 = (bf16[192,256]{1,0:T(8,128)(2,1)S(1)}, bf16[192,256]{1,0:T(8,128)(2,1)S(1)}, u32[]{:S(2)}, u32[]{:S(2)}) collective-permute-start(bf16[192,256]{1,0:T(8,128)(2,1)S(1)} %get-tuple-element.31), channel_id=1, source_target_pairs={{0,48},{1,13},{4,52},{5,9},{8,56},{9,5},{12,60},{13,1},{16,32},{17... | collective-permute-start | bytes 294920 | tf_op jit(solution)/shard_map/ppermute | solution.py:217
  52.5 1.7 %collective-permute-done.7.r2_ref = bf16[192,256]{1,0:T(8,128)(2,1)S(1)} collective-permute-done((bf16[192,256]{1,0:T(8,128)(2,1)S(1)}, bf16[192,256]{1,0:T(8,128)(2,1)S(1)}, u32[]{:S(2)}, u32[]{:S(2)}) %collective-permute-start.7) | collective-permute-done | bytes 98336 | tf_op jit(solution)/shard_map/ppermute | solution.py:217
  54.3 1.0 %collective-permute-done.9.r3_ref = bf16[192,256]{1,0:T(8,128)(2,1)S(1)} collective-permute-done((bf16[192,256]{1,0:T(8,128)(2,1)S(1)}, bf16[192,256]{1,0:T(8,128)(2,1)S(1)}, u32[]{:S(2)}, u32[]{:S(2)}) %collective-permute-start.9) | collective-permute-done | bytes 98336 | tf_op jit(solution)/shard_map/ppermute | solution.py:217
  55.4 2.2 %collective-permute-start.10 = (bf16[192,256]{1,0:T(8,128)(2,1)S(1)}, bf16[192,256]{1,0:T(8,128)(2,1)S(1)}, u32[]{:S(2)}, u32[]{:S(2)}) collective-permute-start(bf16[192,256]{1,0:T(8,128)(2,1)S(1)} %shard_map.98.own_ref), channel_id=1, source_target_pairs={{0,128},{64,192},{128,0},{192,64},{1,129},{65,193},{129,1},{193,65... | collective-permute-start | bytes 294920 | tf_op jit(solution)/shard_map/ppermute | solution.py:207
  57.6 1.4 %collective-permute-start.11 = (bf16[192,256]{1,0:T(8,128)(2,1)S(1)}, bf16[192,256]{1,0:T(8,128)(2,1)S(1)}, u32[]{:S(2)}, u32[]{:S(2)}) collective-permute-start(bf16[192,256]{1,0:T(8,128)(2,1)S(1)} %shard_map.98.own_ref), channel_id=1, source_target_pairs={{0,192},{64,128},{128,64},{192,0},{1,193},{65,129},{129,65},{193,1... | collective-permute-start | bytes 294920 | tf_op jit(solution)/shard_map/ppermute | solution.py:207
  59.8 3.2 %collective-permute-done.11.r3_ref = bf16[192,256]{1,0:T(8,128)(2,1)S(1)} collective-permute-done((bf16[192,256]{1,0:T(8,128)(2,1)S(1)}, bf16[192,256]{1,0:T(8,128)(2,1)S(1)}, u32[]{:S(2)}, u32[]{:S(2)}) %collective-permute-start.11) | collective-permute-done | bytes 98336 | tf_op jit(solution)/shard_map/ppermute | solution.py:207
  63.0 1.2 %collective-permute-done.12.r1_ref = bf16[192,256]{1,0:T(8,128)(2,1)S(1)} collective-permute-done((bf16[192,256]{1,0:T(8,128)(2,1)S(1)}, bf16[192,256]{1,0:T(8,128)(2,1)S(1)}, u32[]{:S(2)}, u32[]{:S(2)}) %collective-permute-start.12) | collective-permute-done | bytes 98336 | tf_op jit(solution)/shard_map/ppermute | solution.py:207
  64.4 22.2 %all_to_all.11.error_ref = bf16[16,192,256]{2,1,0:T(8,128)(2,1)S(1)} all-to-all(bf16[16,192,256]{2,1,0:T(8,128)(2,1)S(1)} %shard_map.99), channel_id=1, replica_groups={{0,16,32,48,4,20,36,52,8,24,40,56,12,28,44,60},{1,5,9,13,17,21,25,29,33..., dimensions={0} | all-to-all | bytes 3145728 | tf_op jit(solution)/shard_map/all_to_all | solution.py:267
  87.2 1.8 %collective-permute-start.13 = (bf16[192,128]{1,0:T(8,128)(2,1)S(1)}, bf16[192,128]{1,0:T(8,128)(2,1)S(1)}, u32[]{:S(2)}, u32[]{:S(2)}) collective-permute-start(bf16[192,128]{1,0:T(8,128)(2,1)S(1)} %shard_map.101), channel_id=1, source_target_pairs={{0,2},{2,0},{1,3},{3,1},{4,6},{6,4},{5,7},{7,5},{8,10},{10,8},{9,1... | collective-permute-start | bytes 147464 | tf_op jit(solution)/shard_map/ppermute | solution.py:207
  89.0 3.0 %shard_map.102 = (f32[256,4096]{1,0:T(8,128)}, f32[1,4096]{1,0:T(1,128)}, f32[8,128]{1,0:T(8,128)S(1)}) custom-call(bf16[16,192,256]{2,1,0:T(8,128)(2,1)S(1)} %all_to_all.11.error_ref, bf16[192,256]{1,0:T(8,128)(2,1)S(1)} %get-tuple-element.23.feats_ref), custom_call_target="tpu_custom_call" | custom-call | tf_op jit(solution)/shard_map/pallas_call | solution.py:25
  92.6 1.5 %collective-permute-done.13.peer_ref = bf16[192,128]{1,0:T(8,128)(2,1)S(1)} collective-permute-done((bf16[192,128]{1,0:T(8,128)(2,1)S(1)}, bf16[192,128]{1,0:T(8,128)(2,1)S(1)}, u32[]{:S(2)}, u32[]{:S(2)}) %collective-permute-start.13) | collective-permute-done | bytes 49184 | tf_op jit(solution)/shard_map/ppermute | solution.py:207
  94.1 6.2 %collective-permute-start.14 = (f32[192,128]{1,0:T(8,128)S(1)}, f32[192,128]{1,0:T(8,128)S(1)}, u32[]{:S(2)}, u32[]{:S(2)}) collective-permute-start(f32[192,128]{1,0:T(8,128)S(1)} %shard_map.103.pair_ref), channel_id=1, source_target_pairs={{0,1},{1,0},{2,3},{3,2},{4,5},{5,4},{6,7},{7,6},{8,9},{9,8},{10,11... | collective-permute-start | bytes 294920 | tf_op jit(solution)/shard_map/ppermute | solution.py:207
  101.3 1.7 %shard_map.104 = (f32[64,4096]{1,0:T(8,128)}, f32[1,64]{1,0:T(1,128)}) custom-call(bf16[384,1024]{1,0:T(8,128)(2,1)S(1)} %bitcast.13, bf16[384,1024]{1,0:T(8,128)(2,1)S(1)} %collective-permute-done.3.other_ref, f32[192,128]{1,0:T(8,128)S(1)} %shard_map.103.pair_ref, f32[192,128]{1,0:T(8,128)S(1)} %collective-permute-done.14.near_ref, ...), custom_call_target="tpu_custom_call" | custom-call | tf_op jit(solution)/shard_map/pallas_call | solution.py:25
  (32 shorter events, 8.0 us)
Async XLA Ops:
  0.6 34.0 %copy-start = (bf16[1,256,4096]{2,1,0:T(8,128)(2,1)S(1)}, bf16[1,256,4096]{2,1,0:T(8,128)(2,1)}, u32[]{:S(2)}) copy-start(bf16[1,256,4096]{2,1,0:T(8,128)(2,1)} %param.9) | copy-start | bytes 6291460
  0.6 9.2 %collective-permute-start = (bf16[3,4096]{1,0:T(4,128)(2,1)}, bf16[3,4096]{1,0:T(4,128)(2,1)S(1)}, u32[]{:S(2)}, u32[]{:S(2)}) collective-permute-start(bf16[3,4096]{1,0:T(4,128)(2,1)} %tokens_ref.1), channel_id=1, source_target_pairs={{0,128},{64,192},{128,2},{192,66},{2,130},{66,194},{130,0},{194,64... | collective-permute-start | bytes 73736 | tf_op jit(solution)/shard_map/ppermute | solution.py:232
  4.5 5.3 %collective-permute-start.1 = (bf16[3,4096]{1,0:T(4,128)(2,1)}, bf16[3,4096]{1,0:T(4,128)(2,1)S(1)}, u32[]{:S(2)}, u32[]{:S(2)}) collective-permute-start(bf16[3,4096]{1,0:T(4,128)(2,1)} %tokens_ref.1), channel_id=1, source_target_pairs={{0,64},{64,128},{128,192},{192,2},{2,66},{66,130},{130,194},{194,0... | collective-permute-start | bytes 73736 | tf_op jit(solution)/shard_map/ppermute | solution.py:232
  6.2 4.5 %collective-permute-start.2 = (bf16[3,4096]{1,0:T(4,128)(2,1)}, bf16[3,4096]{1,0:T(4,128)(2,1)S(1)}, u32[]{:S(2)}, u32[]{:S(2)}) collective-permute-start(bf16[3,4096]{1,0:T(4,128)(2,1)} %tokens_ref.1), channel_id=1, source_target_pairs={{0,194},{64,0},{128,64},{192,128},{2,192},{66,2},{130,66},{194,130... | collective-permute-start | bytes 73736 | tf_op jit(solution)/shard_map/ppermute | solution.py:232
  7.3 1.6 %copy-start.1 = (bf16[4096,256]{1,0:T(8,128)(2,1)S(1)}, bf16[4096,256]{1,0:T(8,128)(2,1)}, u32[]{:S(2)}) copy-start(bf16[4096,256]{1,0:T(8,128)(2,1)} %enc_ref.1) | copy-start | bytes 6291460
  8.9 0.8 copy-start.3
  9.7 25.0 %copy-start.2 = (bf16[1,3,4096]{2,1,0:T(4,128)(2,1)S(1)}, bf16[1,3,4096]{2,1,0:T(4,128)(2,1)}, u32[]{:S(2)}) copy-start(bf16[1,3,4096]{2,1,0:T(4,128)(2,1)} %param.11) | copy-start | bytes 73732
  9.7 25.0 %copy-start.5 = (f32[256]{0:T(256)S(1)}, f32[256]{0:T(256)}, u32[]{:S(2)}) copy-start(f32[256]{0:T(256)} %param.8) | copy-start | bytes 3076
  29.6 5.1 %collective-permute-start.3 = (bf16[384,1024]{1,0:T(8,128)(2,1)S(1)}, bf16[384,1024]{1,0:T(8,128)(2,1)S(1)}, u32[]{:S(2)}, u32[]{:S(2)}) collective-permute-start(bf16[384,1024]{1,0:T(8,128)(2,1)S(1)} %bitcast.11), channel_id=1, source_target_pairs={{0,1},{1,0},{2,3},{3,2},{4,5},{5,4},{6,7},{7,6},{8,9},{9,8},{10,11... | collective-permute-start | bytes 2359304 | tf_op jit(solution)/shard_map/ppermute | solution.py:207
  35.9 28.3 %copy-start.4 = (f32[1,4096]{1,0:T(1,128)S(1)}, f32[1,4096]{1,0:T(1,128)}, u32[]{:S(2)}) copy-start(f32[1,4096]{1,0:T(1,128)} %bias_ref.1) | copy-start | bytes 49156
  36.4 7.0 %collective-permute-start.4 = (bf16[192,1024]{1,0:T(8,128)(2,1)S(1)}, bf16[192,1024]{1,0:T(8,128)(2,1)S(1)}, u32[]{:S(2)}, u32[]{:S(2)}) collective-permute-start(bf16[192,1024]{1,0:T(8,128)(2,1)S(1)} %get-tuple-element.25), channel_id=1, source_target_pairs={{0,4},{1,17},{4,0},{5,21},{8,12},{9,25},{12,8},{13,29},{16,20},{17... | collective-permute-start | bytes 1179656 | tf_op jit(solution)/shard_map/ppermute | solution.py:217
  36.5 12.4 %collective-permute-start.6 = (bf16[192,1024]{1,0:T(8,128)(2,1)S(1)}, bf16[192,1024]{1,0:T(8,128)(2,1)S(1)}, u32[]{:S(2)}, u32[]{:S(2)}) collective-permute-start(bf16[192,1024]{1,0:T(8,128)(2,1)S(1)} %get-tuple-element.27), channel_id=1, source_target_pairs={{0,12},{1,49},{4,8},{5,53},{8,4},{9,57},{12,0},{13,61},{16,28},{17... | collective-permute-start | bytes 1179656 | tf_op jit(solution)/shard_map/ppermute | solution.py:217
  37.4 11.6 %collective-permute-start.5 = (bf16[192,1024]{1,0:T(8,128)(2,1)S(1)}, bf16[192,1024]{1,0:T(8,128)(2,1)S(1)}, u32[]{:S(2)}, u32[]{:S(2)}) collective-permute-start(bf16[192,1024]{1,0:T(8,128)(2,1)S(1)} %get-tuple-element.26), channel_id=1, source_target_pairs={{0,8},{1,33},{4,12},{5,37},{8,0},{9,41},{12,4},{13,45},{16,24},{17... | collective-permute-start | bytes 1179656 | tf_op jit(solution)/shard_map/ppermute | solution.py:217
  49.2 5.1 %collective-permute-start.7 = (bf16[192,256]{1,0:T(8,128)(2,1)S(1)}, bf16[192,256]{1,0:T(8,128)(2,1)S(1)}, u32[]{:S(2)}, u32[]{:S(2)}) collective-permute-start(bf16[192,256]{1,0:T(8,128)(2,1)S(1)} %get-tuple-element.29), channel_id=1, source_target_pairs={{0,32},{1,9},{4,36},{5,13},{8,40},{9,1},{12,44},{13,5},{16,48},{17... | collective-permute-start | bytes 294920 | tf_op jit(solution)/shard_map/ppermute | solution.py:217
  50.0 4.3 %collective-permute-start.8 = (bf16[192,256]{1,0:T(8,128)(2,1)S(1)}, bf16[192,256]{1,0:T(8,128)(2,1)S(1)}, u32[]{:S(2)}, u32[]{:S(2)}) collective-permute-start(bf16[192,256]{1,0:T(8,128)(2,1)S(1)} %get-tuple-element.30), channel_id=1, source_target_pairs={{0,16},{1,5},{4,20},{5,1},{8,24},{9,13},{12,28},{13,9},{16,0},{17,... | collective-permute-start | bytes 294920 | tf_op jit(solution)/shard_map/ppermute | solution.py:217
  50.5 4.9 %collective-permute-start.9 = (bf16[192,256]{1,0:T(8,128)(2,1)S(1)}, bf16[192,256]{1,0:T(8,128)(2,1)S(1)}, u32[]{:S(2)}, u32[]{:S(2)}) collective-permute-start(bf16[192,256]{1,0:T(8,128)(2,1)S(1)} %get-tuple-element.31), channel_id=1, source_target_pairs={{0,48},{1,13},{4,52},{5,9},{8,56},{9,5},{12,60},{13,1},{16,32},{17... | collective-permute-start | bytes 294920 | tf_op jit(solution)/shard_map/ppermute | solution.py:217
  55.4 4.5 %collective-permute-start.10 = (bf16[192,256]{1,0:T(8,128)(2,1)S(1)}, bf16[192,256]{1,0:T(8,128)(2,1)S(1)}, u32[]{:S(2)}, u32[]{:S(2)}) collective-permute-start(bf16[192,256]{1,0:T(8,128)(2,1)S(1)} %shard_map.98.own_ref), channel_id=1, source_target_pairs={{0,128},{64,192},{128,0},{192,64},{1,129},{65,193},{129,1},{193,65... | collective-permute-start | bytes 294920 | tf_op jit(solution)/shard_map/ppermute | solution.py:207
  57.6 5.4 %collective-permute-start.11 = (bf16[192,256]{1,0:T(8,128)(2,1)S(1)}, bf16[192,256]{1,0:T(8,128)(2,1)S(1)}, u32[]{:S(2)}, u32[]{:S(2)}) collective-permute-start(bf16[192,256]{1,0:T(8,128)(2,1)S(1)} %shard_map.98.own_ref), channel_id=1, source_target_pairs={{0,192},{64,128},{128,64},{192,0},{1,193},{65,129},{129,65},{193,1... | collective-permute-start | bytes 294920 | tf_op jit(solution)/shard_map/ppermute | solution.py:207
  59.0 5.2 %collective-permute-start.12 = (bf16[192,256]{1,0:T(8,128)(2,1)S(1)}, bf16[192,256]{1,0:T(8,128)(2,1)S(1)}, u32[]{:S(2)}, u32[]{:S(2)}) collective-permute-start(bf16[192,256]{1,0:T(8,128)(2,1)S(1)} %shard_map.98.own_ref), channel_id=1, source_target_pairs={{0,64},{64,0},{128,192},{192,128},{1,65},{65,1},{129,193},{193,129... | collective-permute-start | bytes 294920 | tf_op jit(solution)/shard_map/ppermute | solution.py:207
  87.2 6.9 %collective-permute-start.13 = (bf16[192,128]{1,0:T(8,128)(2,1)S(1)}, bf16[192,128]{1,0:T(8,128)(2,1)S(1)}, u32[]{:S(2)}, u32[]{:S(2)}) collective-permute-start(bf16[192,128]{1,0:T(8,128)(2,1)S(1)} %shard_map.101), channel_id=1, source_target_pairs={{0,2},{2,0},{1,3},{3,1},{4,6},{6,4},{5,7},{7,5},{8,10},{10,8},{9,1... | collective-permute-start | bytes 147464 | tf_op jit(solution)/shard_map/ppermute | solution.py:207
  94.1 7.2 %collective-permute-start.14 = (f32[192,128]{1,0:T(8,128)S(1)}, f32[192,128]{1,0:T(8,128)S(1)}, u32[]{:S(2)}, u32[]{:S(2)}) collective-permute-start(f32[192,128]{1,0:T(8,128)S(1)} %shard_map.103.pair_ref), channel_id=1, source_target_pairs={{0,1},{1,0},{2,3},{3,2},{4,5},{5,4},{6,7},{7,6},{8,9},{9,8},{10,11... | collective-permute-start | bytes 294920 | tf_op jit(solution)/shard_map/ppermute | solution.py:207
